TPU v7x, 256 devices: a whole 4x4x8 slice. The times are simulated.
256 devices in a mesh: group: 2 (over x_hi), seq: 16 (over x_lo, z), tensor: 8 (over y, core).
Axes of the slice: x: 4 (x_hi: 2, x_lo: 2; x = x_hi * 2 + x_lo), y: 4, z: 8, core: 2. Of those that a mesh axis runs over, the one named last changes fastest.
Arguments:
- tokens: bfloat16 [2, 2048, 8192], P('group', 'seq', 'tensor'), may hold values from -6 to 6
- frame_feats: bfloat16 [2, 512, 1280], P('group', 'seq'), may hold values from -6 to 6
- w_proj: bfloat16 [1280, 8192], P(None, 'tensor'), may hold values from -0.15625 to 0.15625
- frame_pos: int32 [2, 512], P('group', 'seq'), may hold values from 0 to 2047, as said below
- segments: int32 [2, 2048], P('group', 'seq'), may hold values from 0 to 3, never falling along the last dimension, each value on 1 to 1024 neighbouring positions
- signs: int32 [2, 2048], P('group', 'seq'), may hold values from 0 to 1
- w_x: bfloat16 [8192, 8192], P(('group', 'seq'), 'tensor'), may hold values from -0.0625 to 0.0625
- w_bc: bfloat16 [8192, 2048], P(('group', 'seq'), 'tensor'), may hold values from -0.0625 to 0.0625
- w_dt: bfloat16 [8192, 128], P(('group', 'seq'), 'tensor'), may hold values from -0.0625 to 0.0625
- dt_bias: float32 [128], P('tensor'), may hold values from -4 to -2
- decay_rate: float32 [128], P('tensor'), may hold values from 0.0001 to 1
- skip_gain: float32 [128], P('tensor'), may hold values from 0.5 to 6
- probe: bfloat16 [2, 2048, 8192], P('group', 'seq', 'tensor'), may hold values from -6 to 6
Outputs:
- adv_tokens: bfloat16 [2, 2048, 8192], P('group', 'seq', 'tensor')
- adv_frames: bfloat16 [2, 512, 8192], P('group', 'seq', 'tensor')
Inputs may be any that keep to these rules, and one draw needn't show every extreme that they name: `frame_pos`: within a sample the positions are distinct; frame token k * 32 + b * 2 + i (0 <= i < 2) lies in positions b * 128 to (b + 1) * 128 - 1. `segments`: document ids never fall along a sample.
All inputs are finite; a program needn't handle non-finite values.
Results may differ from a plain program's by a relative error of at most 0.0095.
Values may be sent and summed in bfloat16 or wider, within the bound.
No kernel may reach another device: no remote copies, remote signals or barrier semaphores. Data moves between devices by JAX's collectives and lax.ppermute only.
A program may use at most 128 MiB of HBM per device.

v0:
```python
import jax
import jax.numpy as jnp
from jax import lax
from jax.experimental import pallas as pl
from jax.experimental.pallas import tpu as pltpu
from jax.sharding import Mesh, PartitionSpec as P


F32, BF16 = jnp.float32, jnp.bfloat16
AXES = ("x_hi", "x_lo", "z", "y", "core")
X = ("x_hi", "x_lo")
SEQ = ("x_lo", "z")
TENSOR = ("y", "core")
CHUNK = 128
WIDE = 1408
PLACE = (0, 2, 1, 3)
HIGH = lax.Precision.HIGHEST
VMEM = pl.BlockSpec(memory_space=pltpu.VMEM)
SMEM = pl.BlockSpec(memory_space=pltpu.SMEM)


def linear(x, z, y, core):
    return ((x * 8 + z) * 4 + y) * 2 + core


def features_route():
    pairs = []
    for x in range(4):
        for z in range(8):
            for y in range(4):
                for core in range(2):
                    there = linear(y, 4 * (z // 4) + PLACE[x], (z % 4 + x) % 4, core)
                    pairs.append((linear(x, z, y, core), there))
    return pairs


def probe_route():
    pairs = []
    for x in range(4):
        for z in range(8):
            pairs.append((x * 8 + z, (z % 4 + x) % 4 * 8 + 4 * (z // 4) + PLACE[x]))
    return pairs


def quarter_route(k):
    pairs = []
    for z in range(8):
        home = PLACE[z % 4]
        to = (2 * (home % 2) + z // 4 + k) % 4
        pairs.append((z, 4 * (to % 2) + PLACE[home // 2 * 2 + to // 2]))
    return pairs


def dot_nt(a, b):
    return lax.dot_general(a, b, (((1,), (1,)), ((), ())), preferred_element_type=F32)


def dot_tn(a, b):
    return lax.dot_general(a, b, (((0,), (0,)), ((), ())), preferred_element_type=F32)


def dot_nn(a, b):
    return jnp.dot(a, b, preferred_element_type=F32)


def iota(shape, dim):
    return lax.broadcasted_iota(jnp.int32, shape, dim)


def spread(columns):
    left = iota((CHUNK, 128), 1) < 64
    tiles = [
        jnp.where(left, jnp.broadcast_to(columns[2 * i], (CHUNK, 128)), jnp.broadcast_to(columns[2 * i + 1], (CHUNK, 128)))
        for i in range(2)
    ]
    return jnp.concatenate(tiles, axis=1)


def by_head_rows(values):
    rows = iota((256, 128), 0)
    out = jnp.broadcast_to(values[3], (256, 128))
    for h in (2, 1, 0):
        out = jnp.where(rows < 64 * (h + 1), jnp.broadcast_to(values[h], (256, 128)), out)
    return out


def lanes(row):
    return [row[:, h : h + 1] for h in range(4)]


def weights_of(rows, cols):
    seg = cols[:, 12:13]
    prev, last = rows[13:14, 127:128], rows[12:13, 127:128]
    end = cols[127:128, :]
    carry = jnp.where(seg == prev, jnp.exp(cols), 0.0)
    tail = jnp.where(seg == last, jnp.exp(end - cols), 0.0)
    through = jnp.where(last == prev, jnp.exp(end), 0.0)
    return carry, tail, through


def pack_kernel(w_x, w_bc, w_dt, out):
    out[:, 0:1024] = w_x[...]
    out[:, 1024:1280] = w_bc[...]
    out[:, 1280:1408] = jnp.zeros((256, 128), BF16)
    out[:, 1280:1296] = w_dt[...]


def pack(*parts):
    return pl.pallas_call(
        pack_kernel, in_specs=[VMEM] * 3, out_specs=VMEM, out_shape=jax.ShapeDtypeStruct((256, WIDE), BF16)
    )(*parts)


def ring_source(meta, i):
    offset = (0, 7, 1, 6, 2, 5, 3, 4)[i]
    return lax.rem(meta[3] + offset, 8)


def start_copies(blocks, buf, sems):
    copies = []
    for i, ref in enumerate(blocks[:7]):
        copies.append([pltpu.make_async_copy(ref, buf.at[i], sems.at[i])])
    if len(blocks) == 9:
        halves = [pltpu.make_async_copy(blocks[7 + n], buf.at[7, pl.ds(128 * n, 128)], sems.at[7 + n]) for n in range(2)]
        copies.append(halves)
    for group in copies:
        for copy in group:
            copy.start()
    return copies


def feature_columns(meta, own, oth, place):
    half, cols = place // 4, pl.ds(pl.multiple_of(lax.rem(place, 4) * 256, 256), 256)
    mine = half == meta[0]
    parts = []
    for k in range(4):
        at = lax.rem(k + meta[1], 4)
        parts.append(jnp.where(mine, own[at, :, cols].astype(F32), oth[at, :, cols].astype(F32)).astype(BF16))
    return jnp.concatenate(parts, axis=0)


TILES = [(256 * t, min(256 * t + 256, WIDE)) for t in range(6)]


def project_most_kernel(meta, own, oth, *rest):
    blocks, (acc, last), (buf, rows, sems) = rest[:7], rest[7:9], rest[9:]
    copies = start_copies(blocks, buf, sems)
    for i in range(7):
        rows[i] = feature_columns(meta, own, oth, ring_source(meta, i))
    last[...] = feature_columns(meta, own, oth, ring_source(meta, 7))
    for group in copies:
        group[0].wait()
    for lo, hi in TILES:
        total = dot_nn(rows[0], buf[0, :, lo:hi])
        for i in range(1, 7):
            total += dot_nn(rows[i], buf[i, :, lo:hi])
        acc[:, lo:hi] = total


def project_most(meta, own, oth, blocks):
    return pl.pallas_call(
        project_most_kernel,
        in_specs=[SMEM, VMEM, VMEM] + [pl.BlockSpec(memory_space=pl.ANY)] * 7,
        out_specs=[VMEM] * 2,
        out_shape=[jax.ShapeDtypeStruct((512, WIDE), F32), jax.ShapeDtypeStruct((512, 256), BF16)],
        scratch_shapes=[
            pltpu.VMEM((7, 256, WIDE), BF16),
            pltpu.VMEM((7, 512, 256), BF16),
            pltpu.SemaphoreType.DMA((7,)),
        ],
    )(meta, own, oth, *blocks)


def project_last_kernel(rows, acc, upper, lower, probe, out):
    ids = probe[128:144, 0:512].astype(F32)[0:8]
    for d in range(4):
        part = slice(256 * d, 256 * d + 256)
        out[d, 528:592, 0:256] = probe[0:64, part]
        out[d, 528:592, 256:512] = probe[64:128, part]
    for t, (lo, hi) in enumerate(TILES):
        total = acc[:, lo:hi] + dot_nn(rows[:, 0:128], upper[:, lo:hi]) + dot_nn(rows[:, 128:256], lower[:, lo:hi])
        if t < 4:
            out[t, 0:512, 0:256] = total.astype(BF16)
        elif t == 4:
            for d in range(4):
                out[d, 0:512, 256:512] = total.astype(BF16)
        else:
            steps = total.T
            for d in range(4):
                mine = jnp.concatenate([steps[4 * d : 4 * d + 4], jnp.zeros((4, 512), F32), ids], axis=0)
                out[d, 512:528, :] = mine.astype(BF16)


def project_last(*args):
    return pl.pallas_call(
        project_last_kernel,
        in_specs=[VMEM] * 5,
        out_specs=VMEM,
        out_shape=jax.ShapeDtypeStruct((4, 592, 512), BF16),
    )(*args)


def prepare_kernel(meta, r, prm, pay, x, bc, rows_out, cols_out, t_out, q_out, p):
    total = r[0, 0:512, :].astype(F32)
    raw = r[0, 512:528, :].astype(F32)
    for d in range(1, 4):
        total += r[d, 0:512, :].astype(F32)
        raw += r[d, 512:528, :].astype(F32)
    x[...] = total[:, 0:256]
    bc[...] = total[:, 256:512].astype(BF16)
    upper = (iota((128, 128), 0) <= iota((128, 128), 1)).astype(F32)
    top = iota((8, 128), 0) < 4
    bias, rate = prm[0], prm[1]
    through = []
    for k in range(4):
        here = slice(128 * k, 128 * k + 128)
        z = raw[0:8, here] + bias
        dt = jnp.maximum(z, 0.0) + jnp.log1p(jnp.exp(-jnp.abs(z)))
        logs = jnp.dot(-dt * rate, upper, precision=HIGH, preferred_element_type=F32)
        source = lax.rem(k + meta[1], 4)
        p[k, 0:64, :] = r[source, 528:592, 0:256]
        p[k, 64:128, :] = r[source, 528:592, 256:512]
        seg = r[source, 512:528, 0:128].astype(F32)[8:16]
        rows = jnp.concatenate([jnp.where(top, logs, pltpu.roll(dt, 4, 0)), jnp.where(top, z, pltpu.roll(seg, 4, 0))], axis=0)
        cols = jnp.concatenate([rows, jnp.zeros((112, 128), F32)], axis=0).T
        rows_out[k] = rows
        cols_out[k] = cols
        carry, tail, thru = weights_of(rows, cols)
        through.append(thru)
        carry_x = spread(lanes(carry))
        tail_x = spread([tail[:, h : h + 1] * cols[:, 4 + h : 5 + h] for h in range(4)])
        b, c = bc[here, 0:128], bc[here, 128:256]
        t_out[k] = dot_tn((x[here, :] * tail_x).astype(BF16), b)
        q_out[k] = dot_tn((p[k, 0:128, :].astype(F32) * carry_x).astype(BF16), c)
    state = t_out[0]
    grad = q_out[3]
    whole = through[0]
    for k in range(1, 4):
        state = by_head_rows(lanes(through[k])) * state + t_out[k]
        grad = by_head_rows(lanes(through[3 - k])) * grad + q_out[3 - k]
        whole = whole * through[k]
    for k in range(1, 4):
        pay[k - 1, 0:256, :] = jnp.where(meta[2] + k < 4, state, grad).astype(BF16)
        pay[k - 1, 256:272, :] = jnp.broadcast_to(whole, (16, 128)).astype(BF16)


def prepare(meta, r, prm):
    return pl.pallas_call(
        prepare_kernel,
        in_specs=[SMEM, VMEM, VMEM],
        out_specs=[VMEM] * 8,
        out_shape=[
            jax.ShapeDtypeStruct((3, 272, 128), BF16),
            jax.ShapeDtypeStruct((512, 256), F32),
            jax.ShapeDtypeStruct((512, 256), BF16),
            jax.ShapeDtypeStruct((4, 16, 128), F32),
            jax.ShapeDtypeStruct((4, 128, 128), F32),
            jax.ShapeDtypeStruct((4, 256, 128), F32),
            jax.ShapeDtypeStruct((4, 256, 128), F32),
            jax.ShapeDtypeStruct((4, 128, 256), BF16),
        ],
    )(meta, r, prm)


def intra_kernel(x, bc, p, rows_in, cols_in, skip, dx, dbc, e):
    seen = iota((128, 128), 0) >= iota((128, 128), 1)
    lane = iota((128, 128), 1)
    for k in range(4):
        here = slice(128 * k, 128 * k + 128)
        b, c = bc[here, 0:128], bc[here, 128:256]
        rows, cols = rows_in[k], cols_in[k]
        scores = dot_nt(c, b)
        visible = (cols[:, 12:13] == rows[12:13, :]) & seen
        d_scores = jnp.zeros((128, 128), F32)
        by_row = jnp.zeros((128, 128), F32)
        sums = []
        for tile in range(2):
            part = slice(128 * tile, 128 * tile + 128)
            probe = p[k, 0:128, part].astype(F32)
            values = x[here, part].astype(BF16)
            d_values = skip[:, part] * probe
            for a in range(2):
                h = 2 * tile + a
                mine = jnp.where((lane < 64) if a == 0 else (lane >= 64), probe, 0.0).astype(BF16)
                pulled = dot_nt(mine, values)
                decay = jnp.exp(jnp.where(visible, cols[:, h : h + 1] - rows[h : h + 1, :], -1e30))
                steps = rows[4 + h : 5 + h, :]
                weighted = decay * pulled
                decayed = decay * scores
                plain = weighted * scores
                sums.append(jnp.sum(plain, axis=0, keepdims=True))
                by_row = jnp.where(lane == h, jnp.sum(plain * steps, axis=1, keepdims=True), by_row)
                d_scores += weighted * steps
                d_values += dot_tn((decayed * steps).astype(BF16), mine)
            dx[here, part] = d_values
        d_scores = d_scores.astype(BF16)
        dbc[here, 0:128] = dot_tn(d_scores, c)
        dbc[here, 128:256] = dot_nn(d_scores, b)
        sub = iota((8, 128), 0)
        down = jnp.zeros((8, 128), F32)
        for h in range(4):
            down = jnp.where(sub == h, jnp.broadcast_to(sums[h], (8, 128)), down)
        dt = pltpu.roll(rows[0:8], 4, 0)
        e[k, 0:8, :] = down
        e[k, 8:16, :] = by_row.T[0:8] - dt * down


def intra(x, bc, p, rows, cols, skip):
    return pl.pallas_call(
        intra_kernel,
        in_specs=[VMEM] * 6,
        out_specs=[VMEM] * 3,
        out_shape=[
            jax.ShapeDtypeStruct((512, 256), F32),
            jax.ShapeDtypeStruct((512, 256), F32),
            jax.ShapeDtypeStruct((4, 16, 128), F32),
        ],
    )(x, bc, p, rows, cols, skip)


def finish_kernel(meta, r1, r2, r3, x, bc, p, rows_in, cols_in, t_in, q_in, dx, dbc, e, prm, out):
    quarter = meta[2]
    got = (r1, r2, r3)
    parts = [ref[0:256, :].astype(F32) for ref in got]
    decays = [by_head_rows(lanes(ref[256:272, :].astype(F32)[0:1])) for ref in got]

    def total(order):
        out_sum = jnp.zeros((256, 128), F32)
        run = jnp.ones((256, 128), F32)
        for index, valid in order:
            out_sum += jnp.where(valid, run * parts[index], 0.0)
            run = jnp.where(valid, run * decays[index], run)
        return out_sum

    entering = total([(k - 1, quarter - k >= 0) for k in (1, 2, 3)])
    leaving = total([(3 - m, quarter + m <= 3) for m in (1, 2, 3)])
    weights = [weights_of(rows_in[k], cols_in[k]) for k in range(4)]
    through = [by_head_rows(lanes(weights[k][2])) for k in range(4)]
    states, grads = [entering], [leaving]
    for k in range(3):
        states.append(through[k] * states[k] + t_in[k])
        grads.append(through[3 - k] * grads[k] + q_in[3 - k])
    grads = grads[::-1]
    indicator = (iota((8, 256), 1) // 64 == iota((8, 256), 0)).astype(F32)
    lower = (iota((128, 128), 0) >= iota((128, 128), 1)).astype(F32)
    sub, lane = iota((8, 128), 0), iota((8, 128), 1)
    rate = prm[1]

    def by_head(product):
        dims = (((1,), (1,)), ((), ()))
        return lax.dot_general(indicator, product, dims, precision=HIGH, preferred_element_type=F32)

    for k in range(4):
        here = slice(128 * k, 128 * k + 128)
        rows, cols = rows_in[k], cols_in[k]
        carry, tail, thru = weights[k]
        b, c = bc[here, 0:128], bc[here, 128:256]
        carry_x = spread(lanes(carry))
        tail_x = spread(lanes(tail))
        step_x = spread([cols[:, 4 + h : 5 + h] for h in range(4)])
        state, grad = states[k].astype(BF16), grads[k].astype(BF16)
        probe = p[k, 0:128, :].astype(F32) * carry_x
        values = x[here, :] * tail_x
        carried = probe * dot_nt(c, state)
        pulled = dot_nt(b, grad)
        out[here, 0:256] = (dx[here, :] + tail_x * step_x * pulled).astype(BF16)
        d_b = dbc[here, 0:128] + dot_nn((values * step_x).astype(BF16), grad)
        d_c = dbc[here, 128:256] + dot_nn(probe.astype(BF16), state)
        out[here, 256:384] = d_b.astype(BF16)
        out[here, 384:512] = d_c.astype(BF16)
        from_carry = by_head(carried)
        from_tail = by_head(values * pulled)
        dt = pltpu.roll(rows[0:8], 4, 0)
        d_log = e[k, 8:16, :] + from_carry - dt * from_tail
        both = jnp.sum(grads[k] * states[k], axis=1, keepdims=True)
        end = jnp.sum(jnp.where(sub < 4, dt * from_tail, 0.0), axis=1, keepdims=True)
        for h in range(4):
            own = jnp.sum(both[64 * h : 64 * h + 64], axis=0, keepdims=True) * thru[:, h : h + 1]
            end = jnp.where(sub[:, 0:1] == h, end + own, end)
        d_log = jnp.where(lane == 127, d_log + end, d_log)
        d_step = jnp.dot(d_log, lower, precision=HIGH, preferred_element_type=F32)
        d_dt = e[k, 0:8, :] + from_tail - rate * d_step
        z = rows[8:16]
        d_z = jnp.where(sub < 4, d_dt / (1.0 + jnp.exp(-z)), 0.0)
        out[512:528, here] = jnp.concatenate([d_z, jnp.zeros((8, 128), F32)], axis=0).astype(BF16)


def finish(meta, *args):
    return pl.pallas_call(
        finish_kernel,
        in_specs=[SMEM] + [VMEM] * len(args),
        out_specs=VMEM,
        out_shape=jax.ShapeDtypeStruct((528, 512), BF16),
    )(meta, *args)


def pull_kernel(meta, g, *rest):
    blocks, oth, own, (buf, full, sems) = rest[:9], rest[9], rest[10], rest[11:]
    copies = start_copies(blocks, buf, sems)
    shared = g[0, 0:512, 256:512].astype(F32)
    for d in range(4):
        full[256 * d : 256 * d + 256, :] = g[d, 0:512, 0:256].astype(F32).T.astype(BF16)
        if d:
            shared += g[d, 0:512, 256:512].astype(F32)
    full[1024:1280, :] = shared.T.astype(BF16)
    top = iota((8, 512), 0) < 4
    steps = [g[d, 512:528, :].astype(F32)[0:8] for d in range(4)]
    pairs = [jnp.where(top, steps[2 * j], pltpu.roll(steps[2 * j + 1], 4, 0)) for j in range(2)]
    full[1280:1408, :] = jnp.concatenate(pairs + [jnp.zeros((112, 512), F32)], axis=0).astype(BF16)
    for i in range(8):
        for copy in copies[i]:
            copy.wait()
        place = ring_source(meta, i)
        part = dot_nn(buf[i], full[...]).T.astype(BF16)
        cols = pl.ds(pl.multiple_of(lax.rem(place, 4) * 256, 256), 256)
        mine = place // 4 == meta[0]

        def put(ref):
            for k in range(4):
                ref[lax.rem(k + meta[1], 4), :, cols] = part[128 * k : 128 * k + 128]

        @pl.when(mine)
        def _():
            put(own)

        @pl.when(jnp.logical_not(mine))
        def _():
            put(oth)


def pull(meta, g, blocks):
    return pl.pallas_call(
        pull_kernel,
        in_specs=[SMEM, VMEM] + [pl.BlockSpec(memory_space=pl.ANY)] * 9,
        out_specs=[VMEM] * 2,
        out_shape=[jax.ShapeDtypeStruct((4, 128, 1024), BF16)] * 2,
        scratch_shapes=[
            pltpu.VMEM((8, 256, WIDE), BF16),
            pltpu.VMEM((WIDE, 512), BF16),
            pltpu.SemaphoreType.DMA((9,)),
        ],
    )(meta, g, *blocks)


def to_all(x, axis):
    return lax.all_to_all(jnp.broadcast_to(x[None], (4,) + x.shape), axis, split_axis=0, concat_axis=0)


def shifted(x, axis, k):
    return lax.ppermute(x, axis, [(i, (i + k) % 4) for i in range(4)])


def sum_of_four(x, axis):
    return x + shifted(x, axis, 1) + shifted(x, axis, 2) + shifted(x, axis, 3)


SWAP = [(0, 1), (1, 0)]


def body(tokens, frame_feats, w_proj, frame_pos, segments, signs, w_x, w_bc, w_dt, dt_bias, decay_rate, skip_gain, probe):
    x_at, z_at, core_at = lax.axis_index(X), lax.axis_index("z"), lax.axis_index("core")
    across = lax.rem(z_at, 4)
    origin = 2 * lax.rem(across, 2) + across // 2
    quarter = 2 * lax.rem(origin, 2) + z_at // 4
    meta = jnp.stack([core_at, origin, quarter, z_at]).astype(jnp.int32)
    w_all = pack(w_x, w_bc, w_dt)

    def right(v):
        return lax.ppermute(v, "z", [(i, (i + 1) % 8) for i in range(8)])

    def left(v):
        return lax.ppermute(v, "z", [(i, (i + 7) % 8) for i in range(8)])

    frame_emb = jnp.dot(frame_feats[0], w_proj, preferred_element_type=F32).astype(BF16)
    slot = frame_pos[0] - CHUNK * (jnp.arange(32, dtype=jnp.int32) // 2)
    tagged = jnp.concatenate([frame_emb, jnp.broadcast_to(slot.astype(BF16)[:, None], (32, 128))], axis=1)
    arrived = lax.all_to_all(tagged, SEQ, split_axis=0, concat_axis=0, tiled=True)
    r1, l1 = right(w_all), left(w_all)
    local_pos = arrived[:, 1024].astype(jnp.int32)
    merged = tokens[0].at[local_pos].set(arrived[:, :1024])
    segment = segments[0]
    before = lax.ppermute(segment[-1:], X + ("z",), [(i, i + 1) for i in range(31)])

    merged, r1, l1 = lax.optimization_barrier((merged, r1, l1))
    moved = lax.ppermute(merged, AXES, features_route())
    r2, l2 = right(r1), left(l1)
    ids = jnp.concatenate([segment[None], jnp.broadcast_to(before[None], (15, CHUNK))]).astype(BF16)
    probe_ids = jnp.concatenate([probe[0], jnp.tile(ids, (1, 8))], axis=0)
    moved, r2, l2, probe_ids = lax.optimization_barrier((moved, r2, l2, probe_ids))
    r3, l3 = right(r2), left(l2)
    own = to_all(moved, "y")
    own, r3, l3, probe_ids = lax.optimization_barrier((own, r3, l3, probe_ids))
    r4, l4 = right(r3[:128]), left(l3[128:])
    probe_ids = lax.ppermute(probe_ids, X + ("z",), probe_route())
    oth = lax.ppermute(own, "core", SWAP)

    def four(v):
        return lax.dynamic_slice(v, (4 * x_at,), (4,))

    prm = jnp.stack([four(dt_bias), four(decay_rate)])
    prm = jnp.concatenate([prm, jnp.zeros((2, 4), F32)], axis=1)
    prm = jnp.broadcast_to(prm[:, :, None], (2, 8, 128))
    skip = jnp.repeat(four(skip_gain), 64)[None, :]

    blocks = [w_all, r1, l1, r2, l2, r3, l3]
    acc, last = project_most(meta, own, oth, blocks)
    partial_proj = project_last(last, acc, r4, l4, probe_ids)
    received = lax.all_to_all(partial_proj, X, split_axis=0, concat_axis=0)
    pay, values, bc, rows, cols, t_all, q_all, probes = prepare(meta, received, prm)
    got = [lax.ppermute(pay[k - 1], "z", quarter_route(k)) for k in (1, 2, 3)]
    dx, dbc, e = intra(values, bc, probes, rows, cols, skip)
    grads = finish(meta, *got, values, bc, probes, rows, cols, t_all, q_all, dx, dbc, e, prm)
    everyone = to_all(grads, X)
    oth_part, own_part = pull(meta, everyone, blocks + [r4, l4])
    swapped = lax.ppermute(oth_part, "core", SWAP)
    both = (own_part.astype(F32) + swapped.astype(F32)).astype(BF16)
    pieces = lax.all_to_all(both, "y", split_axis=0, concat_axis=0)
    away = jnp.sum(pieces.astype(F32), axis=0)
    squares = jnp.broadcast_to(jnp.sum(away * away), (8, 128))
    back = [(b, a) for a, b in features_route()]
    gradient = lax.ppermute(away.astype(BF16), AXES, back)
    squares = squares + lax.ppermute(squares, "core", SWAP)
    squares = sum_of_four(squares, X)
    squares = lax.ppermute(squares, AXES, back)[0, 0]

    direction = (2 * signs[0] - 1).astype(F32)[:, None]
    step = 0.5 * direction * gradient.astype(F32)
    picked = (direction.astype(BF16) * gradient)[local_pos]
    high = squares.astype(BF16)
    low = (squares - high.astype(F32)).astype(BF16)
    lane = jnp.arange(128)[None, :]
    tail = jnp.broadcast_to(jnp.where(lane < 64, high, low), (32, 128))
    returned = lax.all_to_all(jnp.concatenate([picked, tail], axis=1), SEQ, split_axis=0, concat_axis=0, tiled=True)
    sums = returned[::2, 1024:].astype(F32)
    entries = 2048 * 8192
    grad_scale = jnp.sqrt((jnp.sum(sums[:, 0]) + jnp.sum(sums[:, 64])) / entries + 1e-06)
    adv = (merged.astype(F32) + step / grad_scale).astype(BF16)
    adv_frames = (frame_emb.astype(F32) + 0.5 * returned[:, :1024].astype(F32) / grad_scale).astype(BF16)
    return (adv[None], adv_frames[None])


def solution(mesh):
    mesh = Mesh(mesh.devices.reshape(2, 2, 8, 4, 2), AXES)

    return jax.shard_map(
        body,
        mesh=mesh,
        in_specs=(
            P("x_hi", SEQ, TENSOR),
            P("x_hi", SEQ, None),
            P(None, TENSOR),
            P("x_hi", SEQ),
            P("x_hi", SEQ),
            P("x_hi", SEQ),
            P(("x_hi",) + SEQ, TENSOR),
            P(("x_hi",) + SEQ, TENSOR),
            P(("x_hi",) + SEQ, TENSOR),
            P(TENSOR),
            P(TENSOR),
            P(TENSOR),
            P("x_hi", SEQ, TENSOR),
        ),
        out_specs=(P("x_hi", SEQ, TENSOR), P("x_hi", SEQ, TENSOR)),
        check_vma=False,
    )
```

profile of v0, /device:TPU:4, one launch (start us, length us, event | category | flops | bytes accessed | tf_op | source)
XLA Modules:
  0.0 304.0 jit_solution(6601600058041289105)
XLA Ops:
  3.9 2.1 shard_map.140.rest_0_
  7.9 3.9 %collective-permute-start.1 = (bf16[256,1408]{1,0:T(8,128)(2,1)}, bf16[256,1408]{1,0:T(8,128)(2,1)}, u32[]{:S(2)}, u32[]{:S(2)}) collective-permute-start(bf16[256,1408]{1,0:T(8,128)(2,1)} %shard_map.140.rest_0_), channel_id=1, source_target_pairs={{0,56},{8,0},{16,8},{24,16},{32,24},{40,32},{48,40},{56,48},{1,57}... | collective-permute-start | bytes 2162696 | tf_op jit(solution)/shard_map/ppermute | solution.py:472
  14.0 17.6 %all_to_all.46 = bf16[16,2,1152]{2,1,0:T(2,128)(2,1)} all-to-all(bf16[16,2,1152]{2,1,0:T(2,128)(2,1)} %all_to_all.28), channel_id=1, replica_groups=mesh['x_hi'=2,'x_lo'=2,'z'=8,'y'=4,'core'=2] {'x_lo','z'}, dimensions={0} | all-to-all | bytes 147456 | tf_op jit(solution)/shard_map/all_to_all | solution.py:477
  32.6 2.4 scatter_custom_fusion
  35.0 3.4 %collective-permute-start.3 = (bf16[256,1408]{1,0:T(8,128)(2,1)S(1)}, bf16[256,1408]{1,0:T(8,128)(2,1)S(1)}, u32[]{:S(2)}, u32[]{:S(2)}) collective-permute-start(bf16[256,1408]{1,0:T(8,128)(2,1)S(1)} %collective-permute-done.rest_1_), channel_id=1, source_target_pairs={{0,8},{8,16},{16,24},{24,32},{32,40},{40,48},{48,56},{56,0},{1,9},... | collective-permute-start | bytes 2162696 | tf_op jit(solution)/shard_map/ppermute | solution.py:469
  38.4 6.8 %collective-permute-start.2 = (bf16[128,1024]{1,0:T(8,128)(2,1)}, bf16[128,1024]{1,0:T(8,128)(2,1)S(1)}, u32[]{:S(2)}, u32[]{:S(2)}) collective-permute-start(bf16[128,1024]{1,0:T(8,128)(2,1)} %scatter_custom_fusion), channel_id=1, source_target_pairs={{0,0},{1,1},{2,64},{3,65},{4,128},{5,129},{6,192},{7,193},{8,2},{9... | collective-permute-start | bytes 786440 | tf_op jit(solution)/shard_map/ppermute | solution.py:485
  45.8 2.3 collective-permute-start.5
  48.1 12.1 %collective-permute-done.5 = s32[1]{0:T(128)} collective-permute-done((s32[1]{0:T(128)}, s32[1]{0:T(128)}, u32[]{:S(2)}, u32[]{:S(2)}) %collective-permute-start.5) | collective-permute-done | bytes 36 | tf_op jit(solution)/shard_map/ppermute | solution.py:482
  64.7 12.6 %all-to-all-start.1 = ((bf16[4,128,1024]{2,1,0:T(8,128)(2,1)}), bf16[4,128,1024]{2,1,0:T(8,128)(2,1)}, u32[]{:S(2)}, u32[]{:S(2)}) async-start(bf16[4,128,1024]{2,1,0:T(8,128)(2,1)} %broadcast_in_dim.31), calls=%async_computation.1 | async-start | bytes 2097152 | tf_op jit(solution)/shard_map/all_to_all | solution.py:446
  77.3 3.2 %collective-permute-start.7 = (bf16[256,1408]{1,0:T(8,128)(2,1)}, bf16[256,1408]{1,0:T(8,128)(2,1)}, u32[]{:S(2)}, u32[]{:S(2)}) collective-permute-start(bf16[256,1408]{1,0:T(8,128)(2,1)} %collective-permute-done.4.rest_4_), channel_id=1, source_target_pairs={{0,56},{8,0},{16,8},{24,16},{32,24},{40,32},{48,40},{56,48},{1,57}... | collective-permute-start | bytes 2162696 | tf_op jit(solution)/shard_map/ppermute | solution.py:472
  80.6 12.5 %collective-permute-done.6.rest_5_ = bf16[256,1408]{1,0:T(8,128)(2,1)S(1)} collective-permute-done((bf16[256,1408]{1,0:T(8,128)(2,1)}, bf16[256,1408]{1,0:T(8,128)(2,1)S(1)}, u32[]{:S(2)}, u32[]{:S(2)}) %collective-permute-start.6) | collective-permute-done | bytes 720928 | tf_op jit(solution)/shard_map/ppermute | solution.py:469
  93.1 1.9 slice.47
  95.0 2.8 collective-permute-start.10
  101.3 8.6 %shard_map.141 = (f32[512,1408]{1,0:T(8,128)}, bf16[512,256]{1,0:T(8,128)(2,1)}) custom-call(s32[4]{0:T(128)} %pad_add_fusion.meta, bf16[4,128,1024]{2,1,0:T(8,128)(2,1)} %all-to-all-done.1.own, bf16[4,128,1024]{2,1,0:T(8,128)(2,1)} %collective-permute-done.8.oth, bf16[256,1408]{1,0:T(8,128)(2,1)} %shard_map.140.rest_0_, bf16[256,1408]{1,0:T(8,128)(2,1)} %copy-done.2, ...), custom_call_target="tpu_custom_call" | custom-call | tf_op jit(solution)/shard_map/pallas_call | solution.py:161
  109.9 9.8 %collective-permute-done.11.probe = bf16[144,1024]{1,0:T(8,128)(2,1)} collective-permute-done((bf16[144,1024]{1,0:T(8,128)(2,1)}, bf16[144,1024]{1,0:T(8,128)(2,1)}, u32[]{:S(2)}, u32[]{:S(2)}) %collective-permute-start.11) | collective-permute-done | bytes 294944 | tf_op jit(solution)/shard_map/ppermute | solution.py:494
  119.7 4.6 %shard_map.142 = bf16[4,592,512]{2,1,0:T(8,128)(2,1)} custom-call(bf16[512,256]{1,0:T(8,128)(2,1)} %get-tuple-element.38.rows, f32[512,1408]{1,0:T(8,128)} %get-tuple-element.39.acc, bf16[128,1408]{1,0:T(8,128)(2,1)} %collective-permute-done.9.upper.rest_7_, bf16[128,1408]{1,0:T(8,128)(2,1)} %collective-permute-done.10.lower.rest_8_, ...), custom_call_target="tpu_custom_call" | custom-call | tf_op jit(solution)/shard_map/pallas_call | solution.py:195
  124.3 8.2 %all-to-all-start.2 = ((bf16[4,592,512]{2,1,0:T(8,128)(2,1)}), bf16[4,592,512]{2,1,0:T(8,128)(2,1)}, u32[]{:S(2)}, u32[]{:S(2)}) async-start(bf16[4,592,512]{2,1,0:T(8,128)(2,1)} %shard_map.142), calls=%async_computation.2 | async-start | bytes 4849664 | tf_op jit(solution)/shard_map/all_to_all | solution.py:508
  132.5 28.7 %all-to-all-done.2.r = bf16[4,592,512]{2,1,0:T(8,128)(2,1)} async-done(((bf16[4,592,512]{2,1,0:T(8,128)(2,1)}), bf16[4,592,512]{2,1,0:T(8,128)(2,1)}, u32[]{:S(2)}, u32[]{:S(2)}) %all-to-all-start.2) | async-done | bytes 2424864 | tf_op jit(solution)/shard_map/all_to_all | solution.py:508
  161.9 6.1 %shard_map.143 = (bf16[3,272,128]{2,1,0:T(8,128)(2,1)}, f32[512,256]{1,0:T(8,128)}, bf16[512,256]{1,0:T(8,128)(2,1)}, f32[4,16,128]{2,1,0:T(8,128)}, f32[4,128,1...) custom-call(s32[4]{0:T(128)} %pad_add_fusion.meta, ...), custom_call_target="tpu_custom_call" | custom-call | tf_op jit(solution)/shard_map/pallas_call | solution.py:248
  169.0 3.9 %collective-permute-start.12 = (bf16[272,128]{1,0:T(8,128)(2,1)S(1)}, bf16[272,128]{1,0:T(8,128)(2,1)S(1)}, u32[]{:S(2)}, u32[]{:S(2)}) collective-permute-start(bf16[272,128]{1,0:T(8,128)(2,1)S(1)} %get-tuple-element.60), channel_id=1, source_target_pairs={{0,32},{8,40},{16,48},{24,56},{32,16},{40,24},{48,0},{56,8},{1,33}... | collective-permute-start | bytes 208904 | tf_op jit(solution)/shard_map/ppermute | solution.py:510
  176.8 4.5 %shard_map.144 = (f32[512,256]{1,0:T(8,128)}, f32[512,256]{1,0:T(8,128)}, f32[4,16,128]{2,1,0:T(8,128)}) custom-call(f32[512,256]{1,0:T(8,128)} %get-tuple-element.42.x, bf16[512,256]{1,0:T(8,128)(2,1)} %get-tuple-element.43.bc, bf16[4,128,256]{2,1,0:T(8,128)(2,1)} %get-tuple-element.44.p, f32[4,16,128]{2,1,0:T(8,128)} %get-tuple-element.45.rows_in, ...), custom_call_target="tpu_custom_call" | custom-call | tf_op jit(solution)/shard_map/pallas_call | solution.py:309
  183.8 7.0 %shard_map.145 = bf16[528,512]{1,0:T(8,128)(2,1)} custom-call(s32[4]{0:T(128)} %pad_add_fusion.meta, bf16[272,128]{1,0:T(8,128)(2,1)} %copy-done.5, bf16[272,128]{1,0:T(8,128)(2,1)} %copy-done.6, bf16[272,128]{1,0:T(8,128)(2,1)} %copy-done.7, f32[512,256]{1,0:T(8,128)} %get-tuple-element.42.x, bf16[512,256]{1,0:T(8,128)(2,1)} %get-tuple-element.43.bc, ...), custom_call_target="tpu_custom_call" | custom-call | tf_op jit(solution)/shard_map/pallas_call | solution.py:389
  192.0 29.2 %all_to_all.44.g = bf16[4,528,512]{2,1,0:T(8,128)(2,1)} all-to-all(bf16[4,528,512]{2,1,0:T(8,128)(2,1)S(1)} %broadcast_in_dim.34), channel_id=1, replica_groups=mesh['x_hi'=2,'x_lo'=2,'z'=8,'y'=4,'core'=2] {'x_hi','x_lo'}, dimensions={0} | all-to-all | bytes 4325376 | tf_op jit(solution)/shard_map/all_to_all | solution.py:446
  221.2 9.8 %shard_map.146 = (bf16[4,128,1024]{2,1,0:T(8,128)(2,1)}, bf16[4,128,1024]{2,1,0:T(8,128)(2,1)}) custom-call(s32[4]{0:T(128)} %pad_add_fusion.meta, bf16[4,528,512]{2,1,0:T(8,128)(2,1)} %all_to_all.44.g, bf16[256,1408]{1,0:T(8,128)(2,1)} %shard_map.140.rest_0_, bf16[256,1408]{1,0:T(8,128)(2,1)} %copy-done.2, ...), custom_call_target="tpu_custom_call" | custom-call | tf_op jit(solution)/shard_map/pallas_call | solution.py:432
  231.1 2.9 collective-permute-done.15
  235.6 19.8 %all_to_all.45 = bf16[4,128,1024]{2,1,0:T(8,128)(2,1)S(1)} all-to-all(bf16[4,128,1024]{2,1,0:T(8,128)(2,1)S(1)} %add_convert_fusion), channel_id=1, replica_groups=mesh['x_hi'=2,'x_lo'=2,'z'=8,'y'=4,'core'=2] {'y'}, dimensions={0} | all-to-all | bytes 2097152 | tf_op jit(solution)/shard_map/all_to_all | solution.py:517
  262.0 2.1 collective-permute-start.20
  264.1 3.1 %collective-permute-start.16 = (bf16[128,1024]{1,0:T(8,128)(2,1)S(1)}, bf16[128,1024]{1,0:T(8,128)(2,1)S(1)}, u32[]{:S(2)}, u32[]{:S(2)}) collective-permute-start(bf16[128,1024]{1,0:T(8,128)(2,1)S(1)} %get-tuple-element.57), channel_id=1, source_target_pairs={{0,0},{1,1},{64,2},{65,3},{128,4},{129,5},{192,6},{193,7},{2,8},{3... | collective-permute-start | bytes 786440 | tf_op jit(solution)/shard_map/ppermute | solution.py:521
  268.0 4.7 %collective-permute-start.21 = (f32[8,128]{1,0:T(8,128)S(1)}, f32[8,128]{1,0:T(8,128)S(1)}, u32[]{:S(2)}, u32[]{:S(2)}) collective-permute-start(f32[8,128]{1,0:T(8,128)S(1)} %add_add_fusion), channel_id=1, source_target_pairs={{0,0},{1,1},{64,2},{65,3},{128,4},{129,5},{192,6},{193,7},{2,8},{3... | collective-permute-start | bytes 12296 | tf_op jit(solution)/shard_map/ppermute | solution.py:524
  272.6 9.1 %collective-permute-done.21 = f32[8,128]{1,0:T(8,128)S(1)} collective-permute-done((f32[8,128]{1,0:T(8,128)S(1)}, f32[8,128]{1,0:T(8,128)S(1)}, u32[]{:S(2)}, u32[]{:S(2)}) %collective-permute-start.21) | collective-permute-done | bytes 4128 | tf_op jit(solution)/shard_map/ppermute | solution.py:524
  285.0 6.9 %all-to-all-start.5 = ((bf16[16,2,1152]{2,1,0:T(2,128)(2,1)}), bf16[16,2,1152]{2,1,0:T(2,128)(2,1)S(1)}, u32[]{:S(2)}, u32[]{:S(2)}) async-start(bf16[16,2,1152]{2,1,0:T(2,128)(2,1)} %all_to_all.35), calls=%async_computation.5 | async-start | bytes 147456 | tf_op jit(solution)/shard_map/all_to_all | solution.py:533
  291.9 8.5 %all-to-all-done.5 = bf16[16,2,1152]{2,1,0:T(2,128)(2,1)S(1)} async-done(((bf16[16,2,1152]{2,1,0:T(2,128)(2,1)}), bf16[16,2,1152]{2,1,0:T(2,128)(2,1)S(1)}, u32[]{:S(2)}, u32[]{:S(2)}) %all-to-all-start.5) | async-done | bytes 73760 | tf_op jit(solution)/shard_map/all_to_all | solution.py:533
  (106 shorter events, 38.8 us)
Async XLA Ops:
  0.6 11.2 %copy-start = (bf16[1280,1024]{1,0:T(8,128)(2,1)S(1)}, bf16[1280,1024]{1,0:T(8,128)(2,1)}, u32[]{:S(2)}) copy-start(bf16[1280,1024]{1,0:T(8,128)(2,1)} %param.15) | copy-start | bytes 7864324
  0.6 12.6 %copy-start.10 = (s32[1,32]{1,0:T(1,128)S(1)}, s32[1,32]{1,0:T(1,128)}, u32[]{:S(2)}) copy-start(s32[1,32]{1,0:T(1,128)} %param.16) | copy-start | bytes 388
  3.9 41.3 %copy-start.11 = (s32[1,128]{1,0:T(1,128)S(1)}, s32[1,128]{1,0:T(1,128)}, u32[]{:S(2)}) copy-start(s32[1,128]{1,0:T(1,128)} %param.17) | copy-start | bytes 1540
  6.0 29.1 %collective-permute-start = (bf16[256,1408]{1,0:T(8,128)(2,1)}, bf16[256,1408]{1,0:T(8,128)(2,1)S(1)}, u32[]{:S(2)}, u32[]{:S(2)}) collective-permute-start(bf16[256,1408]{1,0:T(8,128)(2,1)} %shard_map.140.rest_0_), channel_id=1, source_target_pairs={{0,8},{8,16},{16,24},{24,32},{32,40},{40,48},{48,56},{56,0},{1,9},... | collective-permute-start | bytes 2162696 | tf_op jit(solution)/shard_map/ppermute | solution.py:469
  7.9 27.2 %collective-permute-start.1 = (bf16[256,1408]{1,0:T(8,128)(2,1)}, bf16[256,1408]{1,0:T(8,128)(2,1)}, u32[]{:S(2)}, u32[]{:S(2)}) collective-permute-start(bf16[256,1408]{1,0:T(8,128)(2,1)} %shard_map.140.rest_0_), channel_id=1, source_target_pairs={{0,56},{8,0},{16,8},{24,16},{32,24},{40,32},{48,40},{56,48},{1,57}... | collective-permute-start | bytes 2162696 | tf_op jit(solution)/shard_map/ppermute | solution.py:472
  35.0 29.7 %copy-start.2 = (bf16[256,1408]{1,0:T(8,128)(2,1)}, bf16[256,1408]{1,0:T(8,128)(2,1)S(1)}, u32[]{:S(2)}) copy-start(bf16[256,1408]{1,0:T(8,128)(2,1)S(1)} %collective-permute-done.rest_1_) | copy-start | bytes 2162692
  35.0 27.6 %collective-permute-start.3 = (bf16[256,1408]{1,0:T(8,128)(2,1)S(1)}, bf16[256,1408]{1,0:T(8,128)(2,1)S(1)}, u32[]{:S(2)}, u32[]{:S(2)}) collective-permute-start(bf16[256,1408]{1,0:T(8,128)(2,1)S(1)} %collective-permute-done.rest_1_), channel_id=1, source_target_pairs={{0,8},{8,16},{16,24},{24,32},{32,40},{40,48},{48,56},{56,0},{1,9},... | collective-permute-start | bytes 2162696 | tf_op jit(solution)/shard_map/ppermute | solution.py:469
  38.4 25.2 %collective-permute-start.4 = (bf16[256,1408]{1,0:T(8,128)(2,1)}, bf16[256,1408]{1,0:T(8,128)(2,1)}, u32[]{:S(2)}, u32[]{:S(2)}) collective-permute-start(bf16[256,1408]{1,0:T(8,128)(2,1)} %collective-permute-done.1.rest_2_), channel_id=1, source_target_pairs={{0,56},{8,0},{16,8},{24,16},{32,24},{40,32},{48,40},{56,48},{1,57}... | collective-permute-start | bytes 2162696 | tf_op jit(solution)/shard_map/ppermute | solution.py:472
  38.4 24.2 %collective-permute-start.2 = (bf16[128,1024]{1,0:T(8,128)(2,1)}, bf16[128,1024]{1,0:T(8,128)(2,1)S(1)}, u32[]{:S(2)}, u32[]{:S(2)}) collective-permute-start(bf16[128,1024]{1,0:T(8,128)(2,1)} %scatter_custom_fusion), channel_id=1, source_target_pairs={{0,0},{1,1},{2,64},{3,65},{4,128},{5,129},{6,192},{7,193},{8,2},{9... | collective-permute-start | bytes 786440 | tf_op jit(solution)/shard_map/ppermute | solution.py:485
  45.8 14.4 %collective-permute-start.5 = (s32[1]{0:T(128)}, s32[1]{0:T(128)}, u32[]{:S(2)}, u32[]{:S(2)}) collective-permute-start(s32[1]{0:T(128)} %bitcast.9), channel_id=1, source_target_pairs={{0,8},{8,16},{16,24},{24,32},{32,40},{40,48},{48,56},{56,64},{64,7... | collective-permute-start | bytes 20 | tf_op jit(solution)/shard_map/ppermute | solution.py:482
  64.7 28.3 %all-to-all-start.1 = ((bf16[4,128,1024]{2,1,0:T(8,128)(2,1)}), bf16[4,128,1024]{2,1,0:T(8,128)(2,1)}, u32[]{:S(2)}, u32[]{:S(2)}) async-start(bf16[4,128,1024]{2,1,0:T(8,128)(2,1)} %broadcast_in_dim.31), calls=%async_computation.1 | async-start | bytes 2097152 | tf_op jit(solution)/shard_map/all_to_all | solution.py:446
  77.3 15.7 %collective-permute-start.6 = (bf16[256,1408]{1,0:T(8,128)(2,1)}, bf16[256,1408]{1,0:T(8,128)(2,1)S(1)}, u32[]{:S(2)}, u32[]{:S(2)}) collective-permute-start(bf16[256,1408]{1,0:T(8,128)(2,1)} %copy-done.3), channel_id=1, source_target_pairs={{0,8},{8,16},{16,24},{24,32},{32,40},{40,48},{48,56},{56,0},{1,9},... | collective-permute-start | bytes 2162696 | tf_op jit(solution)/shard_map/ppermute | solution.py:469
  77.3 15.7 %collective-permute-start.7 = (bf16[256,1408]{1,0:T(8,128)(2,1)}, bf16[256,1408]{1,0:T(8,128)(2,1)}, u32[]{:S(2)}, u32[]{:S(2)}) collective-permute-start(bf16[256,1408]{1,0:T(8,128)(2,1)} %collective-permute-done.4.rest_4_), channel_id=1, source_target_pairs={{0,56},{8,0},{16,8},{24,16},{32,24},{40,32},{48,40},{56,48},{1,57}... | collective-permute-start | bytes 2162696 | tf_op jit(solution)/shard_map/ppermute | solution.py:472
  93.0 8.2 %collective-permute-start.8 = (bf16[4,128,1024]{2,1,0:T(8,128)(2,1)}, bf16[4,128,1024]{2,1,0:T(8,128)(2,1)}, u32[]{:S(2)}, u32[]{:S(2)}) collective-permute-start(bf16[4,128,1024]{2,1,0:T(8,128)(2,1)} %all-to-all-done.1.own), channel_id=1, source_target_pairs={{0,1},{1,0},{2,3},{3,2},{4,5},{5,4},{6,7},{7,6},{8,9},{9,8},{10,11... | collective-permute-start | bytes 3145736 | tf_op jit(solution)/shard_map/ppermute | solution.py:495
  95.0 24.6 %collective-permute-start.10 = (bf16[128,1408]{1,0:T(8,128)(2,1)}, bf16[128,1408]{1,0:T(8,128)(2,1)}, u32[]{:S(2)}, u32[]{:S(2)}) collective-permute-start(bf16[128,1408]{1,0:T(8,128)(2,1)} %slice.47), channel_id=1, source_target_pairs={{0,56},{8,0},{16,8},{24,16},{32,24},{40,32},{48,40},{56,48},{1,57}... | collective-permute-start | bytes 1081352 | tf_op jit(solution)/shard_map/ppermute | solution.py:472
  98.6 21.1 %collective-permute-start.9 = (bf16[128,1408]{1,0:T(8,128)(2,1)}, bf16[128,1408]{1,0:T(8,128)(2,1)}, u32[]{:S(2)}, u32[]{:S(2)}) collective-permute-start(bf16[128,1408]{1,0:T(8,128)(2,1)} %slice.46), channel_id=1, source_target_pairs={{0,8},{8,16},{16,24},{24,32},{32,40},{40,48},{48,56},{56,0},{1,9},... | collective-permute-start | bytes 1081352 | tf_op jit(solution)/shard_map/ppermute | solution.py:469
  98.6 21.1 %collective-permute-start.11 = (bf16[144,1024]{1,0:T(8,128)(2,1)}, bf16[144,1024]{1,0:T(8,128)(2,1)}, u32[]{:S(2)}, u32[]{:S(2)}) collective-permute-start(bf16[144,1024]{1,0:T(8,128)(2,1)} %pad_maximum_fusion), channel_id=1, source_target_pairs={{0,0},{8,64},{16,128},{24,192},{32,32},{40,96},{48,160},{56,224},{... | collective-permute-start | bytes 884744 | tf_op jit(solution)/shard_map/ppermute | solution.py:494
  124.3 36.9 %all-to-all-start.2 = ((bf16[4,592,512]{2,1,0:T(8,128)(2,1)}), bf16[4,592,512]{2,1,0:T(8,128)(2,1)}, u32[]{:S(2)}, u32[]{:S(2)}) async-start(bf16[4,592,512]{2,1,0:T(8,128)(2,1)} %shard_map.142), calls=%async_computation.2 | async-start | bytes 4849664 | tf_op jit(solution)/shard_map/all_to_all | solution.py:508
  132.4 43.6 %copy-start.12 = (f32[16]{0:T(128)S(1)}, f32[16]{0:T(128)}, u32[]{:S(2)}) copy-start(f32[16]{0:T(128)} %param.24) | copy-start | bytes 196
  169.0 12.4 %collective-permute-start.12 = (bf16[272,128]{1,0:T(8,128)(2,1)S(1)}, bf16[272,128]{1,0:T(8,128)(2,1)S(1)}, u32[]{:S(2)}, u32[]{:S(2)}) collective-permute-start(bf16[272,128]{1,0:T(8,128)(2,1)S(1)} %get-tuple-element.60), channel_id=1, source_target_pairs={{0,32},{8,40},{16,48},{24,56},{32,16},{40,24},{48,0},{56,8},{1,33}... | collective-permute-start | bytes 208904 | tf_op jit(solution)/shard_map/ppermute | solution.py:510
  172.9 8.5 %collective-permute-start.13 = (bf16[272,128]{1,0:T(8,128)(2,1)S(1)}, bf16[272,128]{1,0:T(8,128)(2,1)S(1)}, u32[]{:S(2)}, u32[]{:S(2)}) collective-permute-start(bf16[272,128]{1,0:T(8,128)(2,1)S(1)} %get-tuple-element.59), channel_id=1, source_target_pairs={{0,16},{8,24},{16,0},{24,8},{32,48},{40,56},{48,32},{56,40},{1,17}... | collective-permute-start | bytes 208904 | tf_op jit(solution)/shard_map/ppermute | solution.py:510
  174.7 8.5 %collective-permute-start.14 = (bf16[272,128]{1,0:T(8,128)(2,1)S(1)}, bf16[272,128]{1,0:T(8,128)(2,1)S(1)}, u32[]{:S(2)}, u32[]{:S(2)}) collective-permute-start(bf16[272,128]{1,0:T(8,128)(2,1)S(1)} %get-tuple-element.58), channel_id=1, source_target_pairs={{0,48},{8,56},{16,32},{24,40},{32,0},{40,8},{48,16},{56,24},{1,49}... | collective-permute-start | bytes 208904 | tf_op jit(solution)/shard_map/ppermute | solution.py:510
  231.0 3.0 collective-permute-start.15
  235.6 28.5 %copy-start.13 = (s32[1,128]{1,0:T(1,128)S(1)}, s32[1,128]{1,0:T(1,128)}, u32[]{:S(2)}) copy-start(s32[1,128]{1,0:T(1,128)} %param.18) | copy-start | bytes 1540
  255.4 47.8 %copy-start.4 = (bf16[128,1024]{1,0:T(8,128)(2,1)S(1)}, bf16[128,1024]{1,0:T(8,128)(2,1)}, u32[]{:S(2)}) copy-start(bf16[128,1024]{1,0:T(8,128)(2,1)} %scatter_custom_fusion) | copy-start | bytes 786436
  256.9 1.3 collective-permute-start.17
  258.9 8.4 %collective-permute-start.18 = (f32[8,128]{1,0:T(8,128)S(1)}, f32[8,128]{1,0:T(8,128)S(1)}, u32[]{:S(2)}, u32[]{:S(2)}) collective-permute-start(f32[8,128]{1,0:T(8,128)S(1)} %broadcast_add_fusion), channel_id=1, source_target_pairs={{0,64},{64,128},{128,192},{192,0},{1,65},{65,129},{129,193},{193,1... | collective-permute-start | bytes 12296 | tf_op jit(solution)/shard_map/ppermute | solution.py:450
  260.6 6.7 %collective-permute-start.19 = (f32[8,128]{1,0:T(8,128)S(1)}, f32[8,128]{1,0:T(8,128)S(1)}, u32[]{:S(2)}, u32[]{:S(2)}) collective-permute-start(f32[8,128]{1,0:T(8,128)S(1)} %broadcast_add_fusion), channel_id=1, source_target_pairs={{0,128},{64,192},{128,0},{192,64},{1,129},{65,193},{129,1},{193,65... | collective-permute-start | bytes 12296 | tf_op jit(solution)/shard_map/ppermute | solution.py:450
  262.0 5.3 %collective-permute-start.20 = (f32[8,128]{1,0:T(8,128)S(1)}, f32[8,128]{1,0:T(8,128)S(1)}, u32[]{:S(2)}, u32[]{:S(2)}) collective-permute-start(f32[8,128]{1,0:T(8,128)S(1)} %broadcast_add_fusion), channel_id=1, source_target_pairs={{0,192},{64,0},{128,64},{192,128},{1,193},{65,1},{129,65},{193,129... | collective-permute-start | bytes 12296 | tf_op jit(solution)/shard_map/ppermute | solution.py:450
  264.1 19.5 %collective-permute-start.16 = (bf16[128,1024]{1,0:T(8,128)(2,1)S(1)}, bf16[128,1024]{1,0:T(8,128)(2,1)S(1)}, u32[]{:S(2)}, u32[]{:S(2)}) collective-permute-start(bf16[128,1024]{1,0:T(8,128)(2,1)S(1)} %get-tuple-element.57), channel_id=1, source_target_pairs={{0,0},{1,1},{64,2},{65,3},{128,4},{129,5},{192,6},{193,7},{2,8},{3... | collective-permute-start | bytes 786440 | tf_op jit(solution)/shard_map/ppermute | solution.py:521
  268.0 13.8 %collective-permute-start.21 = (f32[8,128]{1,0:T(8,128)S(1)}, f32[8,128]{1,0:T(8,128)S(1)}, u32[]{:S(2)}, u32[]{:S(2)}) collective-permute-start(f32[8,128]{1,0:T(8,128)S(1)} %add_add_fusion), channel_id=1, source_target_pairs={{0,0},{1,1},{64,2},{65,3},{128,4},{129,5},{192,6},{193,7},{2,8},{3... | collective-permute-start | bytes 12296 | tf_op jit(solution)/shard_map/ppermute | solution.py:524
  285.0 15.4 %all-to-all-start.5 = ((bf16[16,2,1152]{2,1,0:T(2,128)(2,1)}), bf16[16,2,1152]{2,1,0:T(2,128)(2,1)S(1)}, u32[]{:S(2)}, u32[]{:S(2)}) async-start(bf16[16,2,1152]{2,1,0:T(2,128)(2,1)} %all_to_all.35), calls=%async_computation.5 | async-start | bytes 147456 | tf_op jit(solution)/shard_map/all_to_all | solution.py:533
  (7 other events, 29.8 us)
where the time goes:
time: 305 us; the launch traced here: 304 us
  waiting for transfers between devices  86.5 us (28%)
  starting transfers between devices  74.3 us (24%)
  blocking collectives  66.5 us (22%)
  Pallas kernels  42.7 us (14%)
  local copies, waits for them, and re-layouts  19.5 us (6%)
  other arithmetic  8.77 us (3%)
  between operations  4.32 us (1%)
    all_to_all x1, blocking collectives, to_all(): lax.all_to_all(jnp.broadcast_to(x[None], (4,) + x.shape), axis, split_axi...  29.2 us
    all_to_all x1, waiting for transfers between devices, body(): received = lax.all_to_all(partial_proj, X, split_axis=0, concat_axis=0)  28.7 us
    all_to_all x1, blocking collectives, body(): pieces = lax.all_to_all(both, 'y', split_axis=0, concat_axis=0)  19.8 us
    all_to_all x1, blocking collectives, body(): lax.all_to_all(tagged, SEQ, split_axis=0, concat_axis=0, tiled=True)  17.6 us
    all_to_all x1, starting transfers between devices, to_all(): lax.all_to_all(jnp.broadcast_to(x[None], (4,) + x.shape), axis, split_axi...  12.6 us
    ppermute x4, waiting for transfers between devices, right(): return lax.ppermute(v, 'z', [(i, (i + 1) % 8) for i in range(8)])  12.5 us
    ppermute x1, waiting for transfers between devices, body(): lax.ppermute(segment[-1:], X + ('z',), [(i, i + 1) for i in range(31)])  12.1 us
    ppermute x4, starting transfers between devices, left(): return lax.ppermute(v, 'z', [(i, (i + 7) % 8) for i in range(8)])  9.98 us
  transfers between devices with their start and end apart: 25, of which 9 were waited for; matrix products, arithmetic and copies ran while one was open for 4% of the time, Pallas kernels for 4%

commit v1 on v0

--- a/solution.py
+++ b/solution.py
@@ -111,74 +111,31 @@
     )(*parts)
 
 
-def ring_source(meta, i):
-    offset = (0, 7, 1, 6, 2, 5, 3, 4)[i]
-    return lax.rem(meta[3] + offset, 8)
-
-
-def start_copies(blocks, buf, sems):
+TILES = [(256 * t, min(256 * t + 256, WIDE)) for t in range(6)]
+ANY = pl.BlockSpec(memory_space=pl.ANY)
+
+
+def project_kernel(meta, own, oth, w, probe, out, buf, rows, sems):
     copies = []
-    for i, ref in enumerate(blocks[:7]):
-        copies.append([pltpu.make_async_copy(ref, buf.at[i], sems.at[i])])
-    if len(blocks) == 9:
-        halves = [pltpu.make_async_copy(blocks[7 + n], buf.at[7, pl.ds(128 * n, 128)], sems.at[7 + n]) for n in range(2)]
-        copies.append(halves)
-    for group in copies:
-        for copy in group:
-            copy.start()
-    return copies
-
-
-def feature_columns(meta, own, oth, place):
-    half, cols = place // 4, pl.ds(pl.multiple_of(lax.rem(place, 4) * 256, 256), 256)
-    mine = half == meta[0]
-    parts = []
-    for k in range(4):
-        at = lax.rem(k + meta[1], 4)
-        parts.append(jnp.where(mine, own[at, :, cols].astype(F32), oth[at, :, cols].astype(F32)).astype(BF16))
-    return jnp.concatenate(parts, axis=0)
-
-
-TILES = [(256 * t, min(256 * t + 256, WIDE)) for t in range(6)]
-
-
-def project_most_kernel(meta, own, oth, *rest):
-    blocks, (acc, last), (buf, rows, sems) = rest[:7], rest[7:9], rest[9:]
-    copies = start_copies(blocks, buf, sems)
-    for i in range(7):
-        rows[i] = feature_columns(meta, own, oth, ring_source(meta, i))
-    last[...] = feature_columns(meta, own, oth, ring_source(meta, 7))
-    for group in copies:
-        group[0].wait()
-    for lo, hi in TILES:
-        total = dot_nn(rows[0], buf[0, :, lo:hi])
-        for i in range(1, 7):
-            total += dot_nn(rows[i], buf[i, :, lo:hi])
-        acc[:, lo:hi] = total
-
-
-def project_most(meta, own, oth, blocks):
-    return pl.pallas_call(
-        project_most_kernel,
-        in_specs=[SMEM, VMEM, VMEM] + [pl.BlockSpec(memory_space=pl.ANY)] * 7,
-        out_specs=[VMEM] * 2,
-        out_shape=[jax.ShapeDtypeStruct((512, WIDE), F32), jax.ShapeDtypeStruct((512, 256), BF16)],
-        scratch_shapes=[
-            pltpu.VMEM((7, 256, WIDE), BF16),
-            pltpu.VMEM((7, 512, 256), BF16),
-            pltpu.SemaphoreType.DMA((7,)),
-        ],
-    )(meta, own, oth, *blocks)
-
-
-def project_last_kernel(rows, acc, upper, lower, probe, out):
+    for t, (lo, hi) in enumerate(TILES):
+        for n in range(2):
+            here = pl.ds(pl.multiple_of(lax.rem(meta[0] + n, 2) * 1024, 1024), 1024)
+            there = buf.at[1024 * n : 1024 * n + 1024, lo:hi]
+            copies.append(pltpu.make_async_copy(w.at[here, lo:hi], there, sems.at[2 * t + n]))
+    for copy in copies:
+        copy.start()
+    for n, ref in enumerate((own, oth)):
+        for k in range(4):
+            rows[128 * k : 128 * k + 128, 1024 * n : 1024 * n + 1024] = ref[lax.rem(k + meta[1], 4)]
     ids = probe[128:144, 0:512].astype(F32)[0:8]
     for d in range(4):
         part = slice(256 * d, 256 * d + 256)
         out[d, 528:592, 0:256] = probe[0:64, part]
         out[d, 528:592, 256:512] = probe[64:128, part]
     for t, (lo, hi) in enumerate(TILES):
-        total = acc[:, lo:hi] + dot_nn(rows[:, 0:128], upper[:, lo:hi]) + dot_nn(rows[:, 128:256], lower[:, lo:hi])
+        copies[2 * t].wait()
+        copies[2 * t + 1].wait()
+        total = dot_nn(rows[...], buf[:, lo:hi])
         if t < 4:
             out[t, 0:512, 0:256] = total.astype(BF16)
         elif t == 4:
@@ -191,13 +148,18 @@
                 out[d, 512:528, :] = mine.astype(BF16)
 
 
-def project_last(*args):
-    return pl.pallas_call(
-        project_last_kernel,
-        in_specs=[VMEM] * 5,
+def project(meta, own, oth, w, probe):
+    return pl.pallas_call(
+        project_kernel,
+        in_specs=[SMEM, VMEM, VMEM, ANY, VMEM],
         out_specs=VMEM,
         out_shape=jax.ShapeDtypeStruct((4, 592, 512), BF16),
-    )(*args)
+        scratch_shapes=[
+            pltpu.VMEM((2048, WIDE), BF16),
+            pltpu.VMEM((512, 2048), BF16),
+            pltpu.SemaphoreType.DMA((12,)),
+        ],
+    )(meta, own, oth, w, probe)
 
 
 def prepare_kernel(meta, r, prm, pay, x, bc, rows_out, cols_out, t_out, q_out, p):
@@ -394,9 +356,26 @@
     )(meta, *args)
 
 
-def pull_kernel(meta, g, *rest):
-    blocks, oth, own, (buf, full, sems) = rest[:9], rest[9], rest[10], rest[11:]
-    copies = start_copies(blocks, buf, sems)
+def pull_half(flip, meta, w, full, out, buf, sems):
+    half = lax.rem(meta[0] + flip, 2) * 1024
+    copies = []
+    for j in range(4):
+        here = pl.ds(pl.multiple_of(half + 256 * j, 256), 256)
+        copies.append(pltpu.make_async_copy(w.at[here], buf.at[j], sems.at[j]))
+    for copy in copies:
+        copy.start()
+    yield
+    for j in range(4):
+        copies[j].wait()
+        part = dot_nn(buf[j], full[...]).T.astype(BF16)
+        for k in range(4):
+            out[lax.rem(k + meta[1], 4), :, 256 * j : 256 * j + 256] = part[128 * k : 128 * k + 128]
+    yield
+
+
+def pull_first_kernel(meta, g, w, full, out, buf, sems):
+    phases = pull_half(1, meta, w, full, out, buf, sems)
+    next(phases)
     shared = g[0, 0:512, 256:512].astype(F32)
     for d in range(4):
         full[256 * d : 256 * d + 256, :] = g[d, 0:512, 0:256].astype(F32).T.astype(BF16)
@@ -407,39 +386,36 @@
     steps = [g[d, 512:528, :].astype(F32)[0:8] for d in range(4)]
     pairs = [jnp.where(top, steps[2 * j], pltpu.roll(steps[2 * j + 1], 4, 0)) for j in range(2)]
     full[1280:1408, :] = jnp.concatenate(pairs + [jnp.zeros((112, 512), F32)], axis=0).astype(BF16)
-    for i in range(8):
-        for copy in copies[i]:
-            copy.wait()
-        place = ring_source(meta, i)
-        part = dot_nn(buf[i], full[...]).T.astype(BF16)
-        cols = pl.ds(pl.multiple_of(lax.rem(place, 4) * 256, 256), 256)
-        mine = place // 4 == meta[0]
-
-        def put(ref):
-            for k in range(4):
-                ref[lax.rem(k + meta[1], 4), :, cols] = part[128 * k : 128 * k + 128]
-
-        @pl.when(mine)
-        def _():
-            put(own)
-
-        @pl.when(jnp.logical_not(mine))
-        def _():
-            put(oth)
-
-
-def pull(meta, g, blocks):
-    return pl.pallas_call(
-        pull_kernel,
-        in_specs=[SMEM, VMEM] + [pl.BlockSpec(memory_space=pl.ANY)] * 9,
+    next(phases)
+
+
+def pull_second_kernel(meta, full, w, out, buf, sems):
+    for _ in pull_half(0, meta, w, full, out, buf, sems):
+        pass
+
+
+PULL_SCRATCH = [pltpu.VMEM((4, 256, WIDE), BF16), pltpu.SemaphoreType.DMA((4,))]
+PULLED = jax.ShapeDtypeStruct((4, 128, 1024), BF16)
+
+
+def pull_first(meta, g, w):
+    return pl.pallas_call(
+        pull_first_kernel,
+        in_specs=[SMEM, VMEM, ANY],
         out_specs=[VMEM] * 2,
-        out_shape=[jax.ShapeDtypeStruct((4, 128, 1024), BF16)] * 2,
-        scratch_shapes=[
-            pltpu.VMEM((8, 256, WIDE), BF16),
-            pltpu.VMEM((WIDE, 512), BF16),
-            pltpu.SemaphoreType.DMA((9,)),
-        ],
-    )(meta, g, *blocks)
+        out_shape=[jax.ShapeDtypeStruct((WIDE, 512), BF16), PULLED],
+        scratch_shapes=PULL_SCRATCH,
+    )(meta, g, w)
+
+
+def pull_second(meta, full, w):
+    return pl.pallas_call(
+        pull_second_kernel,
+        in_specs=[SMEM, VMEM, ANY],
+        out_specs=VMEM,
+        out_shape=PULLED,
+        scratch_shapes=PULL_SCRATCH,
+    )(meta, full, w)
 
 
 def to_all(x, axis):
@@ -465,33 +441,22 @@
     meta = jnp.stack([core_at, origin, quarter, z_at]).astype(jnp.int32)
     w_all = pack(w_x, w_bc, w_dt)
 
-    def right(v):
-        return lax.ppermute(v, "z", [(i, (i + 1) % 8) for i in range(8)])
-
-    def left(v):
-        return lax.ppermute(v, "z", [(i, (i + 7) % 8) for i in range(8)])
+    weights = lax.all_gather(w_all, "z", axis=0, tiled=True)
 
     frame_emb = jnp.dot(frame_feats[0], w_proj, preferred_element_type=F32).astype(BF16)
     slot = frame_pos[0] - CHUNK * (jnp.arange(32, dtype=jnp.int32) // 2)
     tagged = jnp.concatenate([frame_emb, jnp.broadcast_to(slot.astype(BF16)[:, None], (32, 128))], axis=1)
     arrived = lax.all_to_all(tagged, SEQ, split_axis=0, concat_axis=0, tiled=True)
-    r1, l1 = right(w_all), left(w_all)
+    segment = segments[0]
+    before = lax.ppermute(segment[-1:], X + ("z",), [(i, i + 1) for i in range(31)])
+    ids = jnp.concatenate([segment[None], jnp.broadcast_to(before[None], (15, CHUNK))]).astype(BF16)
+    probe_ids = jnp.concatenate([probe[0], jnp.tile(ids, (1, 8))], axis=0)
     local_pos = arrived[:, 1024].astype(jnp.int32)
     merged = tokens[0].at[local_pos].set(arrived[:, :1024])
-    segment = segments[0]
-    before = lax.ppermute(segment[-1:], X + ("z",), [(i, i + 1) for i in range(31)])
-
-    merged, r1, l1 = lax.optimization_barrier((merged, r1, l1))
     moved = lax.ppermute(merged, AXES, features_route())
-    r2, l2 = right(r1), left(l1)
-    ids = jnp.concatenate([segment[None], jnp.broadcast_to(before[None], (15, CHUNK))]).astype(BF16)
-    probe_ids = jnp.concatenate([probe[0], jnp.tile(ids, (1, 8))], axis=0)
-    moved, r2, l2, probe_ids = lax.optimization_barrier((moved, r2, l2, probe_ids))
-    r3, l3 = right(r2), left(l2)
+    moved, probe_ids = lax.optimization_barrier((moved, probe_ids))
+    probe_ids = lax.ppermute(probe_ids, X + ("z",), probe_route())
     own = to_all(moved, "y")
-    own, r3, l3, probe_ids = lax.optimization_barrier((own, r3, l3, probe_ids))
-    r4, l4 = right(r3[:128]), left(l3[128:])
-    probe_ids = lax.ppermute(probe_ids, X + ("z",), probe_route())
     oth = lax.ppermute(own, "core", SWAP)
 
     def four(v):
@@ -502,17 +467,16 @@
     prm = jnp.broadcast_to(prm[:, :, None], (2, 8, 128))
     skip = jnp.repeat(four(skip_gain), 64)[None, :]
 
-    blocks = [w_all, r1, l1, r2, l2, r3, l3]
-    acc, last = project_most(meta, own, oth, blocks)
-    partial_proj = project_last(last, acc, r4, l4, probe_ids)
+    partial_proj = project(meta, own, oth, weights, probe_ids)
     received = lax.all_to_all(partial_proj, X, split_axis=0, concat_axis=0)
     pay, values, bc, rows, cols, t_all, q_all, probes = prepare(meta, received, prm)
     got = [lax.ppermute(pay[k - 1], "z", quarter_route(k)) for k in (1, 2, 3)]
     dx, dbc, e = intra(values, bc, probes, rows, cols, skip)
     grads = finish(meta, *got, values, bc, probes, rows, cols, t_all, q_all, dx, dbc, e, prm)
     everyone = to_all(grads, X)
-    oth_part, own_part = pull(meta, everyone, blocks + [r4, l4])
+    full, oth_part = pull_first(meta, everyone, weights)
     swapped = lax.ppermute(oth_part, "core", SWAP)
+    own_part = pull_second(meta, full, weights)
     both = (own_part.astype(F32) + swapped.astype(F32)).astype(BF16)
     pieces = lax.all_to_all(both, "y", split_axis=0, concat_axis=0)
     away = jnp.sum(pieces.astype(F32), axis=0)

time: 305 us -> 312 us (1.023)
  blocking collectives: 66.5 us -> 84.7 us
  starting transfers between devices: 74.3 us -> 57.8 us
  between operations: 4.32 us -> 17.7 us
  local copies, waits for them, and re-layouts: 19.5 us -> 10.2 us
    all_to_all x1 -> x2, blocking collectives: 29.2 us -> 47.4 us  [to_all(): lax.all_to_all(jnp.broadcast_to(x[None], (4,) + x.shape), axis, split_axi...]
    ppermute x1, waiting for transfers between devices: 9.82 us -> 25.1 us  [body(): probe_ids = lax.ppermute(probe_ids, X + ('z',), probe_route())]
    ppermute x8 -> x0, starting transfers between devices: 15.3 us -> none  [the longest x4 9.98 us: left(): return lax.ppermute(v, 'z', [(i, (i + 7) % 8) for i in range(8)])]
    all_to_all x1 -> x0, starting transfers between devices: 12.6 us -> none  [to_all(): lax.all_to_all(jnp.broadcast_to(x[None], (4,) + x.shape), axis, split_axi...]
    ppermute x8 -> x0, waiting for transfers between devices: 12.5 us -> none  [the longest x4 12.5 us: right(): return lax.ppermute(v, 'z', [(i, (i + 1) % 8) for i in range(8)])]
    all_to_all x1, starting transfers between devices: 8.18 us -> 18.2 us  [body(): received = lax.all_to_all(partial_proj, X, split_axis=0, concat_axis=0)]
    ppermute x1, waiting for transfers between devices: 0.01 us -> 8.61 us  [body(): moved = lax.ppermute(merged, AXES, features_route())]
    ppermute x1, waiting for transfers between devices: 12.1 us -> 8.57 us  [body(): lax.ppermute(segment[-1:], X + ('z',), [(i, i + 1) for i in range(31)])]
  transfers between devices with their start and end apart: 25 -> 17, of which waited for: 9 -> 8; matrix products, arithmetic and copies ran while one was open for 4% -> 2% of each run, Pallas kernels for 4% -> 3%
where the time goes in v1:
time: 312 us; the launch traced here: 311 us
  waiting for transfers between devices  87.9 us (28%)
  blocking collectives  84.7 us (27%)
  starting transfers between devices  57.8 us (19%)
  Pallas kernels  44.1 us (14%)
  between operations  17.7 us (6%)
  local copies, waits for them, and re-layouts  10.2 us (3%)
  other arithmetic  8.21 us (3%)
    all_to_all x2, blocking collectives, to_all(): lax.all_to_all(jnp.broadcast_to(x[None], (4,) + x.shape), axis, split_axi...  47.4 us
    all_to_all x1, waiting for transfers between devices, body(): received = lax.all_to_all(partial_proj, X, split_axis=0, concat_axis=0)  27 us
    ppermute x1, waiting for transfers between devices, body(): probe_ids = lax.ppermute(probe_ids, X + ('z',), probe_route())  25.1 us
    all_to_all x1, blocking collectives, body(): pieces = lax.all_to_all(both, 'y', split_axis=0, concat_axis=0)  19.8 us
    all_to_all x1, starting transfers between devices, body(): received = lax.all_to_all(partial_proj, X, split_axis=0, concat_axis=0)  18.2 us
    all_to_all x1, blocking collectives, body(): lax.all_to_all(tagged, SEQ, split_axis=0, concat_axis=0, tiled=True)  17.5 us
    pallas_call x1, Pallas kernels, project(): pl.pallas_call(project_kernel, in_specs=[SMEM, VMEM, VMEM, ANY, VMEM], ou...  11.9 us
    ppermute x1, waiting for transfers between devices, body(): moved = lax.ppermute(merged, AXES, features_route())  8.61 us
  transfers between devices with their start and end apart: 17, of which 8 were waited for; matrix products, arithmetic and copies ran while one was open for 2% of the time, Pallas kernels for 3%

profile of v1, /device:TPU:4, one launch (start us, length us, event | category | flops | bytes accessed | tf_op | source)
XLA Modules:
  0.0 311.2 jit_solution(6826551478450861542)
XLA Ops:
  7.2 1.6 copy.16.w_dt
  8.8 2.1 shard_map.140
  11.7 17.5 %all_to_all.47 = bf16[16,2,1152]{2,1,0:T(2,128)(2,1)S(1)} all-to-all(bf16[16,2,1152]{2,1,0:T(2,128)(2,1)S(1)} %all_to_all.28), channel_id=1, replica_groups=mesh['x_hi'=2,'x_lo'=2,'z'=8,'y'=4,'core'=2] {'x_lo','z'}, dimensions={0} | all-to-all | bytes 147456 | tf_op jit(solution)/shard_map/all_to_all | solution.py:449
  30.3 5.7 %collective-permute-start = (bf16[128,1024]{1,0:T(8,128)(2,1)S(1)}, bf16[128,1024]{1,0:T(8,128)(2,1)S(1)}, u32[]{:S(2)}, u32[]{:S(2)}) collective-permute-start(bf16[128,1024]{1,0:T(8,128)(2,1)S(1)} %scatter_custom_fusion), channel_id=1, source_target_pairs={{0,0},{1,1},{2,64},{3,65},{4,128},{5,129},{6,192},{7,193},{8,2},{9... | collective-permute-start | bytes 786440 | tf_op jit(solution)/shard_map/ppermute | solution.py:456
  36.7 2.4 collective-permute-start.1
  39.1 8.6 %collective-permute-done.1 = s32[1]{0:T(128)} collective-permute-done((s32[1]{0:T(128)}, s32[1]{0:T(128)}, u32[]{:S(2)}, u32[]{:S(2)}) %collective-permute-start.1) | collective-permute-done | bytes 36 | tf_op jit(solution)/shard_map/ppermute | solution.py:451
  49.2 8.6 %collective-permute-done = bf16[128,1024]{1,0:T(8,128)(2,1)S(1)} collective-permute-done((bf16[128,1024]{1,0:T(8,128)(2,1)S(1)}, bf16[128,1024]{1,0:T(8,128)(2,1)S(1)}, u32[]{:S(2)}, u32[]{:S(2)}) %collective-permute-start) | collective-permute-done | bytes 262176 | tf_op jit(solution)/shard_map/ppermute | solution.py:456
  58.0 18.8 %all_to_all.44.own = bf16[4,128,1024]{2,1,0:T(8,128)(2,1)} all-to-all(bf16[4,128,1024]{2,1,0:T(8,128)(2,1)S(1)} %broadcast_in_dim.31), channel_id=1, replica_groups=mesh['x_hi'=2,'x_lo'=2,'z'=8,'y'=4,'core'=2] {'y'}, dimensions={0} | all-to-all | bytes 2097152 | tf_op jit(solution)/shard_map/all_to_all | solution.py:422
  76.7 1.9 collective-permute-start.3
  79.3 25.1 %collective-permute-done.3.probe = bf16[144,1024]{1,0:T(8,128)(2,1)} collective-permute-done((bf16[144,1024]{1,0:T(8,128)(2,1)S(1)}, bf16[144,1024]{1,0:T(8,128)(2,1)}, u32[]{:S(2)}, u32[]{:S(2)}) %collective-permute-start.3) | collective-permute-done | bytes 294944 | tf_op jit(solution)/shard_map/ppermute | solution.py:458
  104.4 11.9 %shard_map.141 = bf16[4,592,512]{2,1,0:T(8,128)(2,1)} custom-call(s32[4]{0:T(128)} %pad_add_fusion.meta, bf16[4,128,1024]{2,1,0:T(8,128)(2,1)} %all_to_all.44.own, bf16[4,128,1024]{2,1,0:T(8,128)(2,1)} %collective-permute-done.2.oth, bf16[2048,1408]{1,0:T(8,128)(2,1)} %all-gather.2.cloned.1.call-done.w, bf16[144,1024]{1,0:T(8,128)(2,1)} %collective-permute-done.3.probe), custom_call_target="tpu_custom_call" | custom-call | tf_op jit(solution)/shard_map/pallas_call | solution.py:152
  116.3 18.2 %all-to-all-start.2 = ((bf16[4,592,512]{2,1,0:T(8,128)(2,1)}), bf16[4,592,512]{2,1,0:T(8,128)(2,1)}, u32[]{:S(2)}, u32[]{:S(2)}) async-start(bf16[4,592,512]{2,1,0:T(8,128)(2,1)} %shard_map.141), calls=%async_computation.2 | async-start | bytes 4849664 | tf_op jit(solution)/shard_map/all_to_all | solution.py:471
  134.6 27.0 %all-to-all-done.2.r = bf16[4,592,512]{2,1,0:T(8,128)(2,1)} async-done(((bf16[4,592,512]{2,1,0:T(8,128)(2,1)}), bf16[4,592,512]{2,1,0:T(8,128)(2,1)}, u32[]{:S(2)}, u32[]{:S(2)}) %all-to-all-start.2) | async-done | bytes 2424864 | tf_op jit(solution)/shard_map/all_to_all | solution.py:471
  162.3 6.2 %shard_map.142 = (bf16[3,272,128]{2,1,0:T(8,128)(2,1)}, f32[512,256]{1,0:T(8,128)}, bf16[512,256]{1,0:T(8,128)(2,1)}, f32[4,16,128]{2,1,0:T(8,128)}, f32[4,128,1...) custom-call(s32[4]{0:T(128)} %pad_add_fusion.meta, ...), custom_call_target="tpu_custom_call" | custom-call | tf_op jit(solution)/shard_map/pallas_call | solution.py:210
  169.4 4.9 %collective-permute-start.4 = (bf16[272,128]{1,0:T(8,128)(2,1)S(1)}, bf16[272,128]{1,0:T(8,128)(2,1)S(1)}, u32[]{:S(2)}, u32[]{:S(2)}) collective-permute-start(bf16[272,128]{1,0:T(8,128)(2,1)S(1)} %get-tuple-element.38), channel_id=1, source_target_pairs={{0,32},{8,40},{16,48},{24,56},{32,16},{40,24},{48,0},{56,8},{1,33}... | collective-permute-start | bytes 208904 | tf_op jit(solution)/shard_map/ppermute | solution.py:473
  175.7 4.6 %shard_map.143 = (f32[512,256]{1,0:T(8,128)}, f32[512,256]{1,0:T(8,128)}, f32[4,16,128]{2,1,0:T(8,128)}) custom-call(f32[512,256]{1,0:T(8,128)} %get-tuple-element.20.x, bf16[512,256]{1,0:T(8,128)(2,1)} %get-tuple-element.21.bc, bf16[4,128,256]{2,1,0:T(8,128)(2,1)} %get-tuple-element.22.p, f32[4,16,128]{2,1,0:T(8,128)} %get-tuple-element.23.rows_in, ...), custom_call_target="tpu_custom_call" | custom-call | tf_op jit(solution)/shard_map/pallas_call | solution.py:271
  180.3 2.2 collective-permute-done.6.r3
  183.2 7.0 %shard_map.144 = bf16[528,512]{1,0:T(8,128)(2,1)} custom-call(s32[4]{0:T(128)} %pad_add_fusion.meta, bf16[272,128]{1,0:T(8,128)(2,1)} %copy-done.3, bf16[272,128]{1,0:T(8,128)(2,1)} %copy-done.4, bf16[272,128]{1,0:T(8,128)(2,1)} %copy-done.5, f32[512,256]{1,0:T(8,128)} %get-tuple-element.20.x, bf16[512,256]{1,0:T(8,128)(2,1)} %get-tuple-element.21.bc, ...), custom_call_target="tpu_custom_call" | custom-call | tf_op jit(solution)/shard_map/pallas_call | solution.py:351
  190.2 1.2 broadcast_in_dim.34
  191.4 28.6 %all_to_all.45.g = bf16[4,528,512]{2,1,0:T(8,128)(2,1)} all-to-all(bf16[4,528,512]{2,1,0:T(8,128)(2,1)S(1)} %broadcast_in_dim.34), channel_id=1, replica_groups=mesh['x_hi'=2,'x_lo'=2,'z'=8,'y'=4,'core'=2] {'x_hi','x_lo'}, dimensions={0} | all-to-all | bytes 4325376 | tf_op jit(solution)/shard_map/all_to_all | solution.py:422
  220.0 6.3 %shard_map.145 = (bf16[1408,512]{1,0:T(8,128)(2,1)}, bf16[4,128,1024]{2,1,0:T(8,128)(2,1)}) custom-call(s32[4]{0:T(128)} %pad_add_fusion.meta, bf16[4,528,512]{2,1,0:T(8,128)(2,1)} %all_to_all.45.g, bf16[2048,1408]{1,0:T(8,128)(2,1)} %all-gather.2.cloned.1.call-done.w), custom_call_target="tpu_custom_call" | custom-call | tf_op jit(solution)/shard_map/pallas_call | solution.py:402
  226.4 6.1 %shard_map.146 = bf16[4,128,1024]{2,1,0:T(8,128)(2,1)} custom-call(s32[4]{0:T(128)} %pad_add_fusion.meta, bf16[1408,512]{1,0:T(8,128)(2,1)} %get-tuple-element.30.full, bf16[2048,1408]{1,0:T(8,128)(2,1)} %all-gather.2.cloned.1.call-done.w), custom_call_target="tpu_custom_call" | custom-call | tf_op jit(solution)/shard_map/pallas_call | solution.py:412
  232.5 1.9 add_convert_fusion
  234.5 19.8 %all_to_all.46 = bf16[4,128,1024]{2,1,0:T(8,128)(2,1)S(1)} all-to-all(bf16[4,128,1024]{2,1,0:T(8,128)(2,1)S(1)} %add_convert_fusion), channel_id=1, replica_groups=mesh['x_hi'=2,'x_lo'=2,'z'=8,'y'=4,'core'=2] {'y'}, dimensions={0} | all-to-all | bytes 2097152 | tf_op jit(solution)/shard_map/all_to_all | solution.py:481
  257.8 1.7 collective-permute-start.10
  259.5 1.5 collective-permute-start.11
  261.0 2.1 collective-permute-start.12
  263.0 3.1 %collective-permute-start.8 = (bf16[128,1024]{1,0:T(8,128)(2,1)S(1)}, bf16[128,1024]{1,0:T(8,128)(2,1)S(1)}, u32[]{:S(2)}, u32[]{:S(2)}) collective-permute-start(bf16[128,1024]{1,0:T(8,128)(2,1)S(1)} %get-tuple-element.35), channel_id=1, source_target_pairs={{0,0},{1,1},{64,2},{65,3},{128,4},{129,5},{192,6},{193,7},{2,8},{3... | collective-permute-start | bytes 786440 | tf_op jit(solution)/shard_map/ppermute | solution.py:485
  266.9 7.1 %collective-permute-start.13 = (f32[8,128]{1,0:T(8,128)S(1)}, f32[8,128]{1,0:T(8,128)S(1)}, u32[]{:S(2)}, u32[]{:S(2)}) collective-permute-start(f32[8,128]{1,0:T(8,128)S(1)} %add_add_fusion), channel_id=1, source_target_pairs={{0,0},{1,1},{64,2},{65,3},{128,4},{129,5},{192,6},{193,7},{2,8},{3... | collective-permute-start | bytes 12296 | tf_op jit(solution)/shard_map/ppermute | solution.py:488
  274.0 6.6 %collective-permute-done.13 = f32[8,128]{1,0:T(8,128)S(1)} collective-permute-done((f32[8,128]{1,0:T(8,128)S(1)}, f32[8,128]{1,0:T(8,128)S(1)}, u32[]{:S(2)}, u32[]{:S(2)}) %collective-permute-start.13) | collective-permute-done | bytes 4128 | tf_op jit(solution)/shard_map/ppermute | solution.py:488
  283.9 8.3 %all-to-all-start.5 = ((bf16[16,2,1152]{2,1,0:T(2,128)(2,1)}), bf16[16,2,1152]{2,1,0:T(2,128)(2,1)S(1)}, u32[]{:S(2)}, u32[]{:S(2)}) async-start(bf16[16,2,1152]{2,1,0:T(2,128)(2,1)} %all_to_all.35), calls=%async_computation.5 | async-start | bytes 147456 | tf_op jit(solution)/shard_map/all_to_all | solution.py:497
  292.2 8.5 %all-to-all-done.5 = bf16[16,2,1152]{2,1,0:T(2,128)(2,1)S(1)} async-done(((bf16[16,2,1152]{2,1,0:T(2,128)(2,1)}), bf16[16,2,1152]{2,1,0:T(2,128)(2,1)S(1)}, u32[]{:S(2)}, u32[]{:S(2)}) %all-to-all-start.5) | async-done | bytes 73760 | tf_op jit(solution)/shard_map/all_to_all | solution.py:497
  (85 shorter events, 16.3 us)
Async XLA Ops:
  7.2 3.8 %copy-start = (bf16[1280,1024]{1,0:T(8,128)(2,1)S(1)}, bf16[1280,1024]{1,0:T(8,128)(2,1)}, u32[]{:S(2)}) copy-start(bf16[1280,1024]{1,0:T(8,128)(2,1)} %param.15) | copy-start | bytes 7864324
  7.2 3.8 %copy-start.2 = (bf16[1,32,1280]{2,1,0:T(8,128)(2,1)S(1)}, bf16[1,32,1280]{2,1,0:T(8,128)(2,1)}, u32[]{:S(2)}) copy-start(bf16[1,32,1280]{2,1,0:T(8,128)(2,1)} %param.14) | copy-start | bytes 245764
  7.2 3.8 %copy-start.8 = (s32[1,32]{1,0:T(1,128)S(1)}, s32[1,32]{1,0:T(1,128)}, u32[]{:S(2)}) copy-start(s32[1,32]{1,0:T(1,128)} %param.16) | copy-start | bytes 388
  7.2 97.2 %all-gather.2.cloned.1.call-start = ((), (), s32[]{:S(2)}) async-start(), calls=%async_computation.6 | async-start | bytes 6488064 | tf_op jit(solution)/shard_map/all_gather | solution.py:444
  8.8 20.6 %copy-start.1 = (bf16[1,128,1024]{2,1,0:T(8,128)(2,1)S(1)}, bf16[1,128,1024]{2,1,0:T(8,128)(2,1)}, u32[]{:S(2)}) copy-start(bf16[1,128,1024]{2,1,0:T(8,128)(2,1)} %param.13) | copy-start | bytes 786436
  11.0 25.1 %copy-start.9 = (s32[1,128]{1,0:T(1,128)S(1)}, s32[1,128]{1,0:T(1,128)}, u32[]{:S(2)}) copy-start(s32[1,128]{1,0:T(1,128)} %param.17) | copy-start | bytes 1540
  30.3 27.5 %collective-permute-start = (bf16[128,1024]{1,0:T(8,128)(2,1)S(1)}, bf16[128,1024]{1,0:T(8,128)(2,1)S(1)}, u32[]{:S(2)}, u32[]{:S(2)}) collective-permute-start(bf16[128,1024]{1,0:T(8,128)(2,1)S(1)} %scatter_custom_fusion), channel_id=1, source_target_pairs={{0,0},{1,1},{2,64},{3,65},{4,128},{5,129},{6,192},{7,193},{8,2},{9... | collective-permute-start | bytes 786440 | tf_op jit(solution)/shard_map/ppermute | solution.py:456
  36.7 11.0 %collective-permute-start.1 = (s32[1]{0:T(128)}, s32[1]{0:T(128)}, u32[]{:S(2)}, u32[]{:S(2)}) collective-permute-start(s32[1]{0:T(128)} %bitcast.9), channel_id=1, source_target_pairs={{0,8},{8,16},{16,24},{24,32},{32,40},{40,48},{48,56},{56,64},{64,7... | collective-permute-start | bytes 20 | tf_op jit(solution)/shard_map/ppermute | solution.py:451
  76.7 27.7 %collective-permute-start.2 = (bf16[4,128,1024]{2,1,0:T(8,128)(2,1)}, bf16[4,128,1024]{2,1,0:T(8,128)(2,1)}, u32[]{:S(2)}, u32[]{:S(2)}) collective-permute-start(bf16[4,128,1024]{2,1,0:T(8,128)(2,1)} %all_to_all.44.own), channel_id=1, source_target_pairs={{0,1},{1,0},{2,3},{3,2},{4,5},{5,4},{6,7},{7,6},{8,9},{9,8},{10,11... | collective-permute-start | bytes 3145736 | tf_op jit(solution)/shard_map/ppermute | solution.py:460
  76.7 27.7 %collective-permute-start.3 = (bf16[144,1024]{1,0:T(8,128)(2,1)S(1)}, bf16[144,1024]{1,0:T(8,128)(2,1)}, u32[]{:S(2)}, u32[]{:S(2)}) collective-permute-start(bf16[144,1024]{1,0:T(8,128)(2,1)S(1)} %pad_maximum_fusion), channel_id=1, source_target_pairs={{0,0},{8,64},{16,128},{24,192},{32,32},{40,96},{48,160},{56,224},{... | collective-permute-start | bytes 884744 | tf_op jit(solution)/shard_map/ppermute | solution.py:458
  116.3 18.2 %copy-start.6 = (f32[16]{0:T(128)S(1)}, f32[16]{0:T(128)}, u32[]{:S(2)}) copy-start(f32[16]{0:T(128)} %param.23) | copy-start | bytes 196
  116.3 18.2 %copy-start.7 = (f32[16]{0:T(128)S(1)}, f32[16]{0:T(128)}, u32[]{:S(2)}) copy-start(f32[16]{0:T(128)} %param.22) | copy-start | bytes 196
  116.3 45.3 %all-to-all-start.2 = ((bf16[4,592,512]{2,1,0:T(8,128)(2,1)}), bf16[4,592,512]{2,1,0:T(8,128)(2,1)}, u32[]{:S(2)}, u32[]{:S(2)}) async-start(bf16[4,592,512]{2,1,0:T(8,128)(2,1)} %shard_map.141), calls=%async_computation.2 | async-start | bytes 4849664 | tf_op jit(solution)/shard_map/all_to_all | solution.py:471
  134.5 40.5 %copy-start.10 = (f32[16]{0:T(128)S(1)}, f32[16]{0:T(128)}, u32[]{:S(2)}) copy-start(f32[16]{0:T(128)} %param.24) | copy-start | bytes 196
  169.4 10.9 %collective-permute-start.4 = (bf16[272,128]{1,0:T(8,128)(2,1)S(1)}, bf16[272,128]{1,0:T(8,128)(2,1)S(1)}, u32[]{:S(2)}, u32[]{:S(2)}) collective-permute-start(bf16[272,128]{1,0:T(8,128)(2,1)S(1)} %get-tuple-element.38), channel_id=1, source_target_pairs={{0,32},{8,40},{16,48},{24,56},{32,16},{40,24},{48,0},{56,8},{1,33}... | collective-permute-start | bytes 208904 | tf_op jit(solution)/shard_map/ppermute | solution.py:473
  174.3 6.0 %collective-permute-start.5 = (bf16[272,128]{1,0:T(8,128)(2,1)S(1)}, bf16[272,128]{1,0:T(8,128)(2,1)S(1)}, u32[]{:S(2)}, u32[]{:S(2)}) collective-permute-start(bf16[272,128]{1,0:T(8,128)(2,1)S(1)} %get-tuple-element.37), channel_id=1, source_target_pairs={{0,16},{8,24},{16,0},{24,8},{32,48},{40,56},{48,32},{56,40},{1,17}... | collective-permute-start | bytes 208904 | tf_op jit(solution)/shard_map/ppermute | solution.py:473
  174.3 8.2 %collective-permute-start.6 = (bf16[272,128]{1,0:T(8,128)(2,1)S(1)}, bf16[272,128]{1,0:T(8,128)(2,1)S(1)}, u32[]{:S(2)}, u32[]{:S(2)}) collective-permute-start(bf16[272,128]{1,0:T(8,128)(2,1)S(1)} %get-tuple-element.36), channel_id=1, source_target_pairs={{0,48},{8,56},{16,32},{24,40},{32,0},{40,8},{48,16},{56,24},{1,49}... | collective-permute-start | bytes 208904 | tf_op jit(solution)/shard_map/ppermute | solution.py:473
  180.3 2.2 copy-start.3
  180.3 2.2 copy-start.4
  182.5 0.6 copy-start.5
  226.3 6.2 %collective-permute-start.7 = (bf16[4,128,1024]{2,1,0:T(8,128)(2,1)}, bf16[4,128,1024]{2,1,0:T(8,128)(2,1)}, u32[]{:S(2)}, u32[]{:S(2)}) collective-permute-start(bf16[4,128,1024]{2,1,0:T(8,128)(2,1)} %get-tuple-element.31), channel_id=1, source_target_pairs={{0,1},{1,0},{2,3},{3,2},{4,5},{5,4},{6,7},{7,6},{8,9},{9,8},{10,11... | collective-permute-start | bytes 3145736 | tf_op jit(solution)/shard_map/ppermute | solution.py:478
  234.4 28.6 %copy-start.11 = (s32[1,128]{1,0:T(1,128)S(1)}, s32[1,128]{1,0:T(1,128)}, u32[]{:S(2)}) copy-start(s32[1,128]{1,0:T(1,128)} %param.18) | copy-start | bytes 1540
  255.9 1.3 collective-permute-start.9
  257.8 8.4 %collective-permute-start.10 = (f32[8,128]{1,0:T(8,128)S(1)}, f32[8,128]{1,0:T(8,128)S(1)}, u32[]{:S(2)}, u32[]{:S(2)}) collective-permute-start(f32[8,128]{1,0:T(8,128)S(1)} %broadcast_add_fusion), channel_id=1, source_target_pairs={{0,64},{64,128},{128,192},{192,0},{1,65},{65,129},{129,193},{193,1... | collective-permute-start | bytes 12296 | tf_op jit(solution)/shard_map/ppermute | solution.py:426
  259.5 6.7 %collective-permute-start.11 = (f32[8,128]{1,0:T(8,128)S(1)}, f32[8,128]{1,0:T(8,128)S(1)}, u32[]{:S(2)}, u32[]{:S(2)}) collective-permute-start(f32[8,128]{1,0:T(8,128)S(1)} %broadcast_add_fusion), channel_id=1, source_target_pairs={{0,128},{64,192},{128,0},{192,64},{1,129},{65,193},{129,1},{193,65... | collective-permute-start | bytes 12296 | tf_op jit(solution)/shard_map/ppermute | solution.py:426
  261.0 5.3 %collective-permute-start.12 = (f32[8,128]{1,0:T(8,128)S(1)}, f32[8,128]{1,0:T(8,128)S(1)}, u32[]{:S(2)}, u32[]{:S(2)}) collective-permute-start(f32[8,128]{1,0:T(8,128)S(1)} %broadcast_add_fusion), channel_id=1, source_target_pairs={{0,192},{64,0},{128,64},{192,128},{1,193},{65,1},{129,65},{193,129... | collective-permute-start | bytes 12296 | tf_op jit(solution)/shard_map/ppermute | solution.py:426
  263.0 19.5 %collective-permute-start.8 = (bf16[128,1024]{1,0:T(8,128)(2,1)S(1)}, bf16[128,1024]{1,0:T(8,128)(2,1)S(1)}, u32[]{:S(2)}, u32[]{:S(2)}) collective-permute-start(bf16[128,1024]{1,0:T(8,128)(2,1)S(1)} %get-tuple-element.35), channel_id=1, source_target_pairs={{0,0},{1,1},{64,2},{65,3},{128,4},{129,5},{192,6},{193,7},{2,8},{3... | collective-permute-start | bytes 786440 | tf_op jit(solution)/shard_map/ppermute | solution.py:485
  266.9 13.8 %collective-permute-start.13 = (f32[8,128]{1,0:T(8,128)S(1)}, f32[8,128]{1,0:T(8,128)S(1)}, u32[]{:S(2)}, u32[]{:S(2)}) collective-permute-start(f32[8,128]{1,0:T(8,128)S(1)} %add_add_fusion), channel_id=1, source_target_pairs={{0,0},{1,1},{64,2},{65,3},{128,4},{129,5},{192,6},{193,7},{2,8},{3... | collective-permute-start | bytes 12296 | tf_op jit(solution)/shard_map/ppermute | solution.py:488
  283.9 16.8 %all-to-all-start.5 = ((bf16[16,2,1152]{2,1,0:T(2,128)(2,1)}), bf16[16,2,1152]{2,1,0:T(2,128)(2,1)S(1)}, u32[]{:S(2)}, u32[]{:S(2)}) async-start(bf16[16,2,1152]{2,1,0:T(2,128)(2,1)} %all_to_all.35), calls=%async_computation.5 | async-start | bytes 147456 | tf_op jit(solution)/shard_map/all_to_all | solution.py:497
Sparse Core Ops, SparseCore 0:
  11.1 93.0 all-gather.1

commit v2 on v1

--- a/solution.py
+++ b/solution.py
@@ -14,6 +14,7 @@
 CHUNK = 128
 WIDE = 1408
 PLACE = (0, 2, 1, 3)
+GATHERED = 768
 HIGH = lax.Precision.HIGHEST
 VMEM = pl.BlockSpec(memory_space=pltpu.VMEM)
 SMEM = pl.BlockSpec(memory_space=pltpu.SMEM)
@@ -99,15 +100,15 @@
 
 
 def pack_kernel(w_x, w_bc, w_dt, out):
-    out[:, 0:1024] = w_x[...]
-    out[:, 1024:1280] = w_bc[...]
-    out[:, 1280:1408] = jnp.zeros((256, 128), BF16)
-    out[:, 1280:1296] = w_dt[...]
+    out[:, 0:256] = w_x[:, GATHERED:1024]
+    out[:, 256:512] = w_bc[...]
+    out[:, 512:640] = jnp.zeros((256, 128), BF16)
+    out[:, 512:528] = w_dt[...]
 
 
 def pack(*parts):
     return pl.pallas_call(
-        pack_kernel, in_specs=[VMEM] * 3, out_specs=VMEM, out_shape=jax.ShapeDtypeStruct((256, WIDE), BF16)
+        pack_kernel, in_specs=[VMEM] * 3, out_specs=VMEM, out_shape=jax.ShapeDtypeStruct((256, WIDE - GATHERED), BF16)
     )(*parts)
 
 
@@ -115,13 +116,28 @@
 ANY = pl.BlockSpec(memory_space=pl.ANY)
 
 
-def project_kernel(meta, own, oth, w, probe, out, buf, rows, sems):
+def ring_rows(meta, i):
+    place = lax.rem(meta[3] + (0, 7, 1, 6, 2, 5, 3, 4)[i], 8)
+    row = lax.rem(place // 4 + meta[0], 2) * 1024 + lax.rem(place, 4) * 256
+    return pl.multiple_of(row, 256)
+
+
+def project_kernel(meta, own, oth, probe, w, *rest):
+    blocks, (out, kept), (buf, rows, sems, out_sems) = rest[:9], rest[9:11], rest[11:]
     copies = []
-    for t, (lo, hi) in enumerate(TILES):
+    for t, (lo, hi) in enumerate(TILES[:3]):
         for n in range(2):
             here = pl.ds(pl.multiple_of(lax.rem(meta[0] + n, 2) * 1024, 1024), 1024)
             there = buf.at[1024 * n : 1024 * n + 1024, lo:hi]
             copies.append(pltpu.make_async_copy(w.at[here, lo:hi], there, sems.at[2 * t + n]))
+    for i in range(7):
+        there = buf.at[pl.ds(ring_rows(meta, i), 256), GATHERED:WIDE]
+        copies.append(pltpu.make_async_copy(blocks[i], there, sems.at[6 + i]))
+    for n in range(2):
+        there = buf.at[pl.ds(pl.multiple_of(ring_rows(meta, 7) + 128 * n, 128), 128), GATHERED:WIDE]
+        copies.append(pltpu.make_async_copy(blocks[7 + n], there, sems.at[13 + n]))
+    stores = [pltpu.make_async_copy(buf.at[:, lo:hi], kept.at[:, lo:hi], out_sems.at[t]) for t, (lo, hi) in enumerate(TILES[:3])]
+    stores.append(pltpu.make_async_copy(buf.at[:, GATHERED:WIDE], kept.at[:, GATHERED:WIDE], out_sems.at[3]))
     for copy in copies:
         copy.start()
     for n, ref in enumerate((own, oth)):
@@ -133,8 +149,10 @@
         out[d, 528:592, 0:256] = probe[0:64, part]
         out[d, 528:592, 256:512] = probe[64:128, part]
     for t, (lo, hi) in enumerate(TILES):
-        copies[2 * t].wait()
-        copies[2 * t + 1].wait()
+        if t <= 3:
+            for copy in copies[2 * t : 2 * t + 2] if t < 3 else copies[6:]:
+                copy.wait()
+            stores[t].start()
         total = dot_nn(rows[...], buf[:, lo:hi])
         if t < 4:
             out[t, 0:512, 0:256] = total.astype(BF16)
@@ -146,20 +164,23 @@
             for d in range(4):
                 mine = jnp.concatenate([steps[4 * d : 4 * d + 4], jnp.zeros((4, 512), F32), ids], axis=0)
                 out[d, 512:528, :] = mine.astype(BF16)
-
-
-def project(meta, own, oth, w, probe):
+    for store in stores:
+        store.wait()
+
+
+def project(meta, own, oth, probe, w, blocks):
     return pl.pallas_call(
         project_kernel,
-        in_specs=[SMEM, VMEM, VMEM, ANY, VMEM],
-        out_specs=VMEM,
-        out_shape=jax.ShapeDtypeStruct((4, 592, 512), BF16),
+        in_specs=[SMEM, VMEM, VMEM, VMEM] + [ANY] * 10,
+        out_specs=[VMEM, ANY],
+        out_shape=[jax.ShapeDtypeStruct((4, 592, 512), BF16), jax.ShapeDtypeStruct((2048, WIDE), BF16)],
         scratch_shapes=[
             pltpu.VMEM((2048, WIDE), BF16),
             pltpu.VMEM((512, 2048), BF16),
-            pltpu.SemaphoreType.DMA((12,)),
+            pltpu.SemaphoreType.DMA((15,)),
+            pltpu.SemaphoreType.DMA((4,)),
         ],
-    )(meta, own, oth, w, probe)
+    )(meta, own, oth, probe, w, *blocks)
 
 
 def prepare_kernel(meta, r, prm, pay, x, bc, rows_out, cols_out, t_out, q_out, p):
@@ -227,51 +248,53 @@
 def intra_kernel(x, bc, p, rows_in, cols_in, skip, dx, dbc, e):
     seen = iota((128, 128), 0) >= iota((128, 128), 1)
     lane = iota((128, 128), 1)
-    for k in range(4):
-        here = slice(128 * k, 128 * k + 128)
-        b, c = bc[here, 0:128], bc[here, 128:256]
-        rows, cols = rows_in[k], cols_in[k]
-        scores = dot_nt(c, b)
-        visible = (cols[:, 12:13] == rows[12:13, :]) & seen
-        d_scores = jnp.zeros((128, 128), F32)
-        by_row = jnp.zeros((128, 128), F32)
-        sums = []
-        for tile in range(2):
-            part = slice(128 * tile, 128 * tile + 128)
-            probe = p[k, 0:128, part].astype(F32)
-            values = x[here, part].astype(BF16)
-            d_values = skip[:, part] * probe
-            for a in range(2):
-                h = 2 * tile + a
-                mine = jnp.where((lane < 64) if a == 0 else (lane >= 64), probe, 0.0).astype(BF16)
-                pulled = dot_nt(mine, values)
-                decay = jnp.exp(jnp.where(visible, cols[:, h : h + 1] - rows[h : h + 1, :], -1e30))
-                steps = rows[4 + h : 5 + h, :]
-                weighted = decay * pulled
-                decayed = decay * scores
-                plain = weighted * scores
-                sums.append(jnp.sum(plain, axis=0, keepdims=True))
-                by_row = jnp.where(lane == h, jnp.sum(plain * steps, axis=1, keepdims=True), by_row)
-                d_scores += weighted * steps
-                d_values += dot_tn((decayed * steps).astype(BF16), mine)
-            dx[here, part] = d_values
-        d_scores = d_scores.astype(BF16)
-        dbc[here, 0:128] = dot_tn(d_scores, c)
-        dbc[here, 128:256] = dot_nn(d_scores, b)
-        sub = iota((8, 128), 0)
-        down = jnp.zeros((8, 128), F32)
-        for h in range(4):
-            down = jnp.where(sub == h, jnp.broadcast_to(sums[h], (8, 128)), down)
-        dt = pltpu.roll(rows[0:8], 4, 0)
-        e[k, 0:8, :] = down
-        e[k, 8:16, :] = by_row.T[0:8] - dt * down
+    k, here = 0, slice(0, 128)
+    b, c = bc[here, 0:128], bc[here, 128:256]
+    rows, cols = rows_in[k], cols_in[k]
+    scores = dot_nt(c, b)
+    visible = (cols[:, 12:13] == rows[12:13, :]) & seen
+    d_scores = jnp.zeros((128, 128), F32)
+    by_row = jnp.zeros((128, 128), F32)
+    sums = []
+    for tile in range(2):
+        part = slice(128 * tile, 128 * tile + 128)
+        probe = p[k, 0:128, part].astype(F32)
+        values = x[here, part].astype(BF16)
+        d_values = skip[:, part] * probe
+        for a in range(2):
+            h = 2 * tile + a
+            mine = jnp.where((lane < 64) if a == 0 else (lane >= 64), probe, 0.0).astype(BF16)
+            pulled = dot_nt(mine, values)
+            decay = jnp.exp(jnp.where(visible, cols[:, h : h + 1] - rows[h : h + 1, :], -1e30))
+            steps = rows[4 + h : 5 + h, :]
+            weighted = decay * pulled
+            decayed = decay * scores
+            plain = weighted * scores
+            sums.append(jnp.sum(plain, axis=0, keepdims=True))
+            by_row = jnp.where(lane == h, jnp.sum(plain * steps, axis=1, keepdims=True), by_row)
+            d_scores += weighted * steps
+            d_values += dot_tn((decayed * steps).astype(BF16), mine)
+        dx[here, part] = d_values
+    d_scores = d_scores.astype(BF16)
+    dbc[here, 0:128] = dot_tn(d_scores, c)
+    dbc[here, 128:256] = dot_nn(d_scores, b)
+    sub = iota((8, 128), 0)
+    down = jnp.zeros((8, 128), F32)
+    for h in range(4):
+        down = jnp.where(sub == h, jnp.broadcast_to(sums[h], (8, 128)), down)
+    dt = pltpu.roll(rows[0:8], 4, 0)
+    e[k, 0:8, :] = down
+    e[k, 8:16, :] = by_row.T[0:8] - dt * down
 
 
 def intra(x, bc, p, rows, cols, skip):
+    tall = pl.BlockSpec((128, 256), lambda i: (i, 0))
+    flat = lambda *shape: pl.BlockSpec((1,) + shape, lambda i: (i, 0, 0))
     return pl.pallas_call(
         intra_kernel,
-        in_specs=[VMEM] * 6,
-        out_specs=[VMEM] * 3,
+        grid=(4,),
+        in_specs=[tall, tall, flat(128, 256), flat(16, 128), flat(128, 128), pl.BlockSpec((1, 256), lambda i: (0, 0))],
+        out_specs=[tall, tall, flat(16, 128)],
         out_shape=[
             jax.ShapeDtypeStruct((512, 256), F32),
             jax.ShapeDtypeStruct((512, 256), F32),
@@ -357,11 +380,10 @@
 
 
 def pull_half(flip, meta, w, full, out, buf, sems):
-    half = lax.rem(meta[0] + flip, 2) * 1024
     copies = []
     for j in range(4):
-        here = pl.ds(pl.multiple_of(half + 256 * j, 256), 256)
-        copies.append(pltpu.make_async_copy(w.at[here], buf.at[j], sems.at[j]))
+        row = 1024 * flip + 256 * j
+        copies.append(pltpu.make_async_copy(w.at[row : row + 256], buf.at[j], sems.at[j]))
     for copy in copies:
         copy.start()
     yield
@@ -439,24 +461,35 @@
     origin = 2 * lax.rem(across, 2) + across // 2
     quarter = 2 * lax.rem(origin, 2) + z_at // 4
     meta = jnp.stack([core_at, origin, quarter, z_at]).astype(jnp.int32)
-    w_all = pack(w_x, w_bc, w_dt)
-
-    weights = lax.all_gather(w_all, "z", axis=0, tiled=True)
-
+    gathered = lax.all_gather(w_x[:, :GATHERED], "z", axis=0, tiled=True)
+    segment = segments[0]
+    before = lax.ppermute(segment[-1:], X + ("z",), [(i, i + 1) for i in range(31)])
+    ids = jnp.concatenate([segment[None], jnp.broadcast_to(before[None], (15, CHUNK))]).astype(BF16)
+    probe_ids = jnp.concatenate([probe[0], jnp.tile(ids, (1, 8))], axis=0)
+
+    def right(v):
+        return lax.ppermute(v, "z", [(i, (i + 1) % 8) for i in range(8)])
+
+    def left(v):
+        return lax.ppermute(v, "z", [(i, (i + 7) % 8) for i in range(8)])
+
+    w_ring = pack(w_x, w_bc, w_dt)
+    r1, l1 = right(w_ring), left(w_ring)
     frame_emb = jnp.dot(frame_feats[0], w_proj, preferred_element_type=F32).astype(BF16)
     slot = frame_pos[0] - CHUNK * (jnp.arange(32, dtype=jnp.int32) // 2)
     tagged = jnp.concatenate([frame_emb, jnp.broadcast_to(slot.astype(BF16)[:, None], (32, 128))], axis=1)
     arrived = lax.all_to_all(tagged, SEQ, split_axis=0, concat_axis=0, tiled=True)
-    segment = segments[0]
-    before = lax.ppermute(segment[-1:], X + ("z",), [(i, i + 1) for i in range(31)])
-    ids = jnp.concatenate([segment[None], jnp.broadcast_to(before[None], (15, CHUNK))]).astype(BF16)
-    probe_ids = jnp.concatenate([probe[0], jnp.tile(ids, (1, 8))], axis=0)
     local_pos = arrived[:, 1024].astype(jnp.int32)
     merged = tokens[0].at[local_pos].set(arrived[:, :1024])
+    merged, r1, l1 = lax.optimization_barrier((merged, r1, l1))
     moved = lax.ppermute(merged, AXES, features_route())
-    moved, probe_ids = lax.optimization_barrier((moved, probe_ids))
+    r2, l2 = right(r1), left(l1)
+    moved, r2, l2, probe_ids = lax.optimization_barrier((moved, r2, l2, probe_ids))
+    r3, l3 = right(r2), left(l2)
+    own = to_all(moved, "y")
+    own, r3, l3, probe_ids = lax.optimization_barrier((own, r3, l3, probe_ids))
+    r4, l4 = right(r3[:128]), left(l3[128:])
     probe_ids = lax.ppermute(probe_ids, X + ("z",), probe_route())
-    own = to_all(moved, "y")
     oth = lax.ppermute(own, "core", SWAP)
 
     def four(v):
@@ -467,7 +500,8 @@
     prm = jnp.broadcast_to(prm[:, :, None], (2, 8, 128))
     skip = jnp.repeat(four(skip_gain), 64)[None, :]
 
-    partial_proj = project(meta, own, oth, weights, probe_ids)
+    blocks = (w_ring, r1, l1, r2, l2, r3, l3, r4, l4)
+    partial_proj, weights = project(meta, own, oth, probe_ids, gathered, blocks)
     received = lax.all_to_all(partial_proj, X, split_axis=0, concat_axis=0)
     pay, values, bc, rows, cols, t_all, q_all, probes = prepare(meta, received, prm)
     got = [lax.ppermute(pay[k - 1], "z", quarter_route(k)) for k in (1, 2, 3)]

time: 312 us -> 312 us (level)
  blocking collectives: 84.7 us -> 64.2 us
  starting transfers between devices: 57.8 us -> 76.7 us
  local copies, waits for them, and re-layouts: 10.2 us -> 15.4 us
    all_to_all x2 -> x1, blocking collectives: 47.4 us -> 29.7 us  [to_all(): lax.all_to_all(jnp.broadcast_to(x[None], (4,) + x.shape), axis, split_axi...]
    ppermute x1, waiting for transfers between devices: 25.1 us -> 8.91 us  [body(): probe_ids = lax.ppermute(probe_ids, X + ('z',), probe_route())]
    ppermute x0 -> x8, starting transfers between devices: none -> 15.7 us  [the longest x4 12.6 us: left(): return lax.ppermute(v, 'z', [(i, (i + 7) % 8) for i in range(8)])]
    all_to_all x0 -> x1, starting transfers between devices: none -> 15.6 us  [to_all(): lax.all_to_all(jnp.broadcast_to(x[None], (4,) + x.shape), axis, split_axi...]
    ppermute x0 -> x8, waiting for transfers between devices: none -> 10.6 us  [the longest x4 10.6 us: right(): return lax.ppermute(v, 'z', [(i, (i + 1) % 8) for i in range(8)])]
    ppermute x1, waiting for transfers between devices: 8.61 us -> 0.01 us  [body(): moved = lax.ppermute(merged, AXES, features_route())]
    all_to_all x1, starting transfers between devices: 18.2 us -> 10.9 us  [body(): received = lax.all_to_all(partial_proj, X, split_axis=0, concat_axis=0)]
    ppermute x1, waiting for transfers between devices: 8.57 us -> 15.6 us  [body(): lax.ppermute(segment[-1:], X + ('z',), [(i, i + 1) for i in range(31)])]
  transfers between devices with their start and end apart: 17 -> 26, of which waited for: 8 -> 10; matrix products, arithmetic and copies ran while one was open for 2% -> 3% of each run, Pallas kernels for 3% -> 4%
where the time goes in v2:
time: 312 us; the launch traced here: 311 us
  waiting for transfers between devices  84.8 us (27%)
  starting transfers between devices  76.7 us (25%)
  blocking collectives  64.2 us (21%)
  Pallas kernels  42.6 us (14%)
  between operations  17.7 us (6%)
  local copies, waits for them, and re-layouts  15.4 us (5%)
  other arithmetic  8.94 us (3%)
    all_to_all x1, blocking collectives, to_all(): lax.all_to_all(jnp.broadcast_to(x[None], (4,) + x.shape), axis, split_axi...  29.7 us
    all_to_all x1, waiting for transfers between devices, body(): received = lax.all_to_all(partial_proj, X, split_axis=0, concat_axis=0)  27 us
    all_to_all x1, blocking collectives, body(): pieces = lax.all_to_all(both, 'y', split_axis=0, concat_axis=0)  19.2 us
    ppermute x1, waiting for transfers between devices, body(): lax.ppermute(segment[-1:], X + ('z',), [(i, i + 1) for i in range(31)])  15.6 us
    all_to_all x1, starting transfers between devices, to_all(): lax.all_to_all(jnp.broadcast_to(x[None], (4,) + x.shape), axis, split_axi...  15.6 us
    all_to_all x1, blocking collectives, body(): lax.all_to_all(tagged, SEQ, split_axis=0, concat_axis=0, tiled=True)  15.2 us
    ppermute x4, starting transfers between devices, left(): return lax.ppermute(v, 'z', [(i, (i + 7) % 8) for i in range(8)])  12.6 us
    all_to_all x1, starting transfers between devices, body(): received = lax.all_to_all(partial_proj, X, split_axis=0, concat_axis=0)  10.9 us
  transfers between devices with their start and end apart: 26, of which 10 were waited for; matrix products, arithmetic and copies ran while one was open for 3% of the time, Pallas kernels for 4%

profile of v2, /device:TPU:4, one launch (start us, length us, event | category | flops | bytes accessed | tf_op | source)
XLA Modules:
  0.0 310.9 jit_solution(5980461077539037621)
XLA Ops:
  14.5 3.9 %collective-permute-start.1 = (bf16[256,640]{1,0:T(8,128)(2,1)}, bf16[256,640]{1,0:T(8,128)(2,1)}, u32[]{:S(2)}, u32[]{:S(2)}) collective-permute-start(bf16[256,640]{1,0:T(8,128)(2,1)} %shard_map.140.rest_0_), channel_id=1, source_target_pairs={{0,56},{8,0},{16,8},{24,16},{32,24},{40,32},{48,40},{56,48},{1,57}... | collective-permute-start | bytes 983048 | tf_op jit(solution)/shard_map/ppermute | solution.py:474
  19.2 15.2 %all_to_all.46 = bf16[16,2,1152]{2,1,0:T(2,128)(2,1)S(1)} all-to-all(bf16[16,2,1152]{2,1,0:T(2,128)(2,1)S(1)} %all_to_all.28), channel_id=1, replica_groups=mesh['x_hi'=2,'x_lo'=2,'z'=8,'y'=4,'core'=2] {'x_lo','z'}, dimensions={0} | all-to-all | bytes 147456 | tf_op jit(solution)/shard_map/all_to_all | solution.py:481
  36.6 2.2 collective-permute-start.4
  38.8 4.6 %collective-permute-start.2 = (bf16[128,1024]{1,0:T(8,128)(2,1)S(1)}, bf16[128,1024]{1,0:T(8,128)(2,1)S(1)}, u32[]{:S(2)}, u32[]{:S(2)}) collective-permute-start(bf16[128,1024]{1,0:T(8,128)(2,1)S(1)} %scatter_custom_fusion), channel_id=1, source_target_pairs={{0,0},{1,1},{2,64},{3,65},{4,128},{5,129},{6,192},{7,193},{8,2},{9... | collective-permute-start | bytes 786440 | tf_op jit(solution)/shard_map/ppermute | solution.py:485
  44.0 2.3 collective-permute-start.5
  46.3 15.6 %collective-permute-done.5 = s32[1]{0:T(128)} collective-permute-done((s32[1]{0:T(128)}, s32[1]{0:T(128)}, u32[]{:S(2)}, u32[]{:S(2)}) %collective-permute-start.5) | collective-permute-done | bytes 36 | tf_op jit(solution)/shard_map/ppermute | solution.py:466
  66.1 15.6 %all-to-all-start.1 = ((bf16[4,128,1024]{2,1,0:T(8,128)(2,1)}), bf16[4,128,1024]{2,1,0:T(8,128)(2,1)}, u32[]{:S(2)}, u32[]{:S(2)}) async-start(bf16[4,128,1024]{2,1,0:T(8,128)(2,1)} %broadcast_in_dim.31), calls=%async_computation.1 | async-start | bytes 2097152 | tf_op jit(solution)/shard_map/all_to_all | solution.py:444
  81.7 3.2 %collective-permute-start.7 = (bf16[256,640]{1,0:T(8,128)(2,1)}, bf16[256,640]{1,0:T(8,128)(2,1)}, u32[]{:S(2)}, u32[]{:S(2)}) collective-permute-start(bf16[256,640]{1,0:T(8,128)(2,1)} %collective-permute-done.4.rest_4_), channel_id=1, source_target_pairs={{0,56},{8,0},{16,8},{24,16},{32,24},{40,32},{48,40},{56,48},{1,57}... | collective-permute-start | bytes 983048 | tf_op jit(solution)/shard_map/ppermute | solution.py:474
  84.9 5.3 %collective-permute-done.6.rest_5_ = bf16[256,640]{1,0:T(8,128)(2,1)S(1)} collective-permute-done((bf16[256,640]{1,0:T(8,128)(2,1)}, bf16[256,640]{1,0:T(8,128)(2,1)S(1)}, u32[]{:S(2)}, u32[]{:S(2)}) %collective-permute-start.6) | collective-permute-done | bytes 327712 | tf_op jit(solution)/shard_map/ppermute | solution.py:471
  90.2 3.5 %all-to-all-done.1.own = bf16[4,128,1024]{2,1,0:T(8,128)(2,1)} async-done(((bf16[4,128,1024]{2,1,0:T(8,128)(2,1)}), bf16[4,128,1024]{2,1,0:T(8,128)(2,1)}, u32[]{:S(2)}, u32[]{:S(2)}) %all-to-all-start.1) | async-done | bytes 1048608 | tf_op jit(solution)/shard_map/all_to_all | solution.py:444
  97.3 3.2 %collective-permute-start.11 = (bf16[128,640]{1,0:T(8,128)(2,1)}, bf16[128,640]{1,0:T(8,128)(2,1)}, u32[]{:S(2)}, u32[]{:S(2)}) collective-permute-start(bf16[128,640]{1,0:T(8,128)(2,1)} %slice.51), channel_id=1, source_target_pairs={{0,56},{8,0},{16,8},{24,16},{32,24},{40,32},{48,40},{56,48},{1,57}... | collective-permute-start | bytes 491528 | tf_op jit(solution)/shard_map/ppermute | solution.py:474
  101.1 5.4 %collective-permute-done.10.rest_7_ = bf16[128,640]{1,0:T(8,128)(2,1)} collective-permute-done((bf16[128,640]{1,0:T(8,128)(2,1)S(1)}, bf16[128,640]{1,0:T(8,128)(2,1)}, u32[]{:S(2)}, u32[]{:S(2)}) %collective-permute-start.10) | collective-permute-done | bytes 163872 | tf_op jit(solution)/shard_map/ppermute | solution.py:471
  106.5 8.9 %collective-permute-done.9.probe = bf16[144,1024]{1,0:T(8,128)(2,1)} collective-permute-done((bf16[144,1024]{1,0:T(8,128)(2,1)}, bf16[144,1024]{1,0:T(8,128)(2,1)}, u32[]{:S(2)}, u32[]{:S(2)}) %collective-permute-start.9) | collective-permute-done | bytes 294944 | tf_op jit(solution)/shard_map/ppermute | solution.py:492
  115.4 10.5 %shard_map.141 = (bf16[4,592,512]{2,1,0:T(8,128)(2,1)}, bf16[2048,1408]{1,0:T(8,128)(2,1)}) custom-call(s32[4]{0:T(128)} %pad_add_fusion.meta, bf16[4,128,1024]{2,1,0:T(8,128)(2,1)} %all-to-all-done.1.own, bf16[4,128,1024]{2,1,0:T(8,128)(2,1)} %collective-permute-done.8.oth, bf16[144,1024]{1,0:T(8,128)(2,1)} %collective-permute-done.9.probe, ...), custom_call_target="tpu_custom_call" | custom-call | tf_op jit(solution)/shard_map/pallas_call | solution.py:172
  125.9 10.9 %all-to-all-start.2 = ((bf16[4,592,512]{2,1,0:T(8,128)(2,1)}), bf16[4,592,512]{2,1,0:T(8,128)(2,1)}, u32[]{:S(2)}, u32[]{:S(2)}) async-start(bf16[4,592,512]{2,1,0:T(8,128)(2,1)} %get-tuple-element.39), calls=%async_computation.2 | async-start | bytes 4849664 | tf_op jit(solution)/shard_map/all_to_all | solution.py:505
  136.9 27.0 %all-to-all-done.2.r = bf16[4,592,512]{2,1,0:T(8,128)(2,1)} async-done(((bf16[4,592,512]{2,1,0:T(8,128)(2,1)}), bf16[4,592,512]{2,1,0:T(8,128)(2,1)}, u32[]{:S(2)}, u32[]{:S(2)}) %all-to-all-start.2) | async-done | bytes 2424864 | tf_op jit(solution)/shard_map/all_to_all | solution.py:505
  164.5 6.1 %shard_map.142 = (bf16[3,272,128]{2,1,0:T(8,128)(2,1)}, f32[512,256]{1,0:T(8,128)}, bf16[512,256]{1,0:T(8,128)(2,1)}, f32[4,16,128]{2,1,0:T(8,128)}, f32[4,128,1...) custom-call(s32[4]{0:T(128)} %pad_add_fusion.meta, ...), custom_call_target="tpu_custom_call" | custom-call | tf_op jit(solution)/shard_map/pallas_call | solution.py:231
  171.6 2.5 collective-permute-start.12
  176.7 4.6 %shard_map.143 = (f32[512,256]{1,0:T(8,128)}, f32[512,256]{1,0:T(8,128)}, f32[4,16,128]{2,1,0:T(8,128)}) custom-call(f32[512,256]{1,0:T(8,128)} %get-tuple-element.41.x, bf16[512,256]{1,0:T(8,128)(2,1)} %get-tuple-element.42.bc, bf16[4,128,256]{2,1,0:T(8,128)(2,1)} %get-tuple-element.43.p, f32[4,16,128]{2,1,0:T(8,128)} %get-tuple-element.44.rows_in, ...), custom_call_target="tpu_custom_call" | custom-call | tf_op jit(solution)/shard_map/pallas_call | solution.py:293
  183.4 7.0 %shard_map.144 = bf16[528,512]{1,0:T(8,128)(2,1)} custom-call(s32[4]{0:T(128)} %pad_add_fusion.meta, bf16[272,128]{1,0:T(8,128)(2,1)} %copy-done.6, bf16[272,128]{1,0:T(8,128)(2,1)} %copy-done.7, bf16[272,128]{1,0:T(8,128)(2,1)} %copy-done.8, f32[512,256]{1,0:T(8,128)} %get-tuple-element.41.x, bf16[512,256]{1,0:T(8,128)(2,1)} %get-tuple-element.42.bc, ...), custom_call_target="tpu_custom_call" | custom-call | tf_op jit(solution)/shard_map/pallas_call | solution.py:374
  191.6 29.7 %all_to_all.44.g = bf16[4,528,512]{2,1,0:T(8,128)(2,1)} all-to-all(bf16[4,528,512]{2,1,0:T(8,128)(2,1)S(1)} %broadcast_in_dim.34), channel_id=1, replica_groups=mesh['x_hi'=2,'x_lo'=2,'z'=8,'y'=4,'core'=2] {'x_hi','x_lo'}, dimensions={0} | all-to-all | bytes 4325376 | tf_op jit(solution)/shard_map/all_to_all | solution.py:444
  221.3 6.4 %shard_map.145 = (bf16[1408,512]{1,0:T(8,128)(2,1)}, bf16[4,128,1024]{2,1,0:T(8,128)(2,1)}) custom-call(s32[4]{0:T(128)} %pad_add_fusion.meta, bf16[4,528,512]{2,1,0:T(8,128)(2,1)} %all_to_all.44.g, bf16[2048,1408]{1,0:T(8,128)(2,1)} %get-tuple-element.51.w), custom_call_target="tpu_custom_call" | custom-call | tf_op jit(solution)/shard_map/pallas_call | solution.py:424
  227.8 6.1 %shard_map.146 = bf16[4,128,1024]{2,1,0:T(8,128)(2,1)} custom-call(s32[4]{0:T(128)} %pad_add_fusion.meta, bf16[1408,512]{1,0:T(8,128)(2,1)} %get-tuple-element.52.full, bf16[2048,1408]{1,0:T(8,128)(2,1)} %get-tuple-element.51.w), custom_call_target="tpu_custom_call" | custom-call | tf_op jit(solution)/shard_map/pallas_call | solution.py:434
  233.9 1.9 add_convert_fusion
  235.9 19.2 %all_to_all.45 = bf16[4,128,1024]{2,1,0:T(8,128)(2,1)S(1)} all-to-all(bf16[4,128,1024]{2,1,0:T(8,128)(2,1)S(1)} %add_convert_fusion), channel_id=1, replica_groups=mesh['x_hi'=2,'x_lo'=2,'z'=8,'y'=4,'core'=2] {'y'}, dimensions={0} | all-to-all | bytes 2097152 | tf_op jit(solution)/shard_map/all_to_all | solution.py:515
  258.6 2.0 collective-permute-start.18
  261.8 2.1 collective-permute-start.20
  263.8 3.1 %collective-permute-start.16 = (bf16[128,1024]{1,0:T(8,128)(2,1)S(1)}, bf16[128,1024]{1,0:T(8,128)(2,1)S(1)}, u32[]{:S(2)}, u32[]{:S(2)}) collective-permute-start(bf16[128,1024]{1,0:T(8,128)(2,1)S(1)} %get-tuple-element.57), channel_id=1, source_target_pairs={{0,0},{1,1},{64,2},{65,3},{128,4},{129,5},{192,6},{193,7},{2,8},{3... | collective-permute-start | bytes 786440 | tf_op jit(solution)/shard_map/ppermute | solution.py:519
  267.7 5.7 %collective-permute-start.21 = (f32[8,128]{1,0:T(8,128)S(1)}, f32[8,128]{1,0:T(8,128)S(1)}, u32[]{:S(2)}, u32[]{:S(2)}) collective-permute-start(f32[8,128]{1,0:T(8,128)S(1)} %add_add_fusion), channel_id=1, source_target_pairs={{0,0},{1,1},{64,2},{65,3},{128,4},{129,5},{192,6},{193,7},{2,8},{3... | collective-permute-start | bytes 12296 | tf_op jit(solution)/shard_map/ppermute | solution.py:522
  273.4 8.0 %collective-permute-done.21 = f32[8,128]{1,0:T(8,128)S(1)} collective-permute-done((f32[8,128]{1,0:T(8,128)S(1)}, f32[8,128]{1,0:T(8,128)S(1)}, u32[]{:S(2)}, u32[]{:S(2)}) %collective-permute-start.21) | collective-permute-done | bytes 4128 | tf_op jit(solution)/shard_map/ppermute | solution.py:522
  284.7 7.2 %all-to-all-start.5 = ((bf16[16,2,1152]{2,1,0:T(2,128)(2,1)}), bf16[16,2,1152]{2,1,0:T(2,128)(2,1)S(1)}, u32[]{:S(2)}, u32[]{:S(2)}) async-start(bf16[16,2,1152]{2,1,0:T(2,128)(2,1)} %all_to_all.35), calls=%async_computation.5 | async-start | bytes 147456 | tf_op jit(solution)/shard_map/all_to_all | solution.py:531
  291.9 8.5 %all-to-all-done.5 = bf16[16,2,1152]{2,1,0:T(2,128)(2,1)S(1)} async-done(((bf16[16,2,1152]{2,1,0:T(2,128)(2,1)}), bf16[16,2,1152]{2,1,0:T(2,128)(2,1)S(1)}, u32[]{:S(2)}, u32[]{:S(2)}) %all-to-all-start.5) | async-done | bytes 73760 | tf_op jit(solution)/shard_map/all_to_all | solution.py:531
  (111 shorter events, 35.7 us)
Async XLA Ops:
  7.2 108.2 %all-gather.2.cloned.1.call-start = ((), (), s32[]{:S(2)}) async-start(), calls=%async_computation.6 | async-start | bytes 3538944 | tf_op jit(solution)/shard_map/all_gather | solution.py:464
  9.2 25.4 %copy-start.1 = (bf16[1,128,1024]{2,1,0:T(8,128)(2,1)S(1)}, bf16[1,128,1024]{2,1,0:T(8,128)(2,1)}, u32[]{:S(2)}) copy-start(bf16[1,128,1024]{2,1,0:T(8,128)(2,1)} %param.13) | copy-start | bytes 786436
  9.2 34.2 %copy-start.12 = (s32[1,128]{1,0:T(1,128)S(1)}, s32[1,128]{1,0:T(1,128)}, u32[]{:S(2)}) copy-start(s32[1,128]{1,0:T(1,128)} %param.17) | copy-start | bytes 1540
  12.6 22.9 %collective-permute-start = (bf16[256,640]{1,0:T(8,128)(2,1)}, bf16[256,640]{1,0:T(8,128)(2,1)S(1)}, u32[]{:S(2)}, u32[]{:S(2)}) collective-permute-start(bf16[256,640]{1,0:T(8,128)(2,1)} %shard_map.140.rest_0_), channel_id=1, source_target_pairs={{0,8},{8,16},{16,24},{24,32},{32,40},{40,48},{48,56},{56,0},{1,9},... | collective-permute-start | bytes 983048 | tf_op jit(solution)/shard_map/ppermute | solution.py:471
  14.5 21.0 %collective-permute-start.1 = (bf16[256,640]{1,0:T(8,128)(2,1)}, bf16[256,640]{1,0:T(8,128)(2,1)}, u32[]{:S(2)}, u32[]{:S(2)}) collective-permute-start(bf16[256,640]{1,0:T(8,128)(2,1)} %shard_map.140.rest_0_), channel_id=1, source_target_pairs={{0,56},{8,0},{16,8},{24,16},{32,24},{40,32},{48,40},{56,48},{1,57}... | collective-permute-start | bytes 983048 | tf_op jit(solution)/shard_map/ppermute | solution.py:474
  35.5 30.6 %copy-start.3 = (bf16[256,640]{1,0:T(8,128)(2,1)}, bf16[256,640]{1,0:T(8,128)(2,1)S(1)}, u32[]{:S(2)}) copy-start(bf16[256,640]{1,0:T(8,128)(2,1)S(1)} %collective-permute-done.rest_1_) | copy-start | bytes 983044
  35.5 28.7 %collective-permute-start.3 = (bf16[256,640]{1,0:T(8,128)(2,1)S(1)}, bf16[256,640]{1,0:T(8,128)(2,1)S(1)}, u32[]{:S(2)}, u32[]{:S(2)}) collective-permute-start(bf16[256,640]{1,0:T(8,128)(2,1)S(1)} %collective-permute-done.rest_1_), channel_id=1, source_target_pairs={{0,8},{8,16},{16,24},{24,32},{32,40},{40,48},{48,56},{56,0},{1,9},... | collective-permute-start | bytes 983048 | tf_op jit(solution)/shard_map/ppermute | solution.py:471
  36.6 28.3 %collective-permute-start.4 = (bf16[256,640]{1,0:T(8,128)(2,1)}, bf16[256,640]{1,0:T(8,128)(2,1)}, u32[]{:S(2)}, u32[]{:S(2)}) collective-permute-start(bf16[256,640]{1,0:T(8,128)(2,1)} %collective-permute-done.1.rest_2_), channel_id=1, source_target_pairs={{0,56},{8,0},{16,8},{24,16},{32,24},{40,32},{48,40},{56,48},{1,57}... | collective-permute-start | bytes 983048 | tf_op jit(solution)/shard_map/ppermute | solution.py:474
  38.8 25.4 %collective-permute-start.2 = (bf16[128,1024]{1,0:T(8,128)(2,1)S(1)}, bf16[128,1024]{1,0:T(8,128)(2,1)S(1)}, u32[]{:S(2)}, u32[]{:S(2)}) collective-permute-start(bf16[128,1024]{1,0:T(8,128)(2,1)S(1)} %scatter_custom_fusion), channel_id=1, source_target_pairs={{0,0},{1,1},{2,64},{3,65},{4,128},{5,129},{6,192},{7,193},{8,2},{9... | collective-permute-start | bytes 786440 | tf_op jit(solution)/shard_map/ppermute | solution.py:485
  44.0 17.9 %collective-permute-start.5 = (s32[1]{0:T(128)}, s32[1]{0:T(128)}, u32[]{:S(2)}, u32[]{:S(2)}) collective-permute-start(s32[1]{0:T(128)} %bitcast.9), channel_id=1, source_target_pairs={{0,8},{8,16},{16,24},{24,32},{32,40},{40,48},{48,56},{56,64},{64,7... | collective-permute-start | bytes 20 | tf_op jit(solution)/shard_map/ppermute | solution.py:466
  66.1 27.6 %all-to-all-start.1 = ((bf16[4,128,1024]{2,1,0:T(8,128)(2,1)}), bf16[4,128,1024]{2,1,0:T(8,128)(2,1)}, u32[]{:S(2)}, u32[]{:S(2)}) async-start(bf16[4,128,1024]{2,1,0:T(8,128)(2,1)} %broadcast_in_dim.31), calls=%async_computation.1 | async-start | bytes 2097152 | tf_op jit(solution)/shard_map/all_to_all | solution.py:444
  81.7 8.5 %collective-permute-start.6 = (bf16[256,640]{1,0:T(8,128)(2,1)}, bf16[256,640]{1,0:T(8,128)(2,1)S(1)}, u32[]{:S(2)}, u32[]{:S(2)}) collective-permute-start(bf16[256,640]{1,0:T(8,128)(2,1)} %copy-done.4), channel_id=1, source_target_pairs={{0,8},{8,16},{16,24},{24,32},{32,40},{40,48},{48,56},{56,0},{1,9},... | collective-permute-start | bytes 983048 | tf_op jit(solution)/shard_map/ppermute | solution.py:471
  81.7 8.5 %collective-permute-start.7 = (bf16[256,640]{1,0:T(8,128)(2,1)}, bf16[256,640]{1,0:T(8,128)(2,1)}, u32[]{:S(2)}, u32[]{:S(2)}) collective-permute-start(bf16[256,640]{1,0:T(8,128)(2,1)} %collective-permute-done.4.rest_4_), channel_id=1, source_target_pairs={{0,56},{8,0},{16,8},{24,16},{32,24},{40,32},{48,40},{56,48},{1,57}... | collective-permute-start | bytes 983048 | tf_op jit(solution)/shard_map/ppermute | solution.py:474
  90.1 25.3 %copy-start.2 = (bf16[256,640]{1,0:T(8,128)(2,1)}, bf16[256,640]{1,0:T(8,128)(2,1)S(1)}, u32[]{:S(2)}) copy-start(bf16[256,640]{1,0:T(8,128)(2,1)S(1)} %collective-permute-done.6.rest_5_) | copy-start | bytes 983044
  93.7 21.8 %collective-permute-start.8 = (bf16[4,128,1024]{2,1,0:T(8,128)(2,1)}, bf16[4,128,1024]{2,1,0:T(8,128)(2,1)}, u32[]{:S(2)}, u32[]{:S(2)}) collective-permute-start(bf16[4,128,1024]{2,1,0:T(8,128)(2,1)} %all-to-all-done.1.own), channel_id=1, source_target_pairs={{0,1},{1,0},{2,3},{3,2},{4,5},{5,4},{6,7},{7,6},{8,9},{9,8},{10,11... | collective-permute-start | bytes 3145736 | tf_op jit(solution)/shard_map/ppermute | solution.py:493
  93.7 21.8 %collective-permute-start.9 = (bf16[144,1024]{1,0:T(8,128)(2,1)}, bf16[144,1024]{1,0:T(8,128)(2,1)}, u32[]{:S(2)}, u32[]{:S(2)}) collective-permute-start(bf16[144,1024]{1,0:T(8,128)(2,1)} %pad_maximum_fusion), channel_id=1, source_target_pairs={{0,0},{8,64},{16,128},{24,192},{32,32},{40,96},{48,160},{56,224},{... | collective-permute-start | bytes 884744 | tf_op jit(solution)/shard_map/ppermute | solution.py:492
  95.6 10.9 %collective-permute-start.10 = (bf16[128,640]{1,0:T(8,128)(2,1)S(1)}, bf16[128,640]{1,0:T(8,128)(2,1)}, u32[]{:S(2)}, u32[]{:S(2)}) collective-permute-start(bf16[128,640]{1,0:T(8,128)(2,1)S(1)} %slice.50), channel_id=1, source_target_pairs={{0,8},{8,16},{16,24},{24,32},{32,40},{40,48},{48,56},{56,0},{1,9},... | collective-permute-start | bytes 491528 | tf_op jit(solution)/shard_map/ppermute | solution.py:471
  97.3 9.2 %collective-permute-start.11 = (bf16[128,640]{1,0:T(8,128)(2,1)}, bf16[128,640]{1,0:T(8,128)(2,1)}, u32[]{:S(2)}, u32[]{:S(2)}) collective-permute-start(bf16[128,640]{1,0:T(8,128)(2,1)} %slice.51), channel_id=1, source_target_pairs={{0,56},{8,0},{16,8},{24,16},{32,24},{40,32},{48,40},{56,48},{1,57}... | collective-permute-start | bytes 491528 | tf_op jit(solution)/shard_map/ppermute | solution.py:474
  125.9 37.9 %all-to-all-start.2 = ((bf16[4,592,512]{2,1,0:T(8,128)(2,1)}), bf16[4,592,512]{2,1,0:T(8,128)(2,1)}, u32[]{:S(2)}, u32[]{:S(2)}) async-start(bf16[4,592,512]{2,1,0:T(8,128)(2,1)} %get-tuple-element.39), calls=%async_computation.2 | async-start | bytes 4849664 | tf_op jit(solution)/shard_map/all_to_all | solution.py:505
  136.8 39.1 %copy-start.13 = (f32[16]{0:T(128)S(1)}, f32[16]{0:T(128)}, u32[]{:S(2)}) copy-start(f32[16]{0:T(128)} %param.24) | copy-start | bytes 196
  171.6 9.7 %collective-permute-start.12 = (bf16[272,128]{1,0:T(8,128)(2,1)S(1)}, bf16[272,128]{1,0:T(8,128)(2,1)S(1)}, u32[]{:S(2)}, u32[]{:S(2)}) collective-permute-start(bf16[272,128]{1,0:T(8,128)(2,1)S(1)} %get-tuple-element.60), channel_id=1, source_target_pairs={{0,32},{8,40},{16,48},{24,56},{32,16},{40,24},{48,0},{56,8},{1,33}... | collective-permute-start | bytes 208904 | tf_op jit(solution)/shard_map/ppermute | solution.py:507
  174.1 7.2 %collective-permute-start.13 = (bf16[272,128]{1,0:T(8,128)(2,1)S(1)}, bf16[272,128]{1,0:T(8,128)(2,1)S(1)}, u32[]{:S(2)}, u32[]{:S(2)}) collective-permute-start(bf16[272,128]{1,0:T(8,128)(2,1)S(1)} %get-tuple-element.59), channel_id=1, source_target_pairs={{0,16},{8,24},{16,0},{24,8},{32,48},{40,56},{48,32},{56,40},{1,17}... | collective-permute-start | bytes 208904 | tf_op jit(solution)/shard_map/ppermute | solution.py:507
  174.5 8.3 %collective-permute-start.14 = (bf16[272,128]{1,0:T(8,128)(2,1)S(1)}, bf16[272,128]{1,0:T(8,128)(2,1)S(1)}, u32[]{:S(2)}, u32[]{:S(2)}) collective-permute-start(bf16[272,128]{1,0:T(8,128)(2,1)S(1)} %get-tuple-element.58), channel_id=1, source_target_pairs={{0,48},{8,56},{16,32},{24,40},{32,0},{40,8},{48,16},{56,24},{1,49}... | collective-permute-start | bytes 208904 | tf_op jit(solution)/shard_map/ppermute | solution.py:507
  227.7 6.2 %collective-permute-start.15 = (bf16[4,128,1024]{2,1,0:T(8,128)(2,1)}, bf16[4,128,1024]{2,1,0:T(8,128)(2,1)}, u32[]{:S(2)}, u32[]{:S(2)}) collective-permute-start(bf16[4,128,1024]{2,1,0:T(8,128)(2,1)} %get-tuple-element.53), channel_id=1, source_target_pairs={{0,1},{1,0},{2,3},{3,2},{4,5},{5,4},{6,7},{7,6},{8,9},{9,8},{10,11... | collective-permute-start | bytes 3145736 | tf_op jit(solution)/shard_map/ppermute | solution.py:512
  235.9 28.0 %copy-start.14 = (s32[1,128]{1,0:T(1,128)S(1)}, s32[1,128]{1,0:T(1,128)}, u32[]{:S(2)}) copy-start(s32[1,128]{1,0:T(1,128)} %param.18) | copy-start | bytes 1540
  256.7 1.3 collective-permute-start.17
  258.6 8.4 %collective-permute-start.18 = (f32[8,128]{1,0:T(8,128)S(1)}, f32[8,128]{1,0:T(8,128)S(1)}, u32[]{:S(2)}, u32[]{:S(2)}) collective-permute-start(f32[8,128]{1,0:T(8,128)S(1)} %broadcast_add_fusion), channel_id=1, source_target_pairs={{0,64},{64,128},{128,192},{192,0},{1,65},{65,129},{129,193},{193,1... | collective-permute-start | bytes 12296 | tf_op jit(solution)/shard_map/ppermute | solution.py:448
  260.6 6.4 %collective-permute-start.19 = (f32[8,128]{1,0:T(8,128)S(1)}, f32[8,128]{1,0:T(8,128)S(1)}, u32[]{:S(2)}, u32[]{:S(2)}) collective-permute-start(f32[8,128]{1,0:T(8,128)S(1)} %broadcast_add_fusion), channel_id=1, source_target_pairs={{0,128},{64,192},{128,0},{192,64},{1,129},{65,193},{129,1},{193,65... | collective-permute-start | bytes 12296 | tf_op jit(solution)/shard_map/ppermute | solution.py:448
  261.8 5.3 %collective-permute-start.20 = (f32[8,128]{1,0:T(8,128)S(1)}, f32[8,128]{1,0:T(8,128)S(1)}, u32[]{:S(2)}, u32[]{:S(2)}) collective-permute-start(f32[8,128]{1,0:T(8,128)S(1)} %broadcast_add_fusion), channel_id=1, source_target_pairs={{0,192},{64,0},{128,64},{192,128},{1,193},{65,1},{129,65},{193,129... | collective-permute-start | bytes 12296 | tf_op jit(solution)/shard_map/ppermute | solution.py:448
  263.8 19.5 %collective-permute-start.16 = (bf16[128,1024]{1,0:T(8,128)(2,1)S(1)}, bf16[128,1024]{1,0:T(8,128)(2,1)S(1)}, u32[]{:S(2)}, u32[]{:S(2)}) collective-permute-start(bf16[128,1024]{1,0:T(8,128)(2,1)S(1)} %get-tuple-element.57), channel_id=1, source_target_pairs={{0,0},{1,1},{64,2},{65,3},{128,4},{129,5},{192,6},{193,7},{2,8},{3... | collective-permute-start | bytes 786440 | tf_op jit(solution)/shard_map/ppermute | solution.py:519
  267.7 13.8 %collective-permute-start.21 = (f32[8,128]{1,0:T(8,128)S(1)}, f32[8,128]{1,0:T(8,128)S(1)}, u32[]{:S(2)}, u32[]{:S(2)}) collective-permute-start(f32[8,128]{1,0:T(8,128)S(1)} %add_add_fusion), channel_id=1, source_target_pairs={{0,0},{1,1},{64,2},{65,3},{128,4},{129,5},{192,6},{193,7},{2,8},{3... | collective-permute-start | bytes 12296 | tf_op jit(solution)/shard_map/ppermute | solution.py:522
  284.7 15.7 %all-to-all-start.5 = ((bf16[16,2,1152]{2,1,0:T(2,128)(2,1)}), bf16[16,2,1152]{2,1,0:T(2,128)(2,1)S(1)}, u32[]{:S(2)}, u32[]{:S(2)}) async-start(bf16[16,2,1152]{2,1,0:T(2,128)(2,1)} %all_to_all.35), calls=%async_computation.5 | async-start | bytes 147456 | tf_op jit(solution)/shard_map/all_to_all | solution.py:531
  (9 other events, 59.9 us)
Sparse Core Ops, SparseCore 0:
  9.8 67.5 all-gather.1

commit v3 on v2

--- a/solution.py
+++ b/solution.py
@@ -14,7 +14,6 @@
 CHUNK = 128
 WIDE = 1408
 PLACE = (0, 2, 1, 3)
-GATHERED = 768
 HIGH = lax.Precision.HIGHEST
 VMEM = pl.BlockSpec(memory_space=pltpu.VMEM)
 SMEM = pl.BlockSpec(memory_space=pltpu.SMEM)
@@ -100,15 +99,15 @@
 
 
 def pack_kernel(w_x, w_bc, w_dt, out):
-    out[:, 0:256] = w_x[:, GATHERED:1024]
-    out[:, 256:512] = w_bc[...]
-    out[:, 512:640] = jnp.zeros((256, 128), BF16)
-    out[:, 512:528] = w_dt[...]
+    out[:, 0:1024] = w_x[...]
+    out[:, 1024:1280] = w_bc[...]
+    out[:, 1280:1408] = jnp.zeros((256, 128), BF16)
+    out[:, 1280:1296] = w_dt[...]
 
 
 def pack(*parts):
     return pl.pallas_call(
-        pack_kernel, in_specs=[VMEM] * 3, out_specs=VMEM, out_shape=jax.ShapeDtypeStruct((256, WIDE - GATHERED), BF16)
+        pack_kernel, in_specs=[VMEM] * 3, out_specs=VMEM, out_shape=jax.ShapeDtypeStruct((256, WIDE), BF16)
     )(*parts)
 
 
@@ -122,22 +121,16 @@
     return pl.multiple_of(row, 256)
 
 
-def project_kernel(meta, own, oth, probe, w, *rest):
-    blocks, (out, kept), (buf, rows, sems, out_sems) = rest[:9], rest[9:11], rest[11:]
+def project_kernel(meta, own, oth, probe, *rest):
+    blocks, (out, kept), (buf, rows, sems, out_sem) = rest[:9], rest[9:11], rest[11:]
     copies = []
-    for t, (lo, hi) in enumerate(TILES[:3]):
-        for n in range(2):
-            here = pl.ds(pl.multiple_of(lax.rem(meta[0] + n, 2) * 1024, 1024), 1024)
-            there = buf.at[1024 * n : 1024 * n + 1024, lo:hi]
-            copies.append(pltpu.make_async_copy(w.at[here, lo:hi], there, sems.at[2 * t + n]))
     for i in range(7):
-        there = buf.at[pl.ds(ring_rows(meta, i), 256), GATHERED:WIDE]
-        copies.append(pltpu.make_async_copy(blocks[i], there, sems.at[6 + i]))
+        there = buf.at[pl.ds(ring_rows(meta, i), 256)]
+        copies.append(pltpu.make_async_copy(blocks[i], there, sems.at[i]))
     for n in range(2):
-        there = buf.at[pl.ds(pl.multiple_of(ring_rows(meta, 7) + 128 * n, 128), 128), GATHERED:WIDE]
-        copies.append(pltpu.make_async_copy(blocks[7 + n], there, sems.at[13 + n]))
-    stores = [pltpu.make_async_copy(buf.at[:, lo:hi], kept.at[:, lo:hi], out_sems.at[t]) for t, (lo, hi) in enumerate(TILES[:3])]
-    stores.append(pltpu.make_async_copy(buf.at[:, GATHERED:WIDE], kept.at[:, GATHERED:WIDE], out_sems.at[3]))
+        there = buf.at[pl.ds(pl.multiple_of(ring_rows(meta, 7) + 128 * n, 128), 128)]
+        copies.append(pltpu.make_async_copy(blocks[7 + n], there, sems.at[7 + n]))
+    store = pltpu.make_async_copy(buf, kept, out_sem)
     for copy in copies:
         copy.start()
     for n, ref in enumerate((own, oth)):
@@ -148,11 +141,10 @@
         part = slice(256 * d, 256 * d + 256)
         out[d, 528:592, 0:256] = probe[0:64, part]
         out[d, 528:592, 256:512] = probe[64:128, part]
+    for copy in copies:
+        copy.wait()
+    store.start()
     for t, (lo, hi) in enumerate(TILES):
-        if t <= 3:
-            for copy in copies[2 * t : 2 * t + 2] if t < 3 else copies[6:]:
-                copy.wait()
-            stores[t].start()
         total = dot_nn(rows[...], buf[:, lo:hi])
         if t < 4:
             out[t, 0:512, 0:256] = total.astype(BF16)
@@ -164,23 +156,22 @@
             for d in range(4):
                 mine = jnp.concatenate([steps[4 * d : 4 * d + 4], jnp.zeros((4, 512), F32), ids], axis=0)
                 out[d, 512:528, :] = mine.astype(BF16)
-    for store in stores:
-        store.wait()
-
-
-def project(meta, own, oth, probe, w, blocks):
+    store.wait()
+
+
+def project(meta, own, oth, probe, blocks):
     return pl.pallas_call(
         project_kernel,
-        in_specs=[SMEM, VMEM, VMEM, VMEM] + [ANY] * 10,
+        in_specs=[SMEM, VMEM, VMEM, VMEM] + [ANY] * 9,
         out_specs=[VMEM, ANY],
         out_shape=[jax.ShapeDtypeStruct((4, 592, 512), BF16), jax.ShapeDtypeStruct((2048, WIDE), BF16)],
         scratch_shapes=[
             pltpu.VMEM((2048, WIDE), BF16),
             pltpu.VMEM((512, 2048), BF16),
-            pltpu.SemaphoreType.DMA((15,)),
-            pltpu.SemaphoreType.DMA((4,)),
+            pltpu.SemaphoreType.DMA((9,)),
+            pltpu.SemaphoreType.DMA,
         ],
-    )(meta, own, oth, probe, w, *blocks)
+    )(meta, own, oth, probe, *blocks)
 
 
 def prepare_kernel(meta, r, prm, pay, x, bc, rows_out, cols_out, t_out, q_out, p):
@@ -461,7 +452,6 @@
     origin = 2 * lax.rem(across, 2) + across // 2
     quarter = 2 * lax.rem(origin, 2) + z_at // 4
     meta = jnp.stack([core_at, origin, quarter, z_at]).astype(jnp.int32)
-    gathered = lax.all_gather(w_x[:, :GATHERED], "z", axis=0, tiled=True)
     segment = segments[0]
     before = lax.ppermute(segment[-1:], X + ("z",), [(i, i + 1) for i in range(31)])
     ids = jnp.concatenate([segment[None], jnp.broadcast_to(before[None], (15, CHUNK))]).astype(BF16)
@@ -475,21 +465,18 @@
 
     w_ring = pack(w_x, w_bc, w_dt)
     r1, l1 = right(w_ring), left(w_ring)
+    probe_ids = lax.ppermute(probe_ids, X + ("z",), probe_route())
     frame_emb = jnp.dot(frame_feats[0], w_proj, preferred_element_type=F32).astype(BF16)
     slot = frame_pos[0] - CHUNK * (jnp.arange(32, dtype=jnp.int32) // 2)
     tagged = jnp.concatenate([frame_emb, jnp.broadcast_to(slot.astype(BF16)[:, None], (32, 128))], axis=1)
     arrived = lax.all_to_all(tagged, SEQ, split_axis=0, concat_axis=0, tiled=True)
     local_pos = arrived[:, 1024].astype(jnp.int32)
     merged = tokens[0].at[local_pos].set(arrived[:, :1024])
-    merged, r1, l1 = lax.optimization_barrier((merged, r1, l1))
     moved = lax.ppermute(merged, AXES, features_route())
     r2, l2 = right(r1), left(l1)
-    moved, r2, l2, probe_ids = lax.optimization_barrier((moved, r2, l2, probe_ids))
     r3, l3 = right(r2), left(l2)
     own = to_all(moved, "y")
-    own, r3, l3, probe_ids = lax.optimization_barrier((own, r3, l3, probe_ids))
     r4, l4 = right(r3[:128]), left(l3[128:])
-    probe_ids = lax.ppermute(probe_ids, X + ("z",), probe_route())
     oth = lax.ppermute(own, "core", SWAP)
 
     def four(v):
@@ -501,7 +488,7 @@
     skip = jnp.repeat(four(skip_gain), 64)[None, :]
 
     blocks = (w_ring, r1, l1, r2, l2, r3, l3, r4, l4)
-    partial_proj, weights = project(meta, own, oth, probe_ids, gathered, blocks)
+    partial_proj, weights = project(meta, own, oth, probe_ids, blocks)
     received = lax.all_to_all(partial_proj, X, split_axis=0, concat_axis=0)
     pay, values, bc, rows, cols, t_all, q_all, probes = prepare(meta, received, prm)
     got = [lax.ppermute(pay[k - 1], "z", quarter_route(k)) for k in (1, 2, 3)]

time: 312 us -> 299 us (0.958)
  between operations: 17.7 us -> 4.5 us
  waiting for transfers between devices: 84.8 us -> 97 us
  starting transfers between devices: 76.7 us -> 66.7 us
    ppermute x1, waiting for transfers between devices: 0.01 us -> 17.7 us  [body(): moved = lax.ppermute(merged, AXES, features_route())]
    all_to_all x1, starting transfers between devices: 15.6 us -> 4.25 us  [to_all(): lax.all_to_all(jnp.broadcast_to(x[None], (4,) + x.shape), axis, split_axi...]
    ppermute x4, waiting for transfers between devices: 10.6 us -> 0.01 us  [right(): return lax.ppermute(v, 'z', [(i, (i + 1) % 8) for i in range(8)])]
    ppermute x1, waiting for transfers between devices: 15.6 us -> 5.72 us  [body(): lax.ppermute(segment[-1:], X + ('z',), [(i, i + 1) for i in range(31)])]
    all_to_all x1, waiting for transfers between devices: 3.5 us -> 11.3 us  [to_all(): lax.all_to_all(jnp.broadcast_to(x[None], (4,) + x.shape), axis, split_axi...]
    ppermute x1, waiting for transfers between devices: 8.91 us -> 16.3 us  [body(): probe_ids = lax.ppermute(probe_ids, X + ('z',), probe_route())]
    ppermute x1, starting transfers between devices: 4.62 us -> 8.07 us  [body(): moved = lax.ppermute(merged, AXES, features_route())]
  transfers between devices with their start and end apart: 26 -> 25, of which waited for: 10 -> 9; matrix products, arithmetic and copies ran while one was open for 3% -> 4% of each run, Pallas kernels for 4% -> 4%
where the time goes in v3:
time: 299 us; the launch traced here: 298 us
  waiting for transfers between devices  97 us (32%)
  starting transfers between devices  66.7 us (22%)
  blocking collectives  63.9 us (21%)
  Pallas kernels  41.5 us (14%)
  local copies, waits for them, and re-layouts  13.9 us (5%)
  other arithmetic  8.96 us (3%)
  between operations  4.5 us (2%)
    all_to_all x1, blocking collectives, to_all(): lax.all_to_all(jnp.broadcast_to(x[None], (4,) + x.shape), axis, split_axi...  27.4 us
    all_to_all x1, waiting for transfers between devices, body(): received = lax.all_to_all(partial_proj, X, split_axis=0, concat_axis=0)  27.3 us
    all_to_all x1, blocking collectives, body(): pieces = lax.all_to_all(both, 'y', split_axis=0, concat_axis=0)  18.5 us
    all_to_all x1, blocking collectives, body(): lax.all_to_all(tagged, SEQ, split_axis=0, concat_axis=0, tiled=True)  18.1 us
    ppermute x1, waiting for transfers between devices, body(): moved = lax.ppermute(merged, AXES, features_route())  17.7 us
    ppermute x1, waiting for transfers between devices, body(): probe_ids = lax.ppermute(probe_ids, X + ('z',), probe_route())  16.3 us
    ppermute x4, starting transfers between devices, left(): return lax.ppermute(v, 'z', [(i, (i + 7) % 8) for i in range(8)])  13.2 us
    all_to_all x1, waiting for transfers between devices, to_all(): lax.all_to_all(jnp.broadcast_to(x[None], (4,) + x.shape), axis, split_axi...  11.3 us
  transfers between devices with their start and end apart: 25, of which 9 were waited for; matrix products, arithmetic and copies ran while one was open for 4% of the time, Pallas kernels for 4%

profile of v3, /device:TPU:4, one launch (start us, length us, event | category | flops | bytes accessed | tf_op | source)
XLA Modules:
  0.0 297.9 jit_solution(12674088963487789494)
XLA Ops:
  2.2 2.1 shard_map.140.rest_0_
  4.3 1.9 collective-permute-start.4
  6.2 3.9 %collective-permute-start.5 = (bf16[256,1408]{1,0:T(8,128)(2,1)}, bf16[256,1408]{1,0:T(8,128)(2,1)}, u32[]{:S(2)}, u32[]{:S(2)}) collective-permute-start(bf16[256,1408]{1,0:T(8,128)(2,1)} %shard_map.140.rest_0_), channel_id=1, source_target_pairs={{0,56},{8,0},{16,8},{24,16},{32,24},{40,32},{48,40},{56,48},{1,57}... | collective-permute-start | bytes 2162696 | tf_op jit(solution)/shard_map/ppermute | solution.py:464
  11.8 18.1 %all_to_all.46 = bf16[16,2,1152]{2,1,0:T(2,128)(2,1)S(1)} all-to-all(bf16[16,2,1152]{2,1,0:T(2,128)(2,1)S(1)} %all_to_all.28), channel_id=1, replica_groups=mesh['x_hi'=2,'x_lo'=2,'z'=8,'y'=4,'core'=2] {'x_lo','z'}, dimensions={0} | all-to-all | bytes 147456 | tf_op jit(solution)/shard_map/all_to_all | solution.py:472
  30.9 8.1 %collective-permute-start = (bf16[128,1024]{1,0:T(8,128)(2,1)S(1)}, bf16[128,1024]{1,0:T(8,128)(2,1)S(1)}, u32[]{:S(2)}, u32[]{:S(2)}) collective-permute-start(bf16[128,1024]{1,0:T(8,128)(2,1)S(1)} %scatter_custom_fusion), channel_id=1, source_target_pairs={{0,0},{1,1},{2,64},{3,65},{4,128},{5,129},{6,192},{7,193},{8,2},{9... | collective-permute-start | bytes 786440 | tf_op jit(solution)/shard_map/ppermute | solution.py:475
  39.5 2.9 collective-permute-start.7
  42.4 17.7 %collective-permute-done = bf16[128,1024]{1,0:T(8,128)(2,1)S(1)} collective-permute-done((bf16[128,1024]{1,0:T(8,128)(2,1)S(1)}, bf16[128,1024]{1,0:T(8,128)(2,1)S(1)}, u32[]{:S(2)}, u32[]{:S(2)}) %collective-permute-start) | collective-permute-done | bytes 262176 | tf_op jit(solution)/shard_map/ppermute | solution.py:475
  61.1 4.2 %all-to-all-start.1 = ((bf16[4,128,1024]{2,1,0:T(8,128)(2,1)}), bf16[4,128,1024]{2,1,0:T(8,128)(2,1)}, u32[]{:S(2)}, u32[]{:S(2)}) async-start(bf16[4,128,1024]{2,1,0:T(8,128)(2,1)} %broadcast_in_dim.30), calls=%async_computation.1 | async-start | bytes 2097152 | tf_op jit(solution)/shard_map/all_to_all | solution.py:435
  65.5 3.2 %collective-permute-start.9 = (bf16[256,1408]{1,0:T(8,128)(2,1)}, bf16[256,1408]{1,0:T(8,128)(2,1)}, u32[]{:S(2)}, u32[]{:S(2)}) collective-permute-start(bf16[256,1408]{1,0:T(8,128)(2,1)} %collective-permute-done.7.rest_4_), channel_id=1, source_target_pairs={{0,56},{8,0},{16,8},{24,16},{32,24},{40,32},{48,40},{56,48},{1,57}... | collective-permute-start | bytes 2162696 | tf_op jit(solution)/shard_map/ppermute | solution.py:464
  68.7 11.3 %all-to-all-done.1.own = bf16[4,128,1024]{2,1,0:T(8,128)(2,1)} async-done(((bf16[4,128,1024]{2,1,0:T(8,128)(2,1)}), bf16[4,128,1024]{2,1,0:T(8,128)(2,1)}, u32[]{:S(2)}, u32[]{:S(2)}) %all-to-all-start.1) | async-done | bytes 1048608 | tf_op jit(solution)/shard_map/all_to_all | solution.py:435
  82.5 5.7 %collective-permute-done.2 = s32[1]{0:T(128)} collective-permute-done((s32[1]{0:T(128)}, s32[1]{0:T(128)}, u32[]{:S(2)}, u32[]{:S(2)}) %collective-permute-start.2) | collective-permute-done | bytes 36 | tf_op jit(solution)/shard_map/ppermute | solution.py:456
  91.6 3.2 %collective-permute-start.11 = (bf16[128,1408]{1,0:T(8,128)(2,1)}, bf16[128,1408]{1,0:T(8,128)(2,1)}, u32[]{:S(2)}, u32[]{:S(2)}) collective-permute-start(bf16[128,1408]{1,0:T(8,128)(2,1)} %slice.61), channel_id=1, source_target_pairs={{0,56},{8,0},{16,8},{24,16},{32,24},{40,32},{48,40},{56,48},{1,57}... | collective-permute-start | bytes 1081352 | tf_op jit(solution)/shard_map/ppermute | solution.py:464
  99.1 16.3 %collective-permute-done.3.probe = bf16[144,1024]{1,0:T(8,128)(2,1)} collective-permute-done((bf16[144,1024]{1,0:T(8,128)(2,1)}, bf16[144,1024]{1,0:T(8,128)(2,1)}, u32[]{:S(2)}, u32[]{:S(2)}) %collective-permute-start.3) | collective-permute-done | bytes 294944 | tf_op jit(solution)/shard_map/ppermute | solution.py:468
  115.5 9.3 %shard_map.141 = (bf16[4,592,512]{2,1,0:T(8,128)(2,1)}, bf16[2048,1408]{1,0:T(8,128)(2,1)}) custom-call(s32[4]{0:T(128)} %pad_add_fusion.meta, bf16[4,128,1024]{2,1,0:T(8,128)(2,1)} %all-to-all-done.1.own, bf16[4,128,1024]{2,1,0:T(8,128)(2,1)} %collective-permute-done.1.oth, bf16[144,1024]{1,0:T(8,128)(2,1)} %collective-permute-done.3.probe, ...), custom_call_target="tpu_custom_call" | custom-call | tf_op jit(solution)/shard_map/pallas_call | solution.py:163
  124.7 8.4 %all-to-all-start.2 = ((bf16[4,592,512]{2,1,0:T(8,128)(2,1)}), bf16[4,592,512]{2,1,0:T(8,128)(2,1)}, u32[]{:S(2)}, u32[]{:S(2)}) async-start(bf16[4,592,512]{2,1,0:T(8,128)(2,1)} %get-tuple-element.17), calls=%async_computation.2 | async-start | bytes 4849664 | tf_op jit(solution)/shard_map/all_to_all | solution.py:492
  133.2 27.3 %all-to-all-done.2.r = bf16[4,592,512]{2,1,0:T(8,128)(2,1)} async-done(((bf16[4,592,512]{2,1,0:T(8,128)(2,1)}), bf16[4,592,512]{2,1,0:T(8,128)(2,1)}, u32[]{:S(2)}, u32[]{:S(2)}) %all-to-all-start.2) | async-done | bytes 2424864 | tf_op jit(solution)/shard_map/all_to_all | solution.py:492
  161.2 6.1 %shard_map.142 = (bf16[3,272,128]{2,1,0:T(8,128)(2,1)}, f32[512,256]{1,0:T(8,128)}, bf16[512,256]{1,0:T(8,128)(2,1)}, f32[4,16,128]{2,1,0:T(8,128)}, f32[4,128,1...) custom-call(s32[4]{0:T(128)} %pad_add_fusion.meta, ...), custom_call_target="tpu_custom_call" | custom-call | tf_op jit(solution)/shard_map/pallas_call | solution.py:222
  168.4 2.5 collective-permute-start.12
  173.4 4.7 %shard_map.143 = (f32[512,256]{1,0:T(8,128)}, f32[512,256]{1,0:T(8,128)}, f32[4,16,128]{2,1,0:T(8,128)}) custom-call(f32[512,256]{1,0:T(8,128)} %get-tuple-element.19.x, bf16[512,256]{1,0:T(8,128)(2,1)} %get-tuple-element.20.bc, bf16[4,128,256]{2,1,0:T(8,128)(2,1)} %get-tuple-element.21.p, f32[4,16,128]{2,1,0:T(8,128)} %get-tuple-element.22.rows_in, ...), custom_call_target="tpu_custom_call" | custom-call | tf_op jit(solution)/shard_map/pallas_call | solution.py:284
  180.3 7.0 %shard_map.144 = bf16[528,512]{1,0:T(8,128)(2,1)} custom-call(s32[4]{0:T(128)} %pad_add_fusion.meta, bf16[272,128]{1,0:T(8,128)(2,1)} %copy-done.5, bf16[272,128]{1,0:T(8,128)(2,1)} %copy-done.6, bf16[272,128]{1,0:T(8,128)(2,1)} %copy-done.7, f32[512,256]{1,0:T(8,128)} %get-tuple-element.19.x, bf16[512,256]{1,0:T(8,128)(2,1)} %get-tuple-element.20.bc, ...), custom_call_target="tpu_custom_call" | custom-call | tf_op jit(solution)/shard_map/pallas_call | solution.py:365
  188.4 27.4 %all_to_all.44.g = bf16[4,528,512]{2,1,0:T(8,128)(2,1)} all-to-all(bf16[4,528,512]{2,1,0:T(8,128)(2,1)S(1)} %broadcast_in_dim.34), channel_id=1, replica_groups=mesh['x_hi'=2,'x_lo'=2,'z'=8,'y'=4,'core'=2] {'x_hi','x_lo'}, dimensions={0} | all-to-all | bytes 4325376 | tf_op jit(solution)/shard_map/all_to_all | solution.py:435
  215.8 6.3 %shard_map.145 = (bf16[1408,512]{1,0:T(8,128)(2,1)}, bf16[4,128,1024]{2,1,0:T(8,128)(2,1)}) custom-call(s32[4]{0:T(128)} %pad_add_fusion.meta, bf16[4,528,512]{2,1,0:T(8,128)(2,1)} %all_to_all.44.g, bf16[2048,1408]{1,0:T(8,128)(2,1)} %get-tuple-element.29.w), custom_call_target="tpu_custom_call" | custom-call | tf_op jit(solution)/shard_map/pallas_call | solution.py:415
  222.3 6.1 %shard_map.146 = bf16[4,128,1024]{2,1,0:T(8,128)(2,1)} custom-call(s32[4]{0:T(128)} %pad_add_fusion.meta, bf16[1408,512]{1,0:T(8,128)(2,1)} %get-tuple-element.30.full, bf16[2048,1408]{1,0:T(8,128)(2,1)} %get-tuple-element.29.w), custom_call_target="tpu_custom_call" | custom-call | tf_op jit(solution)/shard_map/pallas_call | solution.py:425
  228.4 1.9 add_convert_fusion
  230.3 18.5 %all_to_all.45 = bf16[4,128,1024]{2,1,0:T(8,128)(2,1)S(1)} all-to-all(bf16[4,128,1024]{2,1,0:T(8,128)(2,1)S(1)} %add_convert_fusion), channel_id=1, replica_groups=mesh['x_hi'=2,'x_lo'=2,'z'=8,'y'=4,'core'=2] {'y'}, dimensions={0} | all-to-all | bytes 2097152 | tf_op jit(solution)/shard_map/all_to_all | solution.py:502
  252.5 2.4 collective-permute-start.18
  255.7 2.1 collective-permute-start.20
  257.7 3.1 %collective-permute-start.16 = (bf16[128,1024]{1,0:T(8,128)(2,1)S(1)}, bf16[128,1024]{1,0:T(8,128)(2,1)S(1)}, u32[]{:S(2)}, u32[]{:S(2)}) collective-permute-start(bf16[128,1024]{1,0:T(8,128)(2,1)S(1)} %get-tuple-element.35), channel_id=1, source_target_pairs={{0,0},{1,1},{64,2},{65,3},{128,4},{129,5},{192,6},{193,7},{2,8},{3... | collective-permute-start | bytes 786440 | tf_op jit(solution)/shard_map/ppermute | solution.py:506
  261.6 6.3 %collective-permute-start.21 = (f32[8,128]{1,0:T(8,128)S(1)}, f32[8,128]{1,0:T(8,128)S(1)}, u32[]{:S(2)}, u32[]{:S(2)}) collective-permute-start(f32[8,128]{1,0:T(8,128)S(1)} %add_add_fusion), channel_id=1, source_target_pairs={{0,0},{1,1},{64,2},{65,3},{128,4},{129,5},{192,6},{193,7},{2,8},{3... | collective-permute-start | bytes 12296 | tf_op jit(solution)/shard_map/ppermute | solution.py:509
  267.9 7.4 %collective-permute-done.21 = f32[8,128]{1,0:T(8,128)S(1)} collective-permute-done((f32[8,128]{1,0:T(8,128)S(1)}, f32[8,128]{1,0:T(8,128)S(1)}, u32[]{:S(2)}, u32[]{:S(2)}) %collective-permute-start.21) | collective-permute-done | bytes 4128 | tf_op jit(solution)/shard_map/ppermute | solution.py:509
  278.6 7.1 %all-to-all-start.5 = ((bf16[16,2,1152]{2,1,0:T(2,128)(2,1)}), bf16[16,2,1152]{2,1,0:T(2,128)(2,1)S(1)}, u32[]{:S(2)}, u32[]{:S(2)}) async-start(bf16[16,2,1152]{2,1,0:T(2,128)(2,1)} %all_to_all.35), calls=%async_computation.5 | async-start | bytes 147456 | tf_op jit(solution)/shard_map/all_to_all | solution.py:518
  285.7 8.5 %all-to-all-done.5 = bf16[16,2,1152]{2,1,0:T(2,128)(2,1)S(1)} async-done(((bf16[16,2,1152]{2,1,0:T(2,128)(2,1)}), bf16[16,2,1152]{2,1,0:T(2,128)(2,1)S(1)}, u32[]{:S(2)}, u32[]{:S(2)}) %all-to-all-start.5) | async-done | bytes 73760 | tf_op jit(solution)/shard_map/all_to_all | solution.py:518
  (105 shorter events, 32.4 us)
Async XLA Ops:
  2.2 27.8 %copy-start.4 = (bf16[1,128,1024]{2,1,0:T(8,128)(2,1)S(1)}, bf16[1,128,1024]{2,1,0:T(8,128)(2,1)}, u32[]{:S(2)}) copy-start(bf16[1,128,1024]{2,1,0:T(8,128)(2,1)} %param.13) | copy-start | bytes 786436
  4.3 34.7 %collective-permute-start.4 = (bf16[256,1408]{1,0:T(8,128)(2,1)}, bf16[256,1408]{1,0:T(8,128)(2,1)}, u32[]{:S(2)}, u32[]{:S(2)}) collective-permute-start(bf16[256,1408]{1,0:T(8,128)(2,1)} %shard_map.140.rest_0_), channel_id=1, source_target_pairs={{0,8},{8,16},{16,24},{24,32},{32,40},{40,48},{48,56},{56,0},{1,9},... | collective-permute-start | bytes 2162696 | tf_op jit(solution)/shard_map/ppermute | solution.py:461
  6.2 33.3 %collective-permute-start.5 = (bf16[256,1408]{1,0:T(8,128)(2,1)}, bf16[256,1408]{1,0:T(8,128)(2,1)}, u32[]{:S(2)}, u32[]{:S(2)}) collective-permute-start(bf16[256,1408]{1,0:T(8,128)(2,1)} %shard_map.140.rest_0_), channel_id=1, source_target_pairs={{0,56},{8,0},{16,8},{24,16},{32,24},{40,32},{48,40},{56,48},{1,57}... | collective-permute-start | bytes 2162696 | tf_op jit(solution)/shard_map/ppermute | solution.py:464
  11.6 68.4 %copy-start.11 = (s32[1,128]{1,0:T(1,128)S(1)}, s32[1,128]{1,0:T(1,128)}, u32[]{:S(2)}) copy-start(s32[1,128]{1,0:T(1,128)} %param.17) | copy-start | bytes 1540
  30.9 34.5 %copy-start.2 = (bf16[128,1024]{1,0:T(8,128)(2,1)}, bf16[128,1024]{1,0:T(8,128)(2,1)S(1)}, u32[]{:S(2)}) copy-start(bf16[128,1024]{1,0:T(8,128)(2,1)S(1)} %scatter_custom_fusion) | copy-start | bytes 786436
  30.9 29.1 %collective-permute-start = (bf16[128,1024]{1,0:T(8,128)(2,1)S(1)}, bf16[128,1024]{1,0:T(8,128)(2,1)S(1)}, u32[]{:S(2)}, u32[]{:S(2)}) collective-permute-start(bf16[128,1024]{1,0:T(8,128)(2,1)S(1)} %scatter_custom_fusion), channel_id=1, source_target_pairs={{0,0},{1,1},{2,64},{3,65},{4,128},{5,129},{6,192},{7,193},{8,2},{9... | collective-permute-start | bytes 786440 | tf_op jit(solution)/shard_map/ppermute | solution.py:475
  39.0 26.4 %collective-permute-start.6 = (bf16[256,1408]{1,0:T(8,128)(2,1)}, bf16[256,1408]{1,0:T(8,128)(2,1)}, u32[]{:S(2)}, u32[]{:S(2)}) collective-permute-start(bf16[256,1408]{1,0:T(8,128)(2,1)} %collective-permute-done.4.rest_1_), channel_id=1, source_target_pairs={{0,8},{8,16},{16,24},{24,32},{32,40},{40,48},{48,56},{56,0},{1,9},... | collective-permute-start | bytes 2162696 | tf_op jit(solution)/shard_map/ppermute | solution.py:461
  39.5 26.0 %collective-permute-start.7 = (bf16[256,1408]{1,0:T(8,128)(2,1)}, bf16[256,1408]{1,0:T(8,128)(2,1)}, u32[]{:S(2)}, u32[]{:S(2)}) collective-permute-start(bf16[256,1408]{1,0:T(8,128)(2,1)} %collective-permute-done.5.rest_2_), channel_id=1, source_target_pairs={{0,56},{8,0},{16,8},{24,16},{32,24},{40,32},{48,40},{56,48},{1,57}... | collective-permute-start | bytes 2162696 | tf_op jit(solution)/shard_map/ppermute | solution.py:464
  61.1 18.9 %all-to-all-start.1 = ((bf16[4,128,1024]{2,1,0:T(8,128)(2,1)}), bf16[4,128,1024]{2,1,0:T(8,128)(2,1)}, u32[]{:S(2)}, u32[]{:S(2)}) async-start(bf16[4,128,1024]{2,1,0:T(8,128)(2,1)} %broadcast_in_dim.30), calls=%async_computation.1 | async-start | bytes 2097152 | tf_op jit(solution)/shard_map/all_to_all | solution.py:435
  65.4 23.6 %collective-permute-start.8 = (bf16[256,1408]{1,0:T(8,128)(2,1)}, bf16[256,1408]{1,0:T(8,128)(2,1)S(1)}, u32[]{:S(2)}, u32[]{:S(2)}) collective-permute-start(bf16[256,1408]{1,0:T(8,128)(2,1)} %collective-permute-done.6.rest_3_), channel_id=1, source_target_pairs={{0,8},{8,16},{16,24},{24,32},{32,40},{40,48},{48,56},{56,0},{1,9},... | collective-permute-start | bytes 2162696 | tf_op jit(solution)/shard_map/ppermute | solution.py:461
  65.5 24.3 %collective-permute-start.9 = (bf16[256,1408]{1,0:T(8,128)(2,1)}, bf16[256,1408]{1,0:T(8,128)(2,1)}, u32[]{:S(2)}, u32[]{:S(2)}) collective-permute-start(bf16[256,1408]{1,0:T(8,128)(2,1)} %collective-permute-done.7.rest_4_), channel_id=1, source_target_pairs={{0,56},{8,0},{16,8},{24,16},{32,24},{40,32},{48,40},{56,48},{1,57}... | collective-permute-start | bytes 2162696 | tf_op jit(solution)/shard_map/ppermute | solution.py:464
  80.0 35.4 %collective-permute-start.1 = (bf16[4,128,1024]{2,1,0:T(8,128)(2,1)}, bf16[4,128,1024]{2,1,0:T(8,128)(2,1)}, u32[]{:S(2)}, u32[]{:S(2)}) collective-permute-start(bf16[4,128,1024]{2,1,0:T(8,128)(2,1)} %all-to-all-done.1.own), channel_id=1, source_target_pairs={{0,1},{1,0},{2,3},{3,2},{4,5},{5,4},{6,7},{7,6},{8,9},{9,8},{10,11... | collective-permute-start | bytes 3145736 | tf_op jit(solution)/shard_map/ppermute | solution.py:480
  80.6 7.6 %collective-permute-start.2 = (s32[1]{0:T(128)}, s32[1]{0:T(128)}, u32[]{:S(2)}, u32[]{:S(2)}) collective-permute-start(s32[1]{0:T(128)} %bitcast.9), channel_id=1, source_target_pairs={{0,8},{8,16},{16,24},{24,32},{32,40},{40,48},{48,56},{56,64},{64,7... | collective-permute-start | bytes 20 | tf_op jit(solution)/shard_map/ppermute | solution.py:456
  89.0 26.5 %copy-start.1 = (bf16[256,1408]{1,0:T(8,128)(2,1)}, bf16[256,1408]{1,0:T(8,128)(2,1)S(1)}, u32[]{:S(2)}) copy-start(bf16[256,1408]{1,0:T(8,128)(2,1)S(1)} %collective-permute-done.8.rest_5_) | copy-start | bytes 2162692
  89.9 25.6 %collective-permute-start.10 = (bf16[128,1408]{1,0:T(8,128)(2,1)}, bf16[128,1408]{1,0:T(8,128)(2,1)}, u32[]{:S(2)}, u32[]{:S(2)}) collective-permute-start(bf16[128,1408]{1,0:T(8,128)(2,1)} %slice.60), channel_id=1, source_target_pairs={{0,8},{8,16},{16,24},{24,32},{32,40},{40,48},{48,56},{56,0},{1,9},... | collective-permute-start | bytes 1081352 | tf_op jit(solution)/shard_map/ppermute | solution.py:461
  91.6 23.8 %collective-permute-start.11 = (bf16[128,1408]{1,0:T(8,128)(2,1)}, bf16[128,1408]{1,0:T(8,128)(2,1)}, u32[]{:S(2)}, u32[]{:S(2)}) collective-permute-start(bf16[128,1408]{1,0:T(8,128)(2,1)} %slice.61), channel_id=1, source_target_pairs={{0,56},{8,0},{16,8},{24,16},{32,24},{40,32},{48,40},{56,48},{1,57}... | collective-permute-start | bytes 1081352 | tf_op jit(solution)/shard_map/ppermute | solution.py:464
  96.5 18.9 %collective-permute-start.3 = (bf16[144,1024]{1,0:T(8,128)(2,1)}, bf16[144,1024]{1,0:T(8,128)(2,1)}, u32[]{:S(2)}, u32[]{:S(2)}) collective-permute-start(bf16[144,1024]{1,0:T(8,128)(2,1)} %pad_maximum_fusion), channel_id=1, source_target_pairs={{0,0},{8,64},{16,128},{24,192},{32,32},{40,96},{48,160},{56,224},{... | collective-permute-start | bytes 884744 | tf_op jit(solution)/shard_map/ppermute | solution.py:468
  124.7 35.9 %all-to-all-start.2 = ((bf16[4,592,512]{2,1,0:T(8,128)(2,1)}), bf16[4,592,512]{2,1,0:T(8,128)(2,1)}, u32[]{:S(2)}, u32[]{:S(2)}) async-start(bf16[4,592,512]{2,1,0:T(8,128)(2,1)} %get-tuple-element.17), calls=%async_computation.2 | async-start | bytes 4849664 | tf_op jit(solution)/shard_map/all_to_all | solution.py:492
  133.1 39.4 %copy-start.12 = (f32[16]{0:T(128)S(1)}, f32[16]{0:T(128)}, u32[]{:S(2)}) copy-start(f32[16]{0:T(128)} %param.24) | copy-start | bytes 196
  168.4 9.7 %collective-permute-start.12 = (bf16[272,128]{1,0:T(8,128)(2,1)S(1)}, bf16[272,128]{1,0:T(8,128)(2,1)S(1)}, u32[]{:S(2)}, u32[]{:S(2)}) collective-permute-start(bf16[272,128]{1,0:T(8,128)(2,1)S(1)} %get-tuple-element.38), channel_id=1, source_target_pairs={{0,32},{8,40},{16,48},{24,56},{32,16},{40,24},{48,0},{56,8},{1,33}... | collective-permute-start | bytes 208904 | tf_op jit(solution)/shard_map/ppermute | solution.py:494
  170.9 7.2 %collective-permute-start.13 = (bf16[272,128]{1,0:T(8,128)(2,1)S(1)}, bf16[272,128]{1,0:T(8,128)(2,1)S(1)}, u32[]{:S(2)}, u32[]{:S(2)}) collective-permute-start(bf16[272,128]{1,0:T(8,128)(2,1)S(1)} %get-tuple-element.37), channel_id=1, source_target_pairs={{0,16},{8,24},{16,0},{24,8},{32,48},{40,56},{48,32},{56,40},{1,17}... | collective-permute-start | bytes 208904 | tf_op jit(solution)/shard_map/ppermute | solution.py:494
  170.9 8.8 %collective-permute-start.14 = (bf16[272,128]{1,0:T(8,128)(2,1)S(1)}, bf16[272,128]{1,0:T(8,128)(2,1)S(1)}, u32[]{:S(2)}, u32[]{:S(2)}) collective-permute-start(bf16[272,128]{1,0:T(8,128)(2,1)S(1)} %get-tuple-element.36), channel_id=1, source_target_pairs={{0,48},{8,56},{16,32},{24,40},{32,0},{40,8},{48,16},{56,24},{1,49}... | collective-permute-start | bytes 208904 | tf_op jit(solution)/shard_map/ppermute | solution.py:494
  222.2 6.2 %collective-permute-start.15 = (bf16[4,128,1024]{2,1,0:T(8,128)(2,1)}, bf16[4,128,1024]{2,1,0:T(8,128)(2,1)}, u32[]{:S(2)}, u32[]{:S(2)}) collective-permute-start(bf16[4,128,1024]{2,1,0:T(8,128)(2,1)} %get-tuple-element.31), channel_id=1, source_target_pairs={{0,1},{1,0},{2,3},{3,2},{4,5},{5,4},{6,7},{7,6},{8,9},{9,8},{10,11... | collective-permute-start | bytes 3145736 | tf_op jit(solution)/shard_map/ppermute | solution.py:499
  230.3 27.4 %copy-start.13 = (s32[1,128]{1,0:T(1,128)S(1)}, s32[1,128]{1,0:T(1,128)}, u32[]{:S(2)}) copy-start(s32[1,128]{1,0:T(1,128)} %param.18) | copy-start | bytes 1540
  248.8 48.2 %copy-start.3 = (bf16[128,1024]{1,0:T(8,128)(2,1)S(1)}, bf16[128,1024]{1,0:T(8,128)(2,1)}, u32[]{:S(2)}) copy-start(bf16[128,1024]{1,0:T(8,128)(2,1)} %copy-done.2) | copy-start | bytes 786436
  250.4 1.5 collective-permute-start.17
  252.5 8.4 %collective-permute-start.18 = (f32[8,128]{1,0:T(8,128)S(1)}, f32[8,128]{1,0:T(8,128)S(1)}, u32[]{:S(2)}, u32[]{:S(2)}) collective-permute-start(f32[8,128]{1,0:T(8,128)S(1)} %broadcast_add_fusion), channel_id=1, source_target_pairs={{0,64},{64,128},{128,192},{192,0},{1,65},{65,129},{129,193},{193,1... | collective-permute-start | bytes 12296 | tf_op jit(solution)/shard_map/ppermute | solution.py:439
  254.8 6.1 %collective-permute-start.19 = (f32[8,128]{1,0:T(8,128)S(1)}, f32[8,128]{1,0:T(8,128)S(1)}, u32[]{:S(2)}, u32[]{:S(2)}) collective-permute-start(f32[8,128]{1,0:T(8,128)S(1)} %broadcast_add_fusion), channel_id=1, source_target_pairs={{0,128},{64,192},{128,0},{192,64},{1,129},{65,193},{129,1},{193,65... | collective-permute-start | bytes 12296 | tf_op jit(solution)/shard_map/ppermute | solution.py:439
  255.7 5.3 %collective-permute-start.20 = (f32[8,128]{1,0:T(8,128)S(1)}, f32[8,128]{1,0:T(8,128)S(1)}, u32[]{:S(2)}, u32[]{:S(2)}) collective-permute-start(f32[8,128]{1,0:T(8,128)S(1)} %broadcast_add_fusion), channel_id=1, source_target_pairs={{0,192},{64,0},{128,64},{192,128},{1,193},{65,1},{129,65},{193,129... | collective-permute-start | bytes 12296 | tf_op jit(solution)/shard_map/ppermute | solution.py:439
  257.7 19.5 %collective-permute-start.16 = (bf16[128,1024]{1,0:T(8,128)(2,1)S(1)}, bf16[128,1024]{1,0:T(8,128)(2,1)S(1)}, u32[]{:S(2)}, u32[]{:S(2)}) collective-permute-start(bf16[128,1024]{1,0:T(8,128)(2,1)S(1)} %get-tuple-element.35), channel_id=1, source_target_pairs={{0,0},{1,1},{64,2},{65,3},{128,4},{129,5},{192,6},{193,7},{2,8},{3... | collective-permute-start | bytes 786440 | tf_op jit(solution)/shard_map/ppermute | solution.py:506
  261.6 13.8 %collective-permute-start.21 = (f32[8,128]{1,0:T(8,128)S(1)}, f32[8,128]{1,0:T(8,128)S(1)}, u32[]{:S(2)}, u32[]{:S(2)}) collective-permute-start(f32[8,128]{1,0:T(8,128)S(1)} %add_add_fusion), channel_id=1, source_target_pairs={{0,0},{1,1},{64,2},{65,3},{128,4},{129,5},{192,6},{193,7},{2,8},{3... | collective-permute-start | bytes 12296 | tf_op jit(solution)/shard_map/ppermute | solution.py:509
  278.6 15.6 %all-to-all-start.5 = ((bf16[16,2,1152]{2,1,0:T(2,128)(2,1)}), bf16[16,2,1152]{2,1,0:T(2,128)(2,1)S(1)}, u32[]{:S(2)}, u32[]{:S(2)}) async-start(bf16[16,2,1152]{2,1,0:T(2,128)(2,1)} %all_to_all.35), calls=%async_computation.5 | async-start | bytes 147456 | tf_op jit(solution)/shard_map/all_to_all | solution.py:518
  (7 other events, 41.1 us)

commit v4 on v3

--- a/solution.py
+++ b/solution.py
@@ -121,7 +121,7 @@
     return pl.multiple_of(row, 256)
 
 
-def project_kernel(meta, own, oth, probe, *rest):
+def project_kernel(meta, own, oth, probe, ids_in, *rest):
     blocks, (out, kept), (buf, rows, sems, out_sem) = rest[:9], rest[9:11], rest[11:]
     copies = []
     for i in range(7):
@@ -136,7 +136,7 @@
     for n, ref in enumerate((own, oth)):
         for k in range(4):
             rows[128 * k : 128 * k + 128, 1024 * n : 1024 * n + 1024] = ref[lax.rem(k + meta[1], 4)]
-    ids = probe[128:144, 0:512].astype(F32)[0:8]
+    ids = jnp.concatenate([ids_in[...]] * 4, axis=1)
     for d in range(4):
         part = slice(256 * d, 256 * d + 256)
         out[d, 528:592, 0:256] = probe[0:64, part]
@@ -159,10 +159,10 @@
     store.wait()
 
 
-def project(meta, own, oth, probe, blocks):
+def project(meta, own, oth, probe, ids, blocks):
     return pl.pallas_call(
         project_kernel,
-        in_specs=[SMEM, VMEM, VMEM, VMEM] + [ANY] * 9,
+        in_specs=[SMEM, VMEM, VMEM, VMEM, VMEM] + [ANY] * 9,
         out_specs=[VMEM, ANY],
         out_shape=[jax.ShapeDtypeStruct((4, 592, 512), BF16), jax.ShapeDtypeStruct((2048, WIDE), BF16)],
         scratch_shapes=[
@@ -171,7 +171,7 @@
             pltpu.SemaphoreType.DMA((9,)),
             pltpu.SemaphoreType.DMA,
         ],
-    )(meta, own, oth, probe, *blocks)
+    )(meta, own, oth, probe, ids, *blocks)
 
 
 def prepare_kernel(meta, r, prm, pay, x, bc, rows_out, cols_out, t_out, q_out, p):
@@ -454,8 +454,8 @@
     meta = jnp.stack([core_at, origin, quarter, z_at]).astype(jnp.int32)
     segment = segments[0]
     before = lax.ppermute(segment[-1:], X + ("z",), [(i, i + 1) for i in range(31)])
-    ids = jnp.concatenate([segment[None], jnp.broadcast_to(before[None], (15, CHUNK))]).astype(BF16)
-    probe_ids = jnp.concatenate([probe[0], jnp.tile(ids, (1, 8))], axis=0)
+    ids = jnp.concatenate([segment[None], jnp.broadcast_to(before[None], (7, CHUNK))]).astype(F32)
+    ids = lax.ppermute(ids, X + ("z",), probe_route())
 
     def right(v):
         return lax.ppermute(v, "z", [(i, (i + 1) % 8) for i in range(8)])
@@ -465,7 +465,7 @@
 
     w_ring = pack(w_x, w_bc, w_dt)
     r1, l1 = right(w_ring), left(w_ring)
-    probe_ids = lax.ppermute(probe_ids, X + ("z",), probe_route())
+    probe_moved = lax.ppermute(probe[0], X + ("z",), probe_route())
     frame_emb = jnp.dot(frame_feats[0], w_proj, preferred_element_type=F32).astype(BF16)
     slot = frame_pos[0] - CHUNK * (jnp.arange(32, dtype=jnp.int32) // 2)
     tagged = jnp.concatenate([frame_emb, jnp.broadcast_to(slot.astype(BF16)[:, None], (32, 128))], axis=1)
@@ -488,7 +488,7 @@
     skip = jnp.repeat(four(skip_gain), 64)[None, :]
 
     blocks = (w_ring, r1, l1, r2, l2, r3, l3, r4, l4)
-    partial_proj, weights = project(meta, own, oth, probe_ids, blocks)
+    partial_proj, weights = project(meta, own, oth, probe_moved, ids, blocks)
     received = lax.all_to_all(partial_proj, X, split_axis=0, concat_axis=0)
     pay, values, bc, rows, cols, t_all, q_all, probes = prepare(meta, received, prm)
     got = [lax.ppermute(pay[k - 1], "z", quarter_route(k)) for k in (1, 2, 3)]

time: 299 us -> 314 us (1.050)
  waiting for transfers between devices: 97 us -> 109 us
    ppermute x4, waiting for transfers between devices: 0.01 us -> 29.7 us  [right(): return lax.ppermute(v, 'z', [(i, (i + 1) % 8) for i in range(8)])]
    all_to_all x1, waiting for transfers between devices: 11.3 us -> 0.01 us  [to_all(): lax.all_to_all(jnp.broadcast_to(x[None], (4,) + x.shape), axis, split_axi...]
    ppermute x1 -> x2, waiting for transfers between devices: 16.3 us -> 6.38 us  [the longest x1 6.38 us: body(): ids = lax.ppermute(ids, X + ('z',), probe_route())]
    ppermute x1, waiting for transfers between devices: 17.7 us -> 21 us  [body(): moved = lax.ppermute(merged, AXES, features_route())]
  transfers between devices with their start and end apart: 25 -> 26, of which waited for: 9 -> 10; matrix products, arithmetic and copies ran while one was open for 4% -> 3% of each run, Pallas kernels for 4% -> 3%
where the time goes in v4:
time: 314 us; the launch traced here: 312 us
  waiting for transfers between devices  109 us (35%)
  starting transfers between devices  67.7 us (22%)
  blocking collectives  66.2 us (21%)
  Pallas kernels  41.5 us (13%)
  local copies, waits for them, and re-layouts  14.4 us (5%)
  other arithmetic  8.57 us (3%)
  between operations  3.77 us (1%)
    ppermute x4, waiting for transfers between devices, right(): return lax.ppermute(v, 'z', [(i, (i + 1) % 8) for i in range(8)])  29.7 us
    all_to_all x1, blocking collectives, to_all(): lax.all_to_all(jnp.broadcast_to(x[None], (4,) + x.shape), axis, split_axi...  27.2 us
    all_to_all x1, waiting for transfers between devices, body(): received = lax.all_to_all(partial_proj, X, split_axis=0, concat_axis=0)  25.5 us
    all_to_all x1, blocking collectives, body(): pieces = lax.all_to_all(both, 'y', split_axis=0, concat_axis=0)  21.6 us
    ppermute x1, waiting for transfers between devices, body(): moved = lax.ppermute(merged, AXES, features_route())  21 us
    all_to_all x1, blocking collectives, body(): lax.all_to_all(tagged, SEQ, split_axis=0, concat_axis=0, tiled=True)  17.4 us
    ppermute x4, starting transfers between devices, left(): return lax.ppermute(v, 'z', [(i, (i + 7) % 8) for i in range(8)])  13.6 us
    ppermute x1, waiting for transfers between devices, body(): squares = lax.ppermute(squares, AXES, back)[0, 0]  9.34 us
  transfers between devices with their start and end apart: 26, of which 10 were waited for; matrix products, arithmetic and copies ran while one was open for 3% of the time, Pallas kernels for 3%

profile of v4, /device:TPU:4, one launch (start us, length us, event | category | flops | bytes accessed | tf_op | source)
XLA Modules:
  0.0 312.3 jit_solution(17547098405911744992)
XLA Ops:
  2.2 2.1 shard_map.140.rest_0_
  6.2 3.9 %collective-permute-start.6 = (bf16[256,1408]{1,0:T(8,128)(2,1)}, bf16[256,1408]{1,0:T(8,128)(2,1)}, u32[]{:S(2)}, u32[]{:S(2)}) collective-permute-start(bf16[256,1408]{1,0:T(8,128)(2,1)} %shard_map.140.rest_0_), channel_id=1, source_target_pairs={{0,56},{8,0},{16,8},{24,16},{32,24},{40,32},{48,40},{56,48},{1,57}... | collective-permute-start | bytes 2162696 | tf_op jit(solution)/shard_map/ppermute | solution.py:464
  12.4 17.4 %all_to_all.46 = bf16[16,2,1152]{2,1,0:T(2,128)(2,1)S(1)} all-to-all(bf16[16,2,1152]{2,1,0:T(2,128)(2,1)S(1)} %all_to_all.28), channel_id=1, replica_groups=mesh['x_hi'=2,'x_lo'=2,'z'=8,'y'=4,'core'=2] {'x_lo','z'}, dimensions={0} | all-to-all | bytes 147456 | tf_op jit(solution)/shard_map/all_to_all | solution.py:472
  31.0 8.2 %collective-permute-start = (bf16[128,1024]{1,0:T(8,128)(2,1)S(1)}, bf16[128,1024]{1,0:T(8,128)(2,1)S(1)}, u32[]{:S(2)}, u32[]{:S(2)}) collective-permute-start(bf16[128,1024]{1,0:T(8,128)(2,1)S(1)} %scatter_custom_fusion), channel_id=1, source_target_pairs={{0,0},{1,1},{2,64},{3,65},{4,128},{5,129},{6,192},{7,193},{8,2},{9... | collective-permute-start | bytes 786440 | tf_op jit(solution)/shard_map/ppermute | solution.py:475
  39.2 21.0 %collective-permute-done = bf16[128,1024]{1,0:T(8,128)(2,1)S(1)} collective-permute-done((bf16[128,1024]{1,0:T(8,128)(2,1)S(1)}, bf16[128,1024]{1,0:T(8,128)(2,1)S(1)}, u32[]{:S(2)}, u32[]{:S(2)}) %collective-permute-start) | collective-permute-done | bytes 262176 | tf_op jit(solution)/shard_map/ppermute | solution.py:475
  61.3 4.3 %all-to-all-start.1 = ((bf16[4,128,1024]{2,1,0:T(8,128)(2,1)}), bf16[4,128,1024]{2,1,0:T(8,128)(2,1)}, u32[]{:S(2)}, u32[]{:S(2)}) async-start(bf16[4,128,1024]{2,1,0:T(8,128)(2,1)} %broadcast_in_dim.27), calls=%async_computation.1 | async-start | bytes 2097152 | tf_op jit(solution)/shard_map/all_to_all | solution.py:435
  65.7 3.2 %collective-permute-start.8 = (bf16[256,1408]{1,0:T(8,128)(2,1)}, bf16[256,1408]{1,0:T(8,128)(2,1)}, u32[]{:S(2)}, u32[]{:S(2)}) collective-permute-start(bf16[256,1408]{1,0:T(8,128)(2,1)} %collective-permute-done.6.rest_2_), channel_id=1, source_target_pairs={{0,56},{8,0},{16,8},{24,16},{32,24},{40,32},{48,40},{56,48},{1,57}... | collective-permute-start | bytes 2162696 | tf_op jit(solution)/shard_map/ppermute | solution.py:464
  68.9 15.3 %collective-permute-done.7.rest_3_ = bf16[256,1408]{1,0:T(8,128)(2,1)} collective-permute-done((bf16[256,1408]{1,0:T(8,128)(2,1)}, bf16[256,1408]{1,0:T(8,128)(2,1)}, u32[]{:S(2)}, u32[]{:S(2)}) %collective-permute-start.7) | collective-permute-done | bytes 720928 | tf_op jit(solution)/shard_map/ppermute | solution.py:461
  84.2 3.2 %collective-permute-start.10 = (bf16[256,1408]{1,0:T(8,128)(2,1)}, bf16[256,1408]{1,0:T(8,128)(2,1)}, u32[]{:S(2)}, u32[]{:S(2)}) collective-permute-start(bf16[256,1408]{1,0:T(8,128)(2,1)} %collective-permute-done.8.rest_4_), channel_id=1, source_target_pairs={{0,56},{8,0},{16,8},{24,16},{32,24},{40,32},{48,40},{56,48},{1,57}... | collective-permute-start | bytes 2162696 | tf_op jit(solution)/shard_map/ppermute | solution.py:464
  87.5 14.4 %collective-permute-done.9.rest_5_ = bf16[256,1408]{1,0:T(8,128)(2,1)S(1)} collective-permute-done((bf16[256,1408]{1,0:T(8,128)(2,1)}, bf16[256,1408]{1,0:T(8,128)(2,1)S(1)}, u32[]{:S(2)}, u32[]{:S(2)}) %collective-permute-start.9) | collective-permute-done | bytes 720928 | tf_op jit(solution)/shard_map/ppermute | solution.py:461
  104.4 3.2 %collective-permute-start.12 = (bf16[128,1408]{1,0:T(8,128)(2,1)}, bf16[128,1408]{1,0:T(8,128)(2,1)}, u32[]{:S(2)}, u32[]{:S(2)}) collective-permute-start(bf16[128,1408]{1,0:T(8,128)(2,1)} %slice.61), channel_id=1, source_target_pairs={{0,56},{8,0},{16,8},{24,16},{32,24},{40,32},{48,40},{56,48},{1,57}... | collective-permute-start | bytes 1081352 | tf_op jit(solution)/shard_map/ppermute | solution.py:464
  112.2 5.8 %collective-permute-done.3 = s32[1]{0:T(128)} collective-permute-done((s32[1]{0:T(128)}, s32[1]{0:T(128)}, u32[]{:S(2)}, u32[]{:S(2)}) %collective-permute-start.3) | collective-permute-done | bytes 36 | tf_op jit(solution)/shard_map/ppermute | solution.py:456
  121.1 6.4 %collective-permute-done.4.ids_in = f32[8,128]{1,0:T(8,128)S(1)} collective-permute-done((f32[8,128]{1,0:T(8,128)S(1)}, f32[8,128]{1,0:T(8,128)S(1)}, u32[]{:S(2)}, u32[]{:S(2)}) %collective-permute-start.4) | collective-permute-done | bytes 4128 | tf_op jit(solution)/shard_map/ppermute | solution.py:458
  128.1 9.2 %shard_map.141 = (bf16[4,592,512]{2,1,0:T(8,128)(2,1)}, bf16[2048,1408]{1,0:T(8,128)(2,1)}) custom-call(s32[4]{0:T(128)} %pad_add_fusion.meta, bf16[4,128,1024]{2,1,0:T(8,128)(2,1)} %all-to-all-done.1.own, bf16[4,128,1024]{2,1,0:T(8,128)(2,1)} %collective-permute-done.1.oth, bf16[128,1024]{1,0:T(8,128)(2,1)} %collective-permute-done.2.probe, ...), custom_call_target="tpu_custom_call" | custom-call | tf_op jit(solution)/shard_map/pallas_call | solution.py:163
  137.4 8.3 %all-to-all-start.2 = ((bf16[4,592,512]{2,1,0:T(8,128)(2,1)}), bf16[4,592,512]{2,1,0:T(8,128)(2,1)}, u32[]{:S(2)}, u32[]{:S(2)}) async-start(bf16[4,592,512]{2,1,0:T(8,128)(2,1)} %get-tuple-element.17), calls=%async_computation.2 | async-start | bytes 4849664 | tf_op jit(solution)/shard_map/all_to_all | solution.py:492
  145.7 25.5 %all-to-all-done.2.r = bf16[4,592,512]{2,1,0:T(8,128)(2,1)} async-done(((bf16[4,592,512]{2,1,0:T(8,128)(2,1)}), bf16[4,592,512]{2,1,0:T(8,128)(2,1)}, u32[]{:S(2)}, u32[]{:S(2)}) %all-to-all-start.2) | async-done | bytes 2424864 | tf_op jit(solution)/shard_map/all_to_all | solution.py:492
  171.9 6.1 %shard_map.142 = (bf16[3,272,128]{2,1,0:T(8,128)(2,1)}, f32[512,256]{1,0:T(8,128)}, bf16[512,256]{1,0:T(8,128)(2,1)}, f32[4,16,128]{2,1,0:T(8,128)}, f32[4,128,1...) custom-call(s32[4]{0:T(128)} %pad_add_fusion.meta, ...), custom_call_target="tpu_custom_call" | custom-call | tf_op jit(solution)/shard_map/pallas_call | solution.py:222
  179.0 3.0 collective-permute-start.13
  183.0 2.0 collective-permute-start.15
  185.8 4.6 %shard_map.143 = (f32[512,256]{1,0:T(8,128)}, f32[512,256]{1,0:T(8,128)}, f32[4,16,128]{2,1,0:T(8,128)}) custom-call(f32[512,256]{1,0:T(8,128)} %get-tuple-element.19.x, bf16[512,256]{1,0:T(8,128)(2,1)} %get-tuple-element.20.bc, bf16[4,128,256]{2,1,0:T(8,128)(2,1)} %get-tuple-element.21.p, f32[4,16,128]{2,1,0:T(8,128)} %get-tuple-element.22.rows_in, ...), custom_call_target="tpu_custom_call" | custom-call | tf_op jit(solution)/shard_map/pallas_call | solution.py:284
  192.6 7.0 %shard_map.144 = bf16[528,512]{1,0:T(8,128)(2,1)} custom-call(s32[4]{0:T(128)} %pad_add_fusion.meta, bf16[272,128]{1,0:T(8,128)(2,1)} %copy-done.5, bf16[272,128]{1,0:T(8,128)(2,1)} %copy-done.6, bf16[272,128]{1,0:T(8,128)(2,1)} %copy-done.7, f32[512,256]{1,0:T(8,128)} %get-tuple-element.19.x, bf16[512,256]{1,0:T(8,128)(2,1)} %get-tuple-element.20.bc, ...), custom_call_target="tpu_custom_call" | custom-call | tf_op jit(solution)/shard_map/pallas_call | solution.py:365
  200.8 27.2 %all_to_all.44.g = bf16[4,528,512]{2,1,0:T(8,128)(2,1)} all-to-all(bf16[4,528,512]{2,1,0:T(8,128)(2,1)S(1)} %broadcast_in_dim.33), channel_id=1, replica_groups=mesh['x_hi'=2,'x_lo'=2,'z'=8,'y'=4,'core'=2] {'x_hi','x_lo'}, dimensions={0} | all-to-all | bytes 4325376 | tf_op jit(solution)/shard_map/all_to_all | solution.py:435
  228.0 6.3 %shard_map.145 = (bf16[1408,512]{1,0:T(8,128)(2,1)}, bf16[4,128,1024]{2,1,0:T(8,128)(2,1)}) custom-call(s32[4]{0:T(128)} %pad_add_fusion.meta, bf16[4,528,512]{2,1,0:T(8,128)(2,1)} %all_to_all.44.g, bf16[2048,1408]{1,0:T(8,128)(2,1)} %get-tuple-element.29.w), custom_call_target="tpu_custom_call" | custom-call | tf_op jit(solution)/shard_map/pallas_call | solution.py:415
  234.4 6.1 %shard_map.146 = bf16[4,128,1024]{2,1,0:T(8,128)(2,1)} custom-call(s32[4]{0:T(128)} %pad_add_fusion.meta, bf16[1408,512]{1,0:T(8,128)(2,1)} %get-tuple-element.30.full, bf16[2048,1408]{1,0:T(8,128)(2,1)} %get-tuple-element.29.w), custom_call_target="tpu_custom_call" | custom-call | tf_op jit(solution)/shard_map/pallas_call | solution.py:425
  240.5 1.9 add_convert_fusion
  242.5 21.6 %all_to_all.45 = bf16[4,128,1024]{2,1,0:T(8,128)(2,1)S(1)} all-to-all(bf16[4,128,1024]{2,1,0:T(8,128)(2,1)S(1)} %add_convert_fusion), channel_id=1, replica_groups=mesh['x_hi'=2,'x_lo'=2,'z'=8,'y'=4,'core'=2] {'y'}, dimensions={0} | all-to-all | bytes 2097152 | tf_op jit(solution)/shard_map/all_to_all | solution.py:502
  270.9 2.1 collective-permute-start.21
  273.0 3.1 %collective-permute-start.17 = (bf16[128,1024]{1,0:T(8,128)(2,1)S(1)}, bf16[128,1024]{1,0:T(8,128)(2,1)S(1)}, u32[]{:S(2)}, u32[]{:S(2)}) collective-permute-start(bf16[128,1024]{1,0:T(8,128)(2,1)S(1)} %get-tuple-element.35), channel_id=1, source_target_pairs={{0,0},{1,1},{64,2},{65,3},{128,4},{129,5},{192,6},{193,7},{2,8},{3... | collective-permute-start | bytes 786440 | tf_op jit(solution)/shard_map/ppermute | solution.py:506
  276.9 4.4 %collective-permute-start.22 = (f32[8,128]{1,0:T(8,128)S(1)}, f32[8,128]{1,0:T(8,128)S(1)}, u32[]{:S(2)}, u32[]{:S(2)}) collective-permute-start(f32[8,128]{1,0:T(8,128)S(1)} %add_add_fusion), channel_id=1, source_target_pairs={{0,0},{1,1},{64,2},{65,3},{128,4},{129,5},{192,6},{193,7},{2,8},{3... | collective-permute-start | bytes 12296 | tf_op jit(solution)/shard_map/ppermute | solution.py:509
  281.3 9.3 %collective-permute-done.22 = f32[8,128]{1,0:T(8,128)S(1)} collective-permute-done((f32[8,128]{1,0:T(8,128)S(1)}, f32[8,128]{1,0:T(8,128)S(1)}, u32[]{:S(2)}, u32[]{:S(2)}) %collective-permute-start.22) | collective-permute-done | bytes 4128 | tf_op jit(solution)/shard_map/ppermute | solution.py:509
  293.9 6.3 %all-to-all-start.5 = ((bf16[16,2,1152]{2,1,0:T(2,128)(2,1)}), bf16[16,2,1152]{2,1,0:T(2,128)(2,1)S(1)}, u32[]{:S(2)}, u32[]{:S(2)}) async-start(bf16[16,2,1152]{2,1,0:T(2,128)(2,1)} %all_to_all.35), calls=%async_computation.5 | async-start | bytes 147456 | tf_op jit(solution)/shard_map/all_to_all | solution.py:518
  300.2 8.5 %all-to-all-done.5 = bf16[16,2,1152]{2,1,0:T(2,128)(2,1)S(1)} async-done(((bf16[16,2,1152]{2,1,0:T(2,128)(2,1)}), bf16[16,2,1152]{2,1,0:T(2,128)(2,1)S(1)}, u32[]{:S(2)}, u32[]{:S(2)}) %all-to-all-start.5) | async-done | bytes 73760 | tf_op jit(solution)/shard_map/all_to_all | solution.py:518
  (103 shorter events, 37.5 us)
Async XLA Ops:
  2.2 27.8 %copy-start.4 = (bf16[1,128,1024]{2,1,0:T(8,128)(2,1)S(1)}, bf16[1,128,1024]{2,1,0:T(8,128)(2,1)}, u32[]{:S(2)}) copy-start(bf16[1,128,1024]{2,1,0:T(8,128)(2,1)} %param.13) | copy-start | bytes 786436
  4.3 61.2 %collective-permute-start.5 = (bf16[256,1408]{1,0:T(8,128)(2,1)}, bf16[256,1408]{1,0:T(8,128)(2,1)}, u32[]{:S(2)}, u32[]{:S(2)}) collective-permute-start(bf16[256,1408]{1,0:T(8,128)(2,1)} %shard_map.140.rest_0_), channel_id=1, source_target_pairs={{0,8},{8,16},{16,24},{24,32},{32,40},{40,48},{48,56},{56,0},{1,9},... | collective-permute-start | bytes 2162696 | tf_op jit(solution)/shard_map/ppermute | solution.py:461
  6.2 59.4 %collective-permute-start.6 = (bf16[256,1408]{1,0:T(8,128)(2,1)}, bf16[256,1408]{1,0:T(8,128)(2,1)}, u32[]{:S(2)}, u32[]{:S(2)}) collective-permute-start(bf16[256,1408]{1,0:T(8,128)(2,1)} %shard_map.140.rest_0_), channel_id=1, source_target_pairs={{0,56},{8,0},{16,8},{24,16},{32,24},{40,32},{48,40},{56,48},{1,57}... | collective-permute-start | bytes 2162696 | tf_op jit(solution)/shard_map/ppermute | solution.py:464
  30.9 37.9 %copy-start.2 = (bf16[128,1024]{1,0:T(8,128)(2,1)}, bf16[128,1024]{1,0:T(8,128)(2,1)S(1)}, u32[]{:S(2)}) copy-start(bf16[128,1024]{1,0:T(8,128)(2,1)S(1)} %scatter_custom_fusion) | copy-start | bytes 786436
  30.9 78.6 %copy-start.9 = (s32[1,128]{1,0:T(1,128)S(1)}, s32[1,128]{1,0:T(1,128)}, u32[]{:S(2)}) copy-start(s32[1,128]{1,0:T(1,128)} %param.17) | copy-start | bytes 1540
  31.0 29.2 %collective-permute-start = (bf16[128,1024]{1,0:T(8,128)(2,1)S(1)}, bf16[128,1024]{1,0:T(8,128)(2,1)S(1)}, u32[]{:S(2)}, u32[]{:S(2)}) collective-permute-start(bf16[128,1024]{1,0:T(8,128)(2,1)S(1)} %scatter_custom_fusion), channel_id=1, source_target_pairs={{0,0},{1,1},{2,64},{3,65},{4,128},{5,129},{6,192},{7,193},{8,2},{9... | collective-permute-start | bytes 786440 | tf_op jit(solution)/shard_map/ppermute | solution.py:475
  61.3 26.2 %all-to-all-start.1 = ((bf16[4,128,1024]{2,1,0:T(8,128)(2,1)}), bf16[4,128,1024]{2,1,0:T(8,128)(2,1)}, u32[]{:S(2)}, u32[]{:S(2)}) async-start(bf16[4,128,1024]{2,1,0:T(8,128)(2,1)} %broadcast_in_dim.27), calls=%async_computation.1 | async-start | bytes 2097152 | tf_op jit(solution)/shard_map/all_to_all | solution.py:435
  65.6 18.6 %collective-permute-start.7 = (bf16[256,1408]{1,0:T(8,128)(2,1)}, bf16[256,1408]{1,0:T(8,128)(2,1)}, u32[]{:S(2)}, u32[]{:S(2)}) collective-permute-start(bf16[256,1408]{1,0:T(8,128)(2,1)} %collective-permute-done.5.rest_1_), channel_id=1, source_target_pairs={{0,8},{8,16},{16,24},{24,32},{32,40},{40,48},{48,56},{56,0},{1,9},... | collective-permute-start | bytes 2162696 | tf_op jit(solution)/shard_map/ppermute | solution.py:461
  65.7 18.6 %collective-permute-start.8 = (bf16[256,1408]{1,0:T(8,128)(2,1)}, bf16[256,1408]{1,0:T(8,128)(2,1)}, u32[]{:S(2)}, u32[]{:S(2)}) collective-permute-start(bf16[256,1408]{1,0:T(8,128)(2,1)} %collective-permute-done.6.rest_2_), channel_id=1, source_target_pairs={{0,56},{8,0},{16,8},{24,16},{32,24},{40,32},{48,40},{56,48},{1,57}... | collective-permute-start | bytes 2162696 | tf_op jit(solution)/shard_map/ppermute | solution.py:464
  84.2 17.6 %collective-permute-start.9 = (bf16[256,1408]{1,0:T(8,128)(2,1)}, bf16[256,1408]{1,0:T(8,128)(2,1)S(1)}, u32[]{:S(2)}, u32[]{:S(2)}) collective-permute-start(bf16[256,1408]{1,0:T(8,128)(2,1)} %collective-permute-done.7.rest_3_), channel_id=1, source_target_pairs={{0,8},{8,16},{16,24},{24,32},{32,40},{40,48},{48,56},{56,0},{1,9},... | collective-permute-start | bytes 2162696 | tf_op jit(solution)/shard_map/ppermute | solution.py:461
  84.2 18.5 %collective-permute-start.10 = (bf16[256,1408]{1,0:T(8,128)(2,1)}, bf16[256,1408]{1,0:T(8,128)(2,1)}, u32[]{:S(2)}, u32[]{:S(2)}) collective-permute-start(bf16[256,1408]{1,0:T(8,128)(2,1)} %collective-permute-done.8.rest_4_), channel_id=1, source_target_pairs={{0,56},{8,0},{16,8},{24,16},{32,24},{40,32},{48,40},{56,48},{1,57}... | collective-permute-start | bytes 2162696 | tf_op jit(solution)/shard_map/ppermute | solution.py:464
  87.5 40.1 %collective-permute-start.1 = (bf16[4,128,1024]{2,1,0:T(8,128)(2,1)}, bf16[4,128,1024]{2,1,0:T(8,128)(2,1)}, u32[]{:S(2)}, u32[]{:S(2)}) collective-permute-start(bf16[4,128,1024]{2,1,0:T(8,128)(2,1)} %all-to-all-done.1.own), channel_id=1, source_target_pairs={{0,1},{1,0},{2,3},{3,2},{4,5},{5,4},{6,7},{7,6},{8,9},{9,8},{10,11... | collective-permute-start | bytes 3145736 | tf_op jit(solution)/shard_map/ppermute | solution.py:480
  102.7 24.9 %collective-permute-start.11 = (bf16[128,1408]{1,0:T(8,128)(2,1)}, bf16[128,1408]{1,0:T(8,128)(2,1)}, u32[]{:S(2)}, u32[]{:S(2)}) collective-permute-start(bf16[128,1408]{1,0:T(8,128)(2,1)} %slice.60), channel_id=1, source_target_pairs={{0,8},{8,16},{16,24},{24,32},{32,40},{40,48},{48,56},{56,0},{1,9},... | collective-permute-start | bytes 1081352 | tf_op jit(solution)/shard_map/ppermute | solution.py:461
  104.4 23.1 %collective-permute-start.12 = (bf16[128,1408]{1,0:T(8,128)(2,1)}, bf16[128,1408]{1,0:T(8,128)(2,1)}, u32[]{:S(2)}, u32[]{:S(2)}) collective-permute-start(bf16[128,1408]{1,0:T(8,128)(2,1)} %slice.61), channel_id=1, source_target_pairs={{0,56},{8,0},{16,8},{24,16},{32,24},{40,32},{48,40},{56,48},{1,57}... | collective-permute-start | bytes 1081352 | tf_op jit(solution)/shard_map/ppermute | solution.py:464
  107.7 19.8 %collective-permute-start.2 = (bf16[128,1024]{1,0:T(8,128)(2,1)}, bf16[128,1024]{1,0:T(8,128)(2,1)}, u32[]{:S(2)}, u32[]{:S(2)}) collective-permute-start(bf16[128,1024]{1,0:T(8,128)(2,1)} %bitcast.34), channel_id=1, source_target_pairs={{0,0},{8,64},{16,128},{24,192},{32,32},{40,96},{48,160},{56,224},{... | collective-permute-start | bytes 786440 | tf_op jit(solution)/shard_map/ppermute | solution.py:468
  110.2 7.7 %collective-permute-start.3 = (s32[1]{0:T(128)}, s32[1]{0:T(128)}, u32[]{:S(2)}, u32[]{:S(2)}) collective-permute-start(s32[1]{0:T(128)} %bitcast.9), channel_id=1, source_target_pairs={{0,8},{8,16},{16,24},{24,32},{32,40},{40,48},{48,56},{56,64},{64,7... | collective-permute-start | bytes 20 | tf_op jit(solution)/shard_map/ppermute | solution.py:456
  118.6 8.9 %collective-permute-start.4 = (f32[8,128]{1,0:T(8,128)S(1)}, f32[8,128]{1,0:T(8,128)S(1)}, u32[]{:S(2)}, u32[]{:S(2)}) collective-permute-start(f32[8,128]{1,0:T(8,128)S(1)} %pad_convert_fusion), channel_id=1, source_target_pairs={{0,0},{8,64},{16,128},{24,192},{32,32},{40,96},{48,160},{56,224},{... | collective-permute-start | bytes 12296 | tf_op jit(solution)/shard_map/ppermute | solution.py:458
  137.4 33.8 %all-to-all-start.2 = ((bf16[4,592,512]{2,1,0:T(8,128)(2,1)}), bf16[4,592,512]{2,1,0:T(8,128)(2,1)}, u32[]{:S(2)}, u32[]{:S(2)}) async-start(bf16[4,592,512]{2,1,0:T(8,128)(2,1)} %get-tuple-element.17), calls=%async_computation.2 | async-start | bytes 4849664 | tf_op jit(solution)/shard_map/all_to_all | solution.py:492
  145.6 39.4 %copy-start.12 = (f32[16]{0:T(128)S(1)}, f32[16]{0:T(128)}, u32[]{:S(2)}) copy-start(f32[16]{0:T(128)} %param.24) | copy-start | bytes 196
  179.0 11.5 %collective-permute-start.13 = (bf16[272,128]{1,0:T(8,128)(2,1)S(1)}, bf16[272,128]{1,0:T(8,128)(2,1)S(1)}, u32[]{:S(2)}, u32[]{:S(2)}) collective-permute-start(bf16[272,128]{1,0:T(8,128)(2,1)S(1)} %get-tuple-element.38), channel_id=1, source_target_pairs={{0,32},{8,40},{16,48},{24,56},{32,16},{40,24},{48,0},{56,8},{1,33}... | collective-permute-start | bytes 208904 | tf_op jit(solution)/shard_map/ppermute | solution.py:494
  182.0 8.5 %collective-permute-start.14 = (bf16[272,128]{1,0:T(8,128)(2,1)S(1)}, bf16[272,128]{1,0:T(8,128)(2,1)S(1)}, u32[]{:S(2)}, u32[]{:S(2)}) collective-permute-start(bf16[272,128]{1,0:T(8,128)(2,1)S(1)} %get-tuple-element.37), channel_id=1, source_target_pairs={{0,16},{8,24},{16,0},{24,8},{32,48},{40,56},{48,32},{56,40},{1,17}... | collective-permute-start | bytes 208904 | tf_op jit(solution)/shard_map/ppermute | solution.py:494
  183.0 9.0 %collective-permute-start.15 = (bf16[272,128]{1,0:T(8,128)(2,1)S(1)}, bf16[272,128]{1,0:T(8,128)(2,1)S(1)}, u32[]{:S(2)}, u32[]{:S(2)}) collective-permute-start(bf16[272,128]{1,0:T(8,128)(2,1)S(1)} %get-tuple-element.36), channel_id=1, source_target_pairs={{0,48},{8,56},{16,32},{24,40},{32,0},{40,8},{48,16},{56,24},{1,49}... | collective-permute-start | bytes 208904 | tf_op jit(solution)/shard_map/ppermute | solution.py:494
  234.3 6.2 %collective-permute-start.16 = (bf16[4,128,1024]{2,1,0:T(8,128)(2,1)}, bf16[4,128,1024]{2,1,0:T(8,128)(2,1)}, u32[]{:S(2)}, u32[]{:S(2)}) collective-permute-start(bf16[4,128,1024]{2,1,0:T(8,128)(2,1)} %get-tuple-element.31), channel_id=1, source_target_pairs={{0,1},{1,0},{2,3},{3,2},{4,5},{5,4},{6,7},{7,6},{8,9},{9,8},{10,11... | collective-permute-start | bytes 3145736 | tf_op jit(solution)/shard_map/ppermute | solution.py:499
  242.5 30.5 %copy-start.13 = (s32[1,128]{1,0:T(1,128)S(1)}, s32[1,128]{1,0:T(1,128)}, u32[]{:S(2)}) copy-start(s32[1,128]{1,0:T(1,128)} %param.18) | copy-start | bytes 1540
  264.0 47.4 %copy-start.3 = (bf16[128,1024]{1,0:T(8,128)(2,1)S(1)}, bf16[128,1024]{1,0:T(8,128)(2,1)}, u32[]{:S(2)}) copy-start(bf16[128,1024]{1,0:T(8,128)(2,1)} %copy-done.2) | copy-start | bytes 786436
  265.6 1.5 collective-permute-start.18
  267.8 8.4 %collective-permute-start.19 = (f32[8,128]{1,0:T(8,128)S(1)}, f32[8,128]{1,0:T(8,128)S(1)}, u32[]{:S(2)}, u32[]{:S(2)}) collective-permute-start(f32[8,128]{1,0:T(8,128)S(1)} %broadcast_add_fusion), channel_id=1, source_target_pairs={{0,64},{64,128},{128,192},{192,0},{1,65},{65,129},{129,193},{193,1... | collective-permute-start | bytes 12296 | tf_op jit(solution)/shard_map/ppermute | solution.py:439
  269.5 6.7 %collective-permute-start.20 = (f32[8,128]{1,0:T(8,128)S(1)}, f32[8,128]{1,0:T(8,128)S(1)}, u32[]{:S(2)}, u32[]{:S(2)}) collective-permute-start(f32[8,128]{1,0:T(8,128)S(1)} %broadcast_add_fusion), channel_id=1, source_target_pairs={{0,128},{64,192},{128,0},{192,64},{1,129},{65,193},{129,1},{193,65... | collective-permute-start | bytes 12296 | tf_op jit(solution)/shard_map/ppermute | solution.py:439
  270.9 5.3 %collective-permute-start.21 = (f32[8,128]{1,0:T(8,128)S(1)}, f32[8,128]{1,0:T(8,128)S(1)}, u32[]{:S(2)}, u32[]{:S(2)}) collective-permute-start(f32[8,128]{1,0:T(8,128)S(1)} %broadcast_add_fusion), channel_id=1, source_target_pairs={{0,192},{64,0},{128,64},{192,128},{1,193},{65,1},{129,65},{193,129... | collective-permute-start | bytes 12296 | tf_op jit(solution)/shard_map/ppermute | solution.py:439
  273.0 19.5 %collective-permute-start.17 = (bf16[128,1024]{1,0:T(8,128)(2,1)S(1)}, bf16[128,1024]{1,0:T(8,128)(2,1)S(1)}, u32[]{:S(2)}, u32[]{:S(2)}) collective-permute-start(bf16[128,1024]{1,0:T(8,128)(2,1)S(1)} %get-tuple-element.35), channel_id=1, source_target_pairs={{0,0},{1,1},{64,2},{65,3},{128,4},{129,5},{192,6},{193,7},{2,8},{3... | collective-permute-start | bytes 786440 | tf_op jit(solution)/shard_map/ppermute | solution.py:506
  276.9 13.8 %collective-permute-start.22 = (f32[8,128]{1,0:T(8,128)S(1)}, f32[8,128]{1,0:T(8,128)S(1)}, u32[]{:S(2)}, u32[]{:S(2)}) collective-permute-start(f32[8,128]{1,0:T(8,128)S(1)} %add_add_fusion), channel_id=1, source_target_pairs={{0,0},{1,1},{64,2},{65,3},{128,4},{129,5},{192,6},{193,7},{2,8},{3... | collective-permute-start | bytes 12296 | tf_op jit(solution)/shard_map/ppermute | solution.py:509
  293.9 14.8 %all-to-all-start.5 = ((bf16[16,2,1152]{2,1,0:T(2,128)(2,1)}), bf16[16,2,1152]{2,1,0:T(2,128)(2,1)S(1)}, u32[]{:S(2)}, u32[]{:S(2)}) async-start(bf16[16,2,1152]{2,1,0:T(2,128)(2,1)} %all_to_all.35), calls=%async_computation.5 | async-start | bytes 147456 | tf_op jit(solution)/shard_map/all_to_all | solution.py:518
  (8 other events, 56.7 us)

commit v5 on v4

--- a/solution.py
+++ b/solution.py
@@ -174,7 +174,7 @@
     )(meta, own, oth, probe, ids, *blocks)
 
 
-def prepare_kernel(meta, r, prm, pay, x, bc, rows_out, cols_out, t_out, q_out, p):
+def prepare_kernel(meta, r, prm, pay1, pay2, pay3, x, bc, rows_out, cols_out, t_out, q_out, p):
     total = r[0, 0:512, :].astype(F32)
     raw = r[0, 512:528, :].astype(F32)
     for d in range(1, 4):
@@ -214,17 +214,20 @@
         grad = by_head_rows(lanes(through[3 - k])) * grad + q_out[3 - k]
         whole = whole * through[k]
     for k in range(1, 4):
-        pay[k - 1, 0:256, :] = jnp.where(meta[2] + k < 4, state, grad).astype(BF16)
-        pay[k - 1, 256:272, :] = jnp.broadcast_to(whole, (16, 128)).astype(BF16)
+        pay = (pay1, pay2, pay3)[k - 1]
+        pay[0:256, :] = jnp.where(meta[2] + k < 4, state, grad).astype(BF16)
+        pay[256:272, :] = jnp.broadcast_to(whole, (16, 128)).astype(BF16)
 
 
 def prepare(meta, r, prm):
     return pl.pallas_call(
         prepare_kernel,
         in_specs=[SMEM, VMEM, VMEM],
-        out_specs=[VMEM] * 8,
+        out_specs=[VMEM] * 10,
         out_shape=[
-            jax.ShapeDtypeStruct((3, 272, 128), BF16),
+            jax.ShapeDtypeStruct((272, 128), BF16),
+            jax.ShapeDtypeStruct((272, 128), BF16),
+            jax.ShapeDtypeStruct((272, 128), BF16),
             jax.ShapeDtypeStruct((512, 256), F32),
             jax.ShapeDtypeStruct((512, 256), BF16),
             jax.ShapeDtypeStruct((4, 16, 128), F32),
@@ -294,7 +297,8 @@
     )(x, bc, p, rows, cols, skip)
 
 
-def finish_kernel(meta, r1, r2, r3, x, bc, p, rows_in, cols_in, t_in, q_in, dx, dbc, e, prm, out):
+def finish_kernel(meta, r1, r2, r3, x, bc, p, rows_in, cols_in, t_in, q_in, dx, dbc, e, prm, copies):
+    out = copies.at[0]
     quarter = meta[2]
     got = (r1, r2, r3)
     parts = [ref[0:256, :].astype(F32) for ref in got]
@@ -359,6 +363,8 @@
         z = rows[8:16]
         d_z = jnp.where(sub < 4, d_dt / (1.0 + jnp.exp(-z)), 0.0)
         out[512:528, here] = jnp.concatenate([d_z, jnp.zeros((8, 128), F32)], axis=0).astype(BF16)
+    for d in range(1, 4):
+        copies[d] = copies[0]
 
 
 def finish(meta, *args):
@@ -366,7 +372,7 @@
         finish_kernel,
         in_specs=[SMEM] + [VMEM] * len(args),
         out_specs=VMEM,
-        out_shape=jax.ShapeDtypeStruct((528, 512), BF16),
+        out_shape=jax.ShapeDtypeStruct((4, 528, 512), BF16),
     )(meta, *args)
 
 
@@ -490,11 +496,11 @@
     blocks = (w_ring, r1, l1, r2, l2, r3, l3, r4, l4)
     partial_proj, weights = project(meta, own, oth, probe_moved, ids, blocks)
     received = lax.all_to_all(partial_proj, X, split_axis=0, concat_axis=0)
-    pay, values, bc, rows, cols, t_all, q_all, probes = prepare(meta, received, prm)
+    *pay, values, bc, rows, cols, t_all, q_all, probes = prepare(meta, received, prm)
     got = [lax.ppermute(pay[k - 1], "z", quarter_route(k)) for k in (1, 2, 3)]
     dx, dbc, e = intra(values, bc, probes, rows, cols, skip)
     grads = finish(meta, *got, values, bc, probes, rows, cols, t_all, q_all, dx, dbc, e, prm)
-    everyone = to_all(grads, X)
+    everyone = lax.all_to_all(grads, X, split_axis=0, concat_axis=0)
     full, oth_part = pull_first(meta, everyone, weights)
     swapped = lax.ppermute(oth_part, "core", SWAP)
     own_part = pull_second(meta, full, weights)

time: 314 us -> 313 us (level)
  transfers between devices with their start and end apart: 26 -> 26, of which waited for: 10 -> 10; matrix products, arithmetic and copies ran while one was open for 3% -> 4% of each run, Pallas kernels for 3% -> 3%
where the time goes in v5:
time: 313 us; the launch traced here: 312 us
  waiting for transfers between devices  110 us (35%)
  blocking collectives  68.1 us (22%)
  starting transfers between devices  65.9 us (21%)
  Pallas kernels  42.1 us (13%)
  local copies, waits for them, and re-layouts  12.3 us (4%)
  other arithmetic  8.56 us (3%)
  between operations  3.76 us (1%)
    ppermute x4, waiting for transfers between devices, right(): return lax.ppermute(v, 'z', [(i, (i + 1) % 8) for i in range(8)])  29.7 us
    all_to_all x1, blocking collectives, body(): everyone = lax.all_to_all(grads, X, split_axis=0, concat_axis=0)  28.7 us
    all_to_all x1, waiting for transfers between devices, body(): received = lax.all_to_all(partial_proj, X, split_axis=0, concat_axis=0)  25.1 us
    all_to_all x1, blocking collectives, body(): pieces = lax.all_to_all(both, 'y', split_axis=0, concat_axis=0)  22 us
    ppermute x1, waiting for transfers between devices, body(): moved = lax.ppermute(merged, AXES, features_route())  21 us
    all_to_all x1, blocking collectives, body(): lax.all_to_all(tagged, SEQ, split_axis=0, concat_axis=0, tiled=True)  17.4 us
    ppermute x4, starting transfers between devices, left(): return lax.ppermute(v, 'z', [(i, (i + 7) % 8) for i in range(8)])  13.6 us
    ppermute x1, waiting for transfers between devices, body(): squares = lax.ppermute(squares, AXES, back)[0, 0]  11.1 us
  transfers between devices with their start and end apart: 26, of which 10 were waited for; matrix products, arithmetic and copies ran while one was open for 4% of the time, Pallas kernels for 3%

profile of v5, /device:TPU:4, one launch (start us, length us, event | category | flops | bytes accessed | tf_op | source)
XLA Modules:
  0.0 312.0 jit_solution(6430092215267321067)
XLA Ops:
  2.2 2.1 shard_map.140.rest_0_
  6.2 3.9 %collective-permute-start.6 = (bf16[256,1408]{1,0:T(8,128)(2,1)}, bf16[256,1408]{1,0:T(8,128)(2,1)}, u32[]{:S(2)}, u32[]{:S(2)}) collective-permute-start(bf16[256,1408]{1,0:T(8,128)(2,1)} %shard_map.140.rest_0_), channel_id=1, source_target_pairs={{0,56},{8,0},{16,8},{24,16},{32,24},{40,32},{48,40},{56,48},{1,57}... | collective-permute-start | bytes 2162696 | tf_op jit(solution)/shard_map/ppermute | solution.py:470
  12.4 17.4 %all_to_all.46 = bf16[16,2,1152]{2,1,0:T(2,128)(2,1)S(1)} all-to-all(bf16[16,2,1152]{2,1,0:T(2,128)(2,1)S(1)} %all_to_all.28), channel_id=1, replica_groups=mesh['x_hi'=2,'x_lo'=2,'z'=8,'y'=4,'core'=2] {'x_lo','z'}, dimensions={0} | all-to-all | bytes 147456 | tf_op jit(solution)/shard_map/all_to_all | solution.py:478
  30.9 8.2 %collective-permute-start = (bf16[128,1024]{1,0:T(8,128)(2,1)S(1)}, bf16[128,1024]{1,0:T(8,128)(2,1)S(1)}, u32[]{:S(2)}, u32[]{:S(2)}) collective-permute-start(bf16[128,1024]{1,0:T(8,128)(2,1)S(1)} %scatter_custom_fusion), channel_id=1, source_target_pairs={{0,0},{1,1},{2,64},{3,65},{4,128},{5,129},{6,192},{7,193},{8,2},{9... | collective-permute-start | bytes 786440 | tf_op jit(solution)/shard_map/ppermute | solution.py:481
  39.2 21.0 %collective-permute-done = bf16[128,1024]{1,0:T(8,128)(2,1)S(1)} collective-permute-done((bf16[128,1024]{1,0:T(8,128)(2,1)S(1)}, bf16[128,1024]{1,0:T(8,128)(2,1)S(1)}, u32[]{:S(2)}, u32[]{:S(2)}) %collective-permute-start) | collective-permute-done | bytes 262176 | tf_op jit(solution)/shard_map/ppermute | solution.py:481
  61.3 4.2 %all-to-all-start.1 = ((bf16[4,128,1024]{2,1,0:T(8,128)(2,1)}), bf16[4,128,1024]{2,1,0:T(8,128)(2,1)}, u32[]{:S(2)}, u32[]{:S(2)}) async-start(bf16[4,128,1024]{2,1,0:T(8,128)(2,1)} %broadcast_in_dim.27), calls=%async_computation.1 | async-start | bytes 2097152 | tf_op jit(solution)/shard_map/all_to_all | solution.py:441
  65.6 3.2 %collective-permute-start.8 = (bf16[256,1408]{1,0:T(8,128)(2,1)}, bf16[256,1408]{1,0:T(8,128)(2,1)}, u32[]{:S(2)}, u32[]{:S(2)}) collective-permute-start(bf16[256,1408]{1,0:T(8,128)(2,1)} %collective-permute-done.6.rest_2_), channel_id=1, source_target_pairs={{0,56},{8,0},{16,8},{24,16},{32,24},{40,32},{48,40},{56,48},{1,57}... | collective-permute-start | bytes 2162696 | tf_op jit(solution)/shard_map/ppermute | solution.py:470
  68.9 15.3 %collective-permute-done.7.rest_3_ = bf16[256,1408]{1,0:T(8,128)(2,1)} collective-permute-done((bf16[256,1408]{1,0:T(8,128)(2,1)}, bf16[256,1408]{1,0:T(8,128)(2,1)}, u32[]{:S(2)}, u32[]{:S(2)}) %collective-permute-start.7) | collective-permute-done | bytes 720928 | tf_op jit(solution)/shard_map/ppermute | solution.py:467
  84.2 3.2 %collective-permute-start.10 = (bf16[256,1408]{1,0:T(8,128)(2,1)}, bf16[256,1408]{1,0:T(8,128)(2,1)}, u32[]{:S(2)}, u32[]{:S(2)}) collective-permute-start(bf16[256,1408]{1,0:T(8,128)(2,1)} %collective-permute-done.8.rest_4_), channel_id=1, source_target_pairs={{0,56},{8,0},{16,8},{24,16},{32,24},{40,32},{48,40},{56,48},{1,57}... | collective-permute-start | bytes 2162696 | tf_op jit(solution)/shard_map/ppermute | solution.py:470
  87.4 14.4 %collective-permute-done.9.rest_5_ = bf16[256,1408]{1,0:T(8,128)(2,1)S(1)} collective-permute-done((bf16[256,1408]{1,0:T(8,128)(2,1)}, bf16[256,1408]{1,0:T(8,128)(2,1)S(1)}, u32[]{:S(2)}, u32[]{:S(2)}) %collective-permute-start.9) | collective-permute-done | bytes 720928 | tf_op jit(solution)/shard_map/ppermute | solution.py:467
  104.4 3.2 %collective-permute-start.12 = (bf16[128,1408]{1,0:T(8,128)(2,1)}, bf16[128,1408]{1,0:T(8,128)(2,1)}, u32[]{:S(2)}, u32[]{:S(2)}) collective-permute-start(bf16[128,1408]{1,0:T(8,128)(2,1)} %slice.49), channel_id=1, source_target_pairs={{0,56},{8,0},{16,8},{24,16},{32,24},{40,32},{48,40},{56,48},{1,57}... | collective-permute-start | bytes 1081352 | tf_op jit(solution)/shard_map/ppermute | solution.py:470
  112.1 5.8 %collective-permute-done.3 = s32[1]{0:T(128)} collective-permute-done((s32[1]{0:T(128)}, s32[1]{0:T(128)}, u32[]{:S(2)}, u32[]{:S(2)}) %collective-permute-start.3) | collective-permute-done | bytes 36 | tf_op jit(solution)/shard_map/ppermute | solution.py:462
  121.1 6.3 %collective-permute-done.4.ids_in = f32[8,128]{1,0:T(8,128)S(1)} collective-permute-done((f32[8,128]{1,0:T(8,128)S(1)}, f32[8,128]{1,0:T(8,128)S(1)}, u32[]{:S(2)}, u32[]{:S(2)}) %collective-permute-start.4) | collective-permute-done | bytes 4128 | tf_op jit(solution)/shard_map/ppermute | solution.py:464
  128.0 9.2 %shard_map.141 = (bf16[4,592,512]{2,1,0:T(8,128)(2,1)}, bf16[2048,1408]{1,0:T(8,128)(2,1)}) custom-call(s32[4]{0:T(128)} %pad_add_fusion.meta, bf16[4,128,1024]{2,1,0:T(8,128)(2,1)} %all-to-all-done.1.own, bf16[4,128,1024]{2,1,0:T(8,128)(2,1)} %collective-permute-done.1.oth, bf16[128,1024]{1,0:T(8,128)(2,1)} %collective-permute-done.2.probe, ...), custom_call_target="tpu_custom_call" | custom-call | tf_op jit(solution)/shard_map/pallas_call | solution.py:163
  137.3 8.4 %all-to-all-start.2 = ((bf16[4,592,512]{2,1,0:T(8,128)(2,1)}), bf16[4,592,512]{2,1,0:T(8,128)(2,1)}, u32[]{:S(2)}, u32[]{:S(2)}) async-start(bf16[4,592,512]{2,1,0:T(8,128)(2,1)} %get-tuple-element.19), calls=%async_computation.2 | async-start | bytes 4849664 | tf_op jit(solution)/shard_map/all_to_all | solution.py:498
  145.8 25.1 %all-to-all-done.2.r = bf16[4,592,512]{2,1,0:T(8,128)(2,1)} async-done(((bf16[4,592,512]{2,1,0:T(8,128)(2,1)}), bf16[4,592,512]{2,1,0:T(8,128)(2,1)}, u32[]{:S(2)}, u32[]{:S(2)}) %all-to-all-start.2) | async-done | bytes 2424864 | tf_op jit(solution)/shard_map/all_to_all | solution.py:498
  171.6 6.1 %shard_map.142 = (bf16[272,128]{1,0:T(8,128)(2,1)}, bf16[272,128]{1,0:T(8,128)(2,1)}, bf16[272,128]{1,0:T(8,128)(2,1)}, f32[512,256]{1,0:T(8,128)}, bf16[512,256...) custom-call(s32[4]{0:T(128)} %pad_add_fusion.meta, ...), custom_call_target="tpu_custom_call" | custom-call | tf_op jit(solution)/shard_map/pallas_call | solution.py:223
  177.7 3.2 %collective-permute-start.13 = (bf16[272,128]{1,0:T(8,128)(2,1)}, bf16[272,128]{1,0:T(8,128)(2,1)S(1)}, u32[]{:S(2)}, u32[]{:S(2)}) collective-permute-start(bf16[272,128]{1,0:T(8,128)(2,1)} %get-tuple-element.20), channel_id=1, source_target_pairs={{0,32},{8,40},{16,48},{24,56},{32,16},{40,24},{48,0},{56,8},{1,33}... | collective-permute-start | bytes 208904 | tf_op jit(solution)/shard_map/ppermute | solution.py:500
  181.9 2.0 collective-permute-start.15
  184.8 4.6 %shard_map.143 = (f32[512,256]{1,0:T(8,128)}, f32[512,256]{1,0:T(8,128)}, f32[4,16,128]{2,1,0:T(8,128)}) custom-call(f32[512,256]{1,0:T(8,128)} %get-tuple-element.23.x, bf16[512,256]{1,0:T(8,128)(2,1)} %get-tuple-element.24.bc, bf16[4,128,256]{2,1,0:T(8,128)(2,1)} %get-tuple-element.25.p, f32[4,16,128]{2,1,0:T(8,128)} %get-tuple-element.26.rows_in, ...), custom_call_target="tpu_custom_call" | custom-call | tf_op jit(solution)/shard_map/pallas_call | solution.py:287
  191.1 7.6 %shard_map.144 = bf16[4,528,512]{2,1,0:T(8,128)(2,1)} custom-call(s32[4]{0:T(128)} %pad_add_fusion.meta, bf16[272,128]{1,0:T(8,128)(2,1)} %copy-done.5, bf16[272,128]{1,0:T(8,128)(2,1)} %copy-done.6, bf16[272,128]{1,0:T(8,128)(2,1)} %copy-done.7, f32[512,256]{1,0:T(8,128)} %get-tuple-element.23.x, bf16[512,256]{1,0:T(8,128)(2,1)} %get-tuple-element.24.bc, ...), custom_call_target="tpu_custom_call" | custom-call | tf_op jit(solution)/shard_map/pallas_call | solution.py:371
  198.7 28.7 %all_to_all.44.g = bf16[4,528,512]{2,1,0:T(8,128)(2,1)} all-to-all(bf16[4,528,512]{2,1,0:T(8,128)(2,1)} %shard_map.144), channel_id=1, replica_groups=mesh['x_hi'=2,'x_lo'=2,'z'=8,'y'=4,'core'=2] {'x_hi','x_lo'}, dimensions={0} | all-to-all | bytes 4325376 | tf_op jit(solution)/shard_map/all_to_all | solution.py:503
  227.4 6.3 %shard_map.145 = (bf16[1408,512]{1,0:T(8,128)(2,1)}, bf16[4,128,1024]{2,1,0:T(8,128)(2,1)}) custom-call(s32[4]{0:T(128)} %pad_add_fusion.meta, bf16[4,528,512]{2,1,0:T(8,128)(2,1)} %all_to_all.44.g, bf16[2048,1408]{1,0:T(8,128)(2,1)} %get-tuple-element.33.w), custom_call_target="tpu_custom_call" | custom-call | tf_op jit(solution)/shard_map/pallas_call | solution.py:421
  233.8 6.2 %shard_map.146 = bf16[4,128,1024]{2,1,0:T(8,128)(2,1)} custom-call(s32[4]{0:T(128)} %pad_add_fusion.meta, bf16[1408,512]{1,0:T(8,128)(2,1)} %get-tuple-element.34.full, bf16[2048,1408]{1,0:T(8,128)(2,1)} %get-tuple-element.33.w), custom_call_target="tpu_custom_call" | custom-call | tf_op jit(solution)/shard_map/pallas_call | solution.py:431
  240.0 1.9 add_convert_fusion
  242.0 22.0 %all_to_all.45 = bf16[4,128,1024]{2,1,0:T(8,128)(2,1)S(1)} all-to-all(bf16[4,128,1024]{2,1,0:T(8,128)(2,1)S(1)} %add_convert_fusion), channel_id=1, replica_groups=mesh['x_hi'=2,'x_lo'=2,'z'=8,'y'=4,'core'=2] {'y'}, dimensions={0} | all-to-all | bytes 2097152 | tf_op jit(solution)/shard_map/all_to_all | solution.py:508
  270.8 2.1 collective-permute-start.21
  272.9 3.1 %collective-permute-start.17 = (bf16[128,1024]{1,0:T(8,128)(2,1)S(1)}, bf16[128,1024]{1,0:T(8,128)(2,1)S(1)}, u32[]{:S(2)}, u32[]{:S(2)}) collective-permute-start(bf16[128,1024]{1,0:T(8,128)(2,1)S(1)} %get-tuple-element.39), channel_id=1, source_target_pairs={{0,0},{1,1},{64,2},{65,3},{128,4},{129,5},{192,6},{193,7},{2,8},{3... | collective-permute-start | bytes 786440 | tf_op jit(solution)/shard_map/ppermute | solution.py:512
  276.8 2.6 collective-permute-start.22
  279.4 11.1 %collective-permute-done.22 = f32[8,128]{1,0:T(8,128)S(1)} collective-permute-done((f32[8,128]{1,0:T(8,128)S(1)}, f32[8,128]{1,0:T(8,128)S(1)}, u32[]{:S(2)}, u32[]{:S(2)}) %collective-permute-start.22) | collective-permute-done | bytes 4128 | tf_op jit(solution)/shard_map/ppermute | solution.py:515
  293.8 6.0 %all-to-all-start.5 = ((bf16[16,2,1152]{2,1,0:T(2,128)(2,1)}), bf16[16,2,1152]{2,1,0:T(2,128)(2,1)S(1)}, u32[]{:S(2)}, u32[]{:S(2)}) async-start(bf16[16,2,1152]{2,1,0:T(2,128)(2,1)} %all_to_all.35), calls=%async_computation.5 | async-start | bytes 147456 | tf_op jit(solution)/shard_map/all_to_all | solution.py:524
  299.9 8.5 %all-to-all-done.5 = bf16[16,2,1152]{2,1,0:T(2,128)(2,1)S(1)} async-done(((bf16[16,2,1152]{2,1,0:T(2,128)(2,1)}), bf16[16,2,1152]{2,1,0:T(2,128)(2,1)S(1)}, u32[]{:S(2)}, u32[]{:S(2)}) %all-to-all-start.5) | async-done | bytes 73760 | tf_op jit(solution)/shard_map/all_to_all | solution.py:524
  (101 shorter events, 34.9 us)
Async XLA Ops:
  2.2 27.8 %copy-start.4 = (bf16[1,128,1024]{2,1,0:T(8,128)(2,1)S(1)}, bf16[1,128,1024]{2,1,0:T(8,128)(2,1)}, u32[]{:S(2)}) copy-start(bf16[1,128,1024]{2,1,0:T(8,128)(2,1)} %param.13) | copy-start | bytes 786436
  4.3 61.2 %collective-permute-start.5 = (bf16[256,1408]{1,0:T(8,128)(2,1)}, bf16[256,1408]{1,0:T(8,128)(2,1)}, u32[]{:S(2)}, u32[]{:S(2)}) collective-permute-start(bf16[256,1408]{1,0:T(8,128)(2,1)} %shard_map.140.rest_0_), channel_id=1, source_target_pairs={{0,8},{8,16},{16,24},{24,32},{32,40},{40,48},{48,56},{56,0},{1,9},... | collective-permute-start | bytes 2162696 | tf_op jit(solution)/shard_map/ppermute | solution.py:467
  6.2 59.4 %collective-permute-start.6 = (bf16[256,1408]{1,0:T(8,128)(2,1)}, bf16[256,1408]{1,0:T(8,128)(2,1)}, u32[]{:S(2)}, u32[]{:S(2)}) collective-permute-start(bf16[256,1408]{1,0:T(8,128)(2,1)} %shard_map.140.rest_0_), channel_id=1, source_target_pairs={{0,56},{8,0},{16,8},{24,16},{32,24},{40,32},{48,40},{56,48},{1,57}... | collective-permute-start | bytes 2162696 | tf_op jit(solution)/shard_map/ppermute | solution.py:470
  30.9 37.9 %copy-start.2 = (bf16[128,1024]{1,0:T(8,128)(2,1)}, bf16[128,1024]{1,0:T(8,128)(2,1)S(1)}, u32[]{:S(2)}) copy-start(bf16[128,1024]{1,0:T(8,128)(2,1)S(1)} %scatter_custom_fusion) | copy-start | bytes 786436
  30.9 78.6 %copy-start.9 = (s32[1,128]{1,0:T(1,128)S(1)}, s32[1,128]{1,0:T(1,128)}, u32[]{:S(2)}) copy-start(s32[1,128]{1,0:T(1,128)} %param.17) | copy-start | bytes 1540
  30.9 29.2 %collective-permute-start = (bf16[128,1024]{1,0:T(8,128)(2,1)S(1)}, bf16[128,1024]{1,0:T(8,128)(2,1)S(1)}, u32[]{:S(2)}, u32[]{:S(2)}) collective-permute-start(bf16[128,1024]{1,0:T(8,128)(2,1)S(1)} %scatter_custom_fusion), channel_id=1, source_target_pairs={{0,0},{1,1},{2,64},{3,65},{4,128},{5,129},{6,192},{7,193},{8,2},{9... | collective-permute-start | bytes 786440 | tf_op jit(solution)/shard_map/ppermute | solution.py:481
  61.3 26.2 %all-to-all-start.1 = ((bf16[4,128,1024]{2,1,0:T(8,128)(2,1)}), bf16[4,128,1024]{2,1,0:T(8,128)(2,1)}, u32[]{:S(2)}, u32[]{:S(2)}) async-start(bf16[4,128,1024]{2,1,0:T(8,128)(2,1)} %broadcast_in_dim.27), calls=%async_computation.1 | async-start | bytes 2097152 | tf_op jit(solution)/shard_map/all_to_all | solution.py:441
  65.5 18.6 %collective-permute-start.7 = (bf16[256,1408]{1,0:T(8,128)(2,1)}, bf16[256,1408]{1,0:T(8,128)(2,1)}, u32[]{:S(2)}, u32[]{:S(2)}) collective-permute-start(bf16[256,1408]{1,0:T(8,128)(2,1)} %collective-permute-done.5.rest_1_), channel_id=1, source_target_pairs={{0,8},{8,16},{16,24},{24,32},{32,40},{40,48},{48,56},{56,0},{1,9},... | collective-permute-start | bytes 2162696 | tf_op jit(solution)/shard_map/ppermute | solution.py:467
  65.6 18.6 %collective-permute-start.8 = (bf16[256,1408]{1,0:T(8,128)(2,1)}, bf16[256,1408]{1,0:T(8,128)(2,1)}, u32[]{:S(2)}, u32[]{:S(2)}) collective-permute-start(bf16[256,1408]{1,0:T(8,128)(2,1)} %collective-permute-done.6.rest_2_), channel_id=1, source_target_pairs={{0,56},{8,0},{16,8},{24,16},{32,24},{40,32},{48,40},{56,48},{1,57}... | collective-permute-start | bytes 2162696 | tf_op jit(solution)/shard_map/ppermute | solution.py:470
  84.2 17.6 %collective-permute-start.9 = (bf16[256,1408]{1,0:T(8,128)(2,1)}, bf16[256,1408]{1,0:T(8,128)(2,1)S(1)}, u32[]{:S(2)}, u32[]{:S(2)}) collective-permute-start(bf16[256,1408]{1,0:T(8,128)(2,1)} %collective-permute-done.7.rest_3_), channel_id=1, source_target_pairs={{0,8},{8,16},{16,24},{24,32},{32,40},{40,48},{48,56},{56,0},{1,9},... | collective-permute-start | bytes 2162696 | tf_op jit(solution)/shard_map/ppermute | solution.py:467
  84.2 18.5 %collective-permute-start.10 = (bf16[256,1408]{1,0:T(8,128)(2,1)}, bf16[256,1408]{1,0:T(8,128)(2,1)}, u32[]{:S(2)}, u32[]{:S(2)}) collective-permute-start(bf16[256,1408]{1,0:T(8,128)(2,1)} %collective-permute-done.8.rest_4_), channel_id=1, source_target_pairs={{0,56},{8,0},{16,8},{24,16},{32,24},{40,32},{48,40},{56,48},{1,57}... | collective-permute-start | bytes 2162696 | tf_op jit(solution)/shard_map/ppermute | solution.py:470
  87.4 40.0 %collective-permute-start.1 = (bf16[4,128,1024]{2,1,0:T(8,128)(2,1)}, bf16[4,128,1024]{2,1,0:T(8,128)(2,1)}, u32[]{:S(2)}, u32[]{:S(2)}) collective-permute-start(bf16[4,128,1024]{2,1,0:T(8,128)(2,1)} %all-to-all-done.1.own), channel_id=1, source_target_pairs={{0,1},{1,0},{2,3},{3,2},{4,5},{5,4},{6,7},{7,6},{8,9},{9,8},{10,11... | collective-permute-start | bytes 3145736 | tf_op jit(solution)/shard_map/ppermute | solution.py:486
  102.6 24.8 %collective-permute-start.11 = (bf16[128,1408]{1,0:T(8,128)(2,1)}, bf16[128,1408]{1,0:T(8,128)(2,1)}, u32[]{:S(2)}, u32[]{:S(2)}) collective-permute-start(bf16[128,1408]{1,0:T(8,128)(2,1)} %slice.48), channel_id=1, source_target_pairs={{0,8},{8,16},{16,24},{24,32},{32,40},{40,48},{48,56},{56,0},{1,9},... | collective-permute-start | bytes 1081352 | tf_op jit(solution)/shard_map/ppermute | solution.py:467
  104.4 23.1 %collective-permute-start.12 = (bf16[128,1408]{1,0:T(8,128)(2,1)}, bf16[128,1408]{1,0:T(8,128)(2,1)}, u32[]{:S(2)}, u32[]{:S(2)}) collective-permute-start(bf16[128,1408]{1,0:T(8,128)(2,1)} %slice.49), channel_id=1, source_target_pairs={{0,56},{8,0},{16,8},{24,16},{32,24},{40,32},{48,40},{56,48},{1,57}... | collective-permute-start | bytes 1081352 | tf_op jit(solution)/shard_map/ppermute | solution.py:470
  107.6 19.8 %collective-permute-start.2 = (bf16[128,1024]{1,0:T(8,128)(2,1)}, bf16[128,1024]{1,0:T(8,128)(2,1)}, u32[]{:S(2)}, u32[]{:S(2)}) collective-permute-start(bf16[128,1024]{1,0:T(8,128)(2,1)} %bitcast.28), channel_id=1, source_target_pairs={{0,0},{8,64},{16,128},{24,192},{32,32},{40,96},{48,160},{56,224},{... | collective-permute-start | bytes 786440 | tf_op jit(solution)/shard_map/ppermute | solution.py:474
  110.2 7.7 %collective-permute-start.3 = (s32[1]{0:T(128)}, s32[1]{0:T(128)}, u32[]{:S(2)}, u32[]{:S(2)}) collective-permute-start(s32[1]{0:T(128)} %bitcast.9), channel_id=1, source_target_pairs={{0,8},{8,16},{16,24},{24,32},{32,40},{40,48},{48,56},{56,64},{64,7... | collective-permute-start | bytes 20 | tf_op jit(solution)/shard_map/ppermute | solution.py:462
  118.5 8.9 %collective-permute-start.4 = (f32[8,128]{1,0:T(8,128)S(1)}, f32[8,128]{1,0:T(8,128)S(1)}, u32[]{:S(2)}, u32[]{:S(2)}) collective-permute-start(f32[8,128]{1,0:T(8,128)S(1)} %pad_convert_fusion), channel_id=1, source_target_pairs={{0,0},{8,64},{16,128},{24,192},{32,32},{40,96},{48,160},{56,224},{... | collective-permute-start | bytes 12296 | tf_op jit(solution)/shard_map/ppermute | solution.py:464
  137.3 33.6 %all-to-all-start.2 = ((bf16[4,592,512]{2,1,0:T(8,128)(2,1)}), bf16[4,592,512]{2,1,0:T(8,128)(2,1)}, u32[]{:S(2)}, u32[]{:S(2)}) async-start(bf16[4,592,512]{2,1,0:T(8,128)(2,1)} %get-tuple-element.19), calls=%async_computation.2 | async-start | bytes 4849664 | tf_op jit(solution)/shard_map/all_to_all | solution.py:498
  145.7 38.2 %copy-start.12 = (f32[16]{0:T(128)S(1)}, f32[16]{0:T(128)}, u32[]{:S(2)}) copy-start(f32[16]{0:T(128)} %param.24) | copy-start | bytes 196
  177.7 11.7 %collective-permute-start.13 = (bf16[272,128]{1,0:T(8,128)(2,1)}, bf16[272,128]{1,0:T(8,128)(2,1)S(1)}, u32[]{:S(2)}, u32[]{:S(2)}) collective-permute-start(bf16[272,128]{1,0:T(8,128)(2,1)} %get-tuple-element.20), channel_id=1, source_target_pairs={{0,32},{8,40},{16,48},{24,56},{32,16},{40,24},{48,0},{56,8},{1,33}... | collective-permute-start | bytes 208904 | tf_op jit(solution)/shard_map/ppermute | solution.py:500
  180.9 8.5 %collective-permute-start.14 = (bf16[272,128]{1,0:T(8,128)(2,1)}, bf16[272,128]{1,0:T(8,128)(2,1)S(1)}, u32[]{:S(2)}, u32[]{:S(2)}) collective-permute-start(bf16[272,128]{1,0:T(8,128)(2,1)} %get-tuple-element.21), channel_id=1, source_target_pairs={{0,16},{8,24},{16,0},{24,8},{32,48},{40,56},{48,32},{56,40},{1,17}... | collective-permute-start | bytes 208904 | tf_op jit(solution)/shard_map/ppermute | solution.py:500
  181.9 8.6 %collective-permute-start.15 = (bf16[272,128]{1,0:T(8,128)(2,1)}, bf16[272,128]{1,0:T(8,128)(2,1)S(1)}, u32[]{:S(2)}, u32[]{:S(2)}) collective-permute-start(bf16[272,128]{1,0:T(8,128)(2,1)} %get-tuple-element.22), channel_id=1, source_target_pairs={{0,48},{8,56},{16,32},{24,40},{32,0},{40,8},{48,16},{56,24},{1,49}... | collective-permute-start | bytes 208904 | tf_op jit(solution)/shard_map/ppermute | solution.py:500
  233.7 6.3 %collective-permute-start.16 = (bf16[4,128,1024]{2,1,0:T(8,128)(2,1)}, bf16[4,128,1024]{2,1,0:T(8,128)(2,1)}, u32[]{:S(2)}, u32[]{:S(2)}) collective-permute-start(bf16[4,128,1024]{2,1,0:T(8,128)(2,1)} %get-tuple-element.35), channel_id=1, source_target_pairs={{0,1},{1,0},{2,3},{3,2},{4,5},{5,4},{6,7},{7,6},{8,9},{9,8},{10,11... | collective-permute-start | bytes 3145736 | tf_op jit(solution)/shard_map/ppermute | solution.py:505
  242.0 30.9 %copy-start.13 = (s32[1,128]{1,0:T(1,128)S(1)}, s32[1,128]{1,0:T(1,128)}, u32[]{:S(2)}) copy-start(s32[1,128]{1,0:T(1,128)} %param.18) | copy-start | bytes 1540
  264.0 47.2 %copy-start.3 = (bf16[128,1024]{1,0:T(8,128)(2,1)S(1)}, bf16[128,1024]{1,0:T(8,128)(2,1)}, u32[]{:S(2)}) copy-start(bf16[128,1024]{1,0:T(8,128)(2,1)} %copy-done.2) | copy-start | bytes 786436
  265.5 1.5 collective-permute-start.18
  267.7 8.4 %collective-permute-start.19 = (f32[8,128]{1,0:T(8,128)S(1)}, f32[8,128]{1,0:T(8,128)S(1)}, u32[]{:S(2)}, u32[]{:S(2)}) collective-permute-start(f32[8,128]{1,0:T(8,128)S(1)} %broadcast_add_fusion), channel_id=1, source_target_pairs={{0,64},{64,128},{128,192},{192,0},{1,65},{65,129},{129,193},{193,1... | collective-permute-start | bytes 12296 | tf_op jit(solution)/shard_map/ppermute | solution.py:445
  269.4 6.7 %collective-permute-start.20 = (f32[8,128]{1,0:T(8,128)S(1)}, f32[8,128]{1,0:T(8,128)S(1)}, u32[]{:S(2)}, u32[]{:S(2)}) collective-permute-start(f32[8,128]{1,0:T(8,128)S(1)} %broadcast_add_fusion), channel_id=1, source_target_pairs={{0,128},{64,192},{128,0},{192,64},{1,129},{65,193},{129,1},{193,65... | collective-permute-start | bytes 12296 | tf_op jit(solution)/shard_map/ppermute | solution.py:445
  270.8 5.3 %collective-permute-start.21 = (f32[8,128]{1,0:T(8,128)S(1)}, f32[8,128]{1,0:T(8,128)S(1)}, u32[]{:S(2)}, u32[]{:S(2)}) collective-permute-start(f32[8,128]{1,0:T(8,128)S(1)} %broadcast_add_fusion), channel_id=1, source_target_pairs={{0,192},{64,0},{128,64},{192,128},{1,193},{65,1},{129,65},{193,129... | collective-permute-start | bytes 12296 | tf_op jit(solution)/shard_map/ppermute | solution.py:445
  272.9 19.5 %collective-permute-start.17 = (bf16[128,1024]{1,0:T(8,128)(2,1)S(1)}, bf16[128,1024]{1,0:T(8,128)(2,1)S(1)}, u32[]{:S(2)}, u32[]{:S(2)}) collective-permute-start(bf16[128,1024]{1,0:T(8,128)(2,1)S(1)} %get-tuple-element.39), channel_id=1, source_target_pairs={{0,0},{1,1},{64,2},{65,3},{128,4},{129,5},{192,6},{193,7},{2,8},{3... | collective-permute-start | bytes 786440 | tf_op jit(solution)/shard_map/ppermute | solution.py:512
  276.8 13.8 %collective-permute-start.22 = (f32[8,128]{1,0:T(8,128)S(1)}, f32[8,128]{1,0:T(8,128)S(1)}, u32[]{:S(2)}, u32[]{:S(2)}) collective-permute-start(f32[8,128]{1,0:T(8,128)S(1)} %add_add_fusion), channel_id=1, source_target_pairs={{0,0},{1,1},{64,2},{65,3},{128,4},{129,5},{192,6},{193,7},{2,8},{3... | collective-permute-start | bytes 12296 | tf_op jit(solution)/shard_map/ppermute | solution.py:515
  293.8 14.6 %all-to-all-start.5 = ((bf16[16,2,1152]{2,1,0:T(2,128)(2,1)}), bf16[16,2,1152]{2,1,0:T(2,128)(2,1)S(1)}, u32[]{:S(2)}, u32[]{:S(2)}) async-start(bf16[16,2,1152]{2,1,0:T(2,128)(2,1)} %all_to_all.35), calls=%async_computation.5 | async-start | bytes 147456 | tf_op jit(solution)/shard_map/all_to_all | solution.py:524
  (8 other events, 56.0 us)
